TPU v7x, 32 devices: a whole 2x2x4 slice. The times are simulated.
32 devices in a mesh: weight: 2 (over x), ctx: 4 (over z), tensor: 4 (over y, core).
Axes of the slice: x: 2, y: 2, z: 4, core: 2. Of those that a mesh axis runs over, the one named last changes fastest.
Arguments:
- inputs: bfloat16 [2, 1024, 1024], P('weight', 'ctx'), may hold values from -40 to 40
- w_qkv: bfloat16 [1024, 3, 1024], P('weight', None, 'tensor'), may hold values from -4 to 4
- w_out: bfloat16 [1024, 1024], P('weight', 'tensor'), may hold values from -2 to 2
- w_up: bfloat16 [1024, 4096], P('weight', 'tensor'), may hold values from -0.1875 to 0.1875
- w_down: bfloat16 [1024, 4096], P('weight', 'tensor'), may hold values from -0.09375 to 0.09375
- head_bias: float32 [2, 1024], P(None, 'tensor'), may hold values from -3 to 3
- up_bias: float32 [4096], P('tensor'), may hold values from -3 to 3
- out_biases: float32 [2, 1024], replicated, may hold values from -3 to 3
- norm_gains: float32 [2, 1024], replicated, may hold values from 0.1 to 1.9
- norm_shifts: float32 [2, 1024], replicated, may hold values from -3 to 3
- cotangent: bfloat16 [2, 1024, 1024], P('weight', 'ctx'), may hold values from -6 to 6
Outputs:
- layer_out: bfloat16 [2, 1024, 1024], P('weight', 'ctx')
- grad_input: bfloat16 [2, 1024, 1024], P('weight', 'ctx')
- grad_w_qkv: float32 [1024, 3, 1024], P(('weight', 'ctx'), None, 'tensor')
- grad_w_out: float32 [1024, 1024], P(('weight', 'ctx'), 'tensor')
- grad_w_up: float32 [1024, 4096], P(('weight', 'ctx'), 'tensor')
- grad_w_down: float32 [1024, 4096], P(('weight', 'ctx'), 'tensor')
- grad_head_bias: float32 [2, 1024], P(None, 'tensor')
- grad_up_bias: float32 [4096], P('tensor')
- grad_out_biases: float32 [2, 1024], replicated
- grad_norm_gains: float32 [2, 1024], replicated
- grad_norm_shifts: float32 [2, 1024], replicated
All inputs are finite; a program needn't handle non-finite values.
Results may differ from a plain program's by a relative error of at most 0.038.
Values may be sent and summed in bfloat16 or wider, within the bound.
No kernel may reach another device: no remote copies, remote signals or barrier semaphores. Data moves between devices by JAX's collectives and lax.ppermute only.
A program may use at most 128 MiB of HBM per device.

v0:
```python
import math

import jax
import jax.numpy as jnp
from jax import lax
from jax.experimental import pallas as pl
from jax.experimental.pallas import tpu as pltpu
from jax.sharding import PartitionSpec as P


HD = 64
ROOM = pltpu.CompilerParams(vmem_limit_bytes=20 << 20)
BF = jnp.bfloat16
F32 = jnp.float32


norm_epsilon = 1e-05
inv_root_two = 1.0 / math.sqrt(2.0)
inv_root_tau = 1.0 / math.sqrt(2.0 * math.pi)

NT = (((1,), (1,)), ((), ()))
NN = (((1,), (0,)), ((), ()))
TN = (((0,), (0,)), ((), ()))


def dot(a, b, dims):
    return lax.dot_general(a, b, dims, preferred_element_type=F32)


def layer_stats(hidden):
    mean_row = jnp.mean(hidden, axis=-1, keepdims=True)
    centred = hidden - mean_row
    inverse_spread = lax.rsqrt(jnp.mean(centred * centred, axis=-1, keepdims=True) + norm_epsilon)
    return (centred * inverse_spread, inverse_spread)


def layer_back(grad_norm, normed, inverse_spread):
    return inverse_spread * (
        grad_norm
        - jnp.mean(grad_norm, axis=-1, keepdims=True)
        - normed * jnp.mean(grad_norm * normed, axis=-1, keepdims=True)
    )


def gelu_value(pre_act):
    return 0.5 * pre_act * (1.0 + lax.erf(pre_act * inv_root_two))


def gelu_slope(pre_act):
    return (
        0.5 * (1.0 + lax.erf(pre_act * inv_root_two))
        + pre_act * jnp.exp(-0.5 * pre_act * pre_act) * inv_root_tau
    )


def head_mask(shape, head):
    lane = lax.broadcasted_iota(jnp.int32, shape, 1)
    return (lane >= head * HD) & (lane < (head + 1) * HD)


def as_rows(columns, rows):
    tokens = columns[0].shape[0]
    lane = lax.broadcasted_iota(jnp.int32, (tokens, 128), 1)
    tile = jnp.zeros((tokens, 128), F32)
    for i, col in enumerate(columns):
        tile = jnp.where(lane == i, col, tile)
    return tile.T[:rows]


def halves(refs):
    cols = refs[0].shape[1] // 2
    return [r.at[:, pl.ds(0, cols)] for r in refs], [r.at[:, pl.ds(cols, cols)] for r in refs]


def attend_kernel(n, heads, *refs):
    q_ref, near_ref, far_ref, kv_refs = refs[0], refs[1], refs[2], refs[3 : 3 + n]
    out_ref, lse_ref, keep_ref, sent_ref = refs[3 + n :]
    q = q_ref[...]
    k_refs, v_refs = halves(kv_refs)
    out = jnp.zeros(q.shape, F32)
    lses = []
    for h in range(heads):
        mask = head_mask(q.shape, h)
        qh = jnp.where(mask, q, jnp.zeros_like(q))
        scores = [dot(qh, k[...], NT) for k in k_refs]
        top = scores[0]
        for s in scores[1:]:
            top = jnp.maximum(top, s)
        top = jnp.max(top, axis=1, keepdims=True)
        total = jnp.zeros(top.shape, F32)
        acc = jnp.zeros(q.shape, F32)
        psum = None
        for s, v in zip(scores, v_refs):
            p = jnp.exp(s - top)
            psum = p if psum is None else psum + p
            acc = acc + dot(p.astype(BF), v[...], NN)
        total = jnp.sum(psum, axis=1, keepdims=True)
        out = jnp.where(mask, acc / total, out)
        lses.append(top + jnp.log(total))
    out_ref[...] = out.astype(BF)
    lse_ref[...] = as_rows(lses, heads)
    weight = pl.ds(near_ref.shape[1] - q.shape[1], q.shape[1])
    out_kernel(out_ref, near_ref.at[:, weight], far_ref.at[:, weight], keep_ref, sent_ref)


def attend(q, near, far, kvs):
    n, (tokens, cols) = len(kvs), q.shape
    width = 2 * near.shape[0]
    heads = cols // HD
    keys = n * tokens
    return pl.pallas_call(
        lambda *r: attend_kernel(n, heads, *r),
        out_shape=(
            jax.ShapeDtypeStruct((tokens, cols), BF),
            jax.ShapeDtypeStruct((heads, tokens), F32),
            jax.ShapeDtypeStruct((tokens // 2, width), F32),
            jax.ShapeDtypeStruct((tokens // 2, width), BF),
        ),
        cost_estimate=pl.CostEstimate(
            flops=4 * tokens * keys * cols * heads,
            bytes_accessed=2 * (2 * keys + 2 * tokens) * cols,
            transcendentals=tokens * keys * heads,
        ),
        name="attend",
        compiler_params=ROOM,
    )(q, near, far, *kvs)


def split_rows(rows):
    high = rows.astype(BF)
    rest = rows - high.astype(F32)
    middle = rest.astype(BF)
    low = (rest - middle.astype(F32)).astype(BF)
    return [high, middle, low]


def message_rows(tokens, heads):
    return tokens + -(-6 * heads // 16) * 16


def pack_kernel(heads, own_ref, got_ref, near_ref, far_ref, at_ref, lse_ref, msg_ref):
    half = near_ref.shape[0]
    one = jnp.concatenate([own_ref[...], got_ref[...]], axis=0)
    cols = at_ref.shape[1]
    out = pl.ds(near_ref.shape[1] - cols, cols)
    da = dot(one[:, :half], near_ref[:, out], NN) + dot(one[:, half:], far_ref[:, out], NN)
    da = da.astype(BF)
    tokens = da.shape[0]
    prod = da.astype(F32) * at_ref[...].astype(F32)
    deltas = []
    for h in range(heads):
        mask = head_mask(da.shape, h)
        deltas.append(jnp.sum(jnp.where(mask, prod, 0.0), axis=1, keepdims=True))
    rows = split_rows(lse_ref[...]) + split_rows(as_rows(deltas, heads))
    spare = msg_ref.shape[0] - tokens - 6 * heads
    if spare:
        rows.append(jnp.zeros((spare, tokens), BF))
    msg_ref[:tokens, :] = da
    msg_ref[tokens:, :] = jnp.concatenate([r.astype(F32) for r in rows], axis=0).astype(BF)


def pack_message(own, got, near, far, attended, lse):
    tokens, cols = attended.shape
    heads = cols // HD
    if tokens != cols:
        raise ValueError("message shape")
    return pl.pallas_call(
        lambda *r: pack_kernel(heads, *r),
        out_shape=jax.ShapeDtypeStruct((message_rows(tokens, heads), cols), BF),
        cost_estimate=pl.CostEstimate(
            flops=2 * tokens * own.shape[1] * cols,
            bytes_accessed=2 * (2 * own.size + near.size + far.size + 2 * attended.size),
            transcendentals=0,
        ),
        name="pack_message",
        compiler_params=ROOM,
    )(own, got, near, far, attended, lse)


def query_kernel(n, heads, *refs):
    q_ref, da_ref, at_ref, lse_ref = refs[:4]
    k_refs, v_refs = halves(refs[4 : 4 + n])
    dq_ref, sum_ref = refs[4 + n :]
    q = q_ref[...]
    tokens = q.shape[0]
    da = da_ref[:tokens, :]
    prod = da.astype(F32) * at_ref[...].astype(F32)
    lse_pad = jnp.concatenate([lse_ref[...], jnp.zeros((128 - heads, tokens), F32)], axis=0).T
    out = jnp.zeros(q.shape, F32)
    for h in range(heads):
        mask = head_mask(q.shape, h)
        zero = jnp.zeros_like(q)
        qh, dah = jnp.where(mask, q, zero), jnp.where(mask, da, zero)
        delta = jnp.sum(jnp.where(mask, prod, 0.0), axis=1, keepdims=True)
        lse = lse_pad[:, h : h + 1]
        acc = jnp.zeros(q.shape, F32)
        for k, v in zip(k_refs, v_refs):
            p = jnp.exp(dot(qh, k[...], NT) - lse)
            ds = (p * (dot(dah, v[...], NT) - delta)).astype(BF)
            acc = acc + dot(ds, k[...], NN)
        out = jnp.where(mask, acc, out)
    out = out * (HD**-0.5)
    dq_ref[...] = out.astype(BF)
    sum_ref[...] = jnp.sum(out, axis=0, keepdims=True)


def query_grads(q, msg, attended, lse, kvs):
    n, (tokens, cols) = len(kvs), q.shape
    heads, keys = cols // HD, len(kvs) * q.shape[0]
    return pl.pallas_call(
        lambda *r: query_kernel(n, heads, *r),
        out_shape=(
            jax.ShapeDtypeStruct((tokens, cols), BF),
            jax.ShapeDtypeStruct((1, cols), F32),
        ),
        cost_estimate=pl.CostEstimate(
            flops=6 * tokens * keys * cols * heads,
            bytes_accessed=2 * (2 * keys + 4 * tokens) * cols,
            transcendentals=tokens * keys * heads,
        ),
        name="query_grads",
        compiler_params=ROOM,
    )(q, msg, attended, lse, *kvs)


def key_kernel(m, n, heads, *refs):
    kv_ref = refs[0]
    tokens, cols = kv_ref.shape[0], kv_ref.shape[1] // 2
    qs = [
        r.at[pl.ds(i * tokens, tokens)]
        for r in refs[1 : 1 + m]
        for i in range(r.shape[0] // tokens)
    ]
    msgs = refs[1 + m : 1 + m + n]
    out_ref, sum_ref = refs[1 + m + n :]
    k, v = kv_ref[:, :cols], kv_ref[:, cols:]
    stats = []
    for msg in msgs:
        rows = msg[tokens:, :].astype(F32)
        part = [rows[i * heads : (i + 1) * heads] for i in range(6)]
        stats.append((part[0] + part[1] + part[2], part[3] + part[4] + part[5]))
    dk, dv = jnp.zeros(k.shape, F32), jnp.zeros(k.shape, F32)
    for h in range(heads):
        mask = head_mask(k.shape, h)
        zero = jnp.zeros_like(k)
        kh, vh = jnp.where(mask, k, zero), jnp.where(mask, v, zero)
        dk_acc, dv_acc = jnp.zeros(k.shape, F32), jnp.zeros(k.shape, F32)
        for q, msg, (lse, delta) in zip(qs, msgs, stats):
            da = msg[:tokens, :]
            p = jnp.exp(dot(kh, q[...], NT) - lse[h : h + 1, :])
            dv_acc = dv_acc + dot(p.astype(BF), da, NN)
            ds = (p * (dot(vh, da, NT) - delta[h : h + 1, :])).astype(BF)
            dk_acc = dk_acc + dot(ds, q[...], NN)
        dk, dv = jnp.where(mask, dk_acc, dk), jnp.where(mask, dv_acc, dv)
    out_ref[:, :cols] = dk.astype(BF)
    out_ref[:, cols:] = dv.astype(BF)
    sum_ref[...] = jnp.sum(dv, axis=0, keepdims=True)


def key_grads(kv, qs, msgs):
    m, n, tokens, cols = len(qs), len(msgs), kv.shape[0], kv.shape[1] // 2
    heads, rows = cols // HD, n * tokens
    return pl.pallas_call(
        lambda *r: key_kernel(m, n, heads, *r),
        out_shape=(
            jax.ShapeDtypeStruct((tokens, 2 * cols), BF),
            jax.ShapeDtypeStruct((1, cols), F32),
        ),
        cost_estimate=pl.CostEstimate(
            flops=8 * tokens * rows * cols * heads,
            bytes_accessed=2 * (2 * rows + 4 * tokens) * cols,
            transcendentals=tokens * rows * heads,
        ),
        name="key_grads",
        compiler_params=ROOM,
    )(kv, *qs, *msgs)


def shape(rows, cols, dtype):
    return jax.ShapeDtypeStruct((rows, cols), dtype)


def call(kernel, outs, *args, flops=0, scalars=0):
    outs_list = outs if isinstance(outs, (tuple, list)) else (outs,)
    total = sum(math.prod(a.shape) * a.dtype.itemsize for a in list(args) + list(outs_list))
    return pl.pallas_call(
        kernel,
        out_shape=outs,
        in_specs=[
            pl.BlockSpec(memory_space=pltpu.SMEM if i < scalars else pltpu.VMEM)
            for i in range(len(args))
        ],
        cost_estimate=pl.CostEstimate(flops=flops, bytes_accessed=total, transcendentals=0),
        compiler_params=ROOM,
    )(*args)


def column_blocks(cols):
    size = 256 if cols % 256 == 0 else cols
    return [pl.ds(i, size) for i in range(0, cols, size)]


def put_partial(block, value, keep_ref, sent_ref):
    half = keep_ref.shape[0]
    keep_ref[:, block] = value[:half]
    sent_ref[:, block] = value[half:].astype(BF)


def out_kernel(at_ref, near_ref, far_ref, keep_ref, sent_ref):
    at = at_ref[...]
    half = near_ref.shape[0]
    for start, ref in ((0, near_ref), (half, far_ref)):
        for rows in column_blocks(half):
            value = dot(at, ref[rows, :], NT)
            put_partial(pl.ds(start + rows.start, rows.size), value, keep_ref, sent_ref)


def norm_one_kernel(sent_ref, got_ref, x_ref, bias_ref, gain_ref, shift_ref, *outs):
    mixed_ref, normed_ref, inverse_ref, own_ref = outs
    summed = sent_ref[...].astype(F32) + got_ref[...].astype(F32)
    hidden = x_ref[...].astype(F32) + summed + bias_ref[0:1, :]
    normed, inverse = layer_stats(hidden)
    mixed = normed * gain_ref[0:1, :] + shift_ref[0:1, :]
    mixed_ref[...] = mixed
    normed_ref[...] = normed
    inverse_ref[...] = jnp.broadcast_to(inverse, inverse_ref.shape)
    own_ref[...] = mixed.astype(BF)


def up_kernel(own_ref, got_ref, near_ref, far_ref, bias_ref, pre_ref, act_ref):
    half = near_ref.shape[0]
    mixed = jnp.concatenate([own_ref[...], got_ref[...]], axis=0)
    low, high = mixed[:, :half], mixed[:, half:]
    for block in column_blocks(near_ref.shape[1]):
        pre = dot(low, near_ref[:, block], NN) + dot(high, far_ref[:, block], NN)
        pre = pre + bias_ref[:, block]
        pre_ref[:, block] = pre
        act_ref[:, block] = gelu_value(pre).astype(BF)


def offsets(n):
    held = [0]
    for bit in levels(n):
        held = held + [i ^ bit for i in held]
    return held


def down_kernel(rank_ref, act_ref, near_ref, *refs):
    pieces, (far_ref, keep_ref, sent_ref) = refs[:-3], refs[-3:]
    rows = pieces[0].shape[0]
    for offset, piece in zip(offsets(len(pieces)), pieces):
        at = pl.multiple_of(jnp.bitwise_xor(rank_ref[0], offset) * rows, rows)
        far_ref[pl.ds(at, rows), :] = piece[...]
    out_kernel(act_ref, near_ref, far_ref, keep_ref, sent_ref)


def norm_two_kernel(
    sent_ref, got_ref, mixed_ref, cot_ref, bias_ref, gain_ref, shift_ref, pair_ref, grad_ref, sum_ref
):
    summed = sent_ref[...].astype(F32) + got_ref[...].astype(F32)
    normed, inverse = layer_stats(mixed_ref[...] + summed + bias_ref[1:2, :])
    gain = gain_ref[1:2, :]
    cot = cot_ref[...].astype(F32)
    grad = layer_back(cot * gain, normed, inverse)
    half = grad.shape[0]
    pair_ref[:half, :] = grad.astype(BF)
    pair_ref[half:, :] = (normed * gain + shift_ref[1:2, :]).astype(BF)
    grad_ref[...] = grad
    sum_ref[0:1, :] = jnp.sum(grad, axis=0, keepdims=True)
    sum_ref[1:2, :] = jnp.sum(cot * normed, axis=0, keepdims=True)
    sum_ref[2:3, :] = jnp.sum(cot, axis=0, keepdims=True)


def back_kernel(own_ref, got_ref, dn_ref, df_ref, pre_ref, un_ref, uf_ref, *outs):
    grad_ref, sum_ref, keep_ref, sent_ref = outs
    half = dn_ref.shape[0]
    tokens = own_ref.shape[0] // 2
    two = jnp.concatenate([own_ref[:tokens, :], got_ref[:tokens, :]], axis=0)
    low, high = two[:, :half], two[:, half:]
    for block in column_blocks(dn_ref.shape[1]):
        grad = dot(low, dn_ref[:, block], NN) + dot(high, df_ref[:, block], NN)
        grad = grad * gelu_slope(pre_ref[:, block])
        sum_ref[:, block] = jnp.sum(grad, axis=0, keepdims=True)
        grad_ref[:, block] = grad.astype(BF)
    out_kernel(grad_ref, un_ref, uf_ref, keep_ref, sent_ref)


def norm_back_kernel(sent_ref, got_ref, two_ref, normed_ref, inverse_ref, gain_ref, *outs):
    own_ref, grad_ref, sum_ref = outs
    normed = normed_ref[...]
    mixed = two_ref[...] + (sent_ref[...].astype(F32) + got_ref[...].astype(F32))
    grad = layer_back(mixed * gain_ref[0:1, :], normed, inverse_ref[:, 0:1])
    own_ref[...] = grad.astype(BF)
    grad_ref[...] = grad
    sum_ref[0:1, :] = jnp.sum(grad, axis=0, keepdims=True)
    sum_ref[1:2, :] = jnp.sum(mixed * normed, axis=0, keepdims=True)
    sum_ref[2:3, :] = jnp.sum(mixed, axis=0, keepdims=True)


def input_kernel(dq_ref, dkv_ref, qo_ref, qo_far_ref, kv_ref, kv_far_ref, keep_ref, sent_ref):
    dq, dkv = dq_ref[...], dkv_ref[...]
    cols, half = dq.shape[1], qo_ref.shape[0]
    for start, q_ref, k_ref in ((0, qo_ref, kv_ref), (half, qo_far_ref, kv_far_ref)):
        for rows in column_blocks(half):
            value = dot(dq, q_ref[rows, pl.ds(0, cols)], NT) + dot(dkv, k_ref[rows, :], NT)
            put_partial(pl.ds(start + rows.start, rows.size), value, keep_ref, sent_ref)


def weight_kernel(n, terms, mine_ref, *refs):
    ins, (away_ref, stay_ref) = refs[:-2], refs[-2:]
    rows = away_ref.shape[1]
    mine = mine_ref[0]
    for i in range(n // 2):
        for out, side in ((away_ref, 1 - mine), (stay_ref, mine)):
            at = pl.multiple_of((2 * i + side) * rows, rows)
            col, k = 0, 0
            for count in terms:
                value = None
                for _ in range(count):
                    a, b = ins[k], ins[k + 1]
                    k += 2
                    term = dot(a[:, pl.ds(at, rows)], b[...], TN)
                    value = term if value is None else value + term
                out[i, :, pl.ds(col, value.shape[1])] = value.astype(BF)
                col += value.shape[1]


def levels(n):
    return [1 << i for i in reversed(range(n.bit_length() - 1))]


def build(nw, nc, nt):
    if nw != 2 or nt % 2 or nc & (nc - 1) or nt & (nt - 1):
        raise ValueError("mesh")
    sizes = {"weight": nw, "ctx": nc, "tensor": nt}

    def send(a, axis, bit=1):
        return lax.ppermute(a, axis, [(i, i ^ bit) for i in range(sizes[axis])])

    def settle(keep, sent):
        total = keep + send(sent, "tensor").astype(F32)
        bit = 2
        while bit < nt:
            sent = total.astype(BF)
            got = send(sent, "tensor", bit)
            total = sent.astype(F32) + got.astype(F32)
            bit *= 2
        return sent, got

    def gather(a):
        held, bit = [a], nc // 2
        while bit:
            held = held + [send(h, "ctx", bit) for h in held]
            bit //= 2
        return held

    def gather_few(a):
        held, bit = [a], nc // 2
        while bit:
            whole = held[0] if len(held) == 1 else jnp.concatenate(held, axis=0)
            held = held + [send(whole, "ctx", bit)]
            bit //= 2
        return held

    def owned(products, after):
        rank = lax.axis_index("ctx")
        rows = products[0][0][0].shape[1] // nc
        cols = sum(p[0][1].shape[1] for p in products)
        mine = jnp.bitwise_and(rank, 1)
        if rows % 128 == 0:
            flat = [m for p in products for term in p for m in term]
            terms = [len(p) for p in products]
            part = jax.ShapeDtypeStruct((nc // 2, rows, cols), BF)
            away, stay = call(
                lambda *r: weight_kernel(nc, terms, *r),
                (part, part),
                mine.reshape(1),
                *flat,
                flops=sum(2 * m.shape[0] * m.shape[1] * rows * nc for m in flat[1::2]),
                scalars=1,
            )
        else:
            grad = [sum(dot(a_, b_, TN) for a_, b_ in p).astype(BF) for p in products]
            view = jnp.concatenate(grad, axis=1).reshape(nc // 2, 2, rows, cols)
            away = lax.dynamic_index_in_dim(view, 1 - mine, 1, keepdims=False)
            stay = lax.dynamic_index_in_dim(view, mine, 1, keepdims=False)
        bit = 1
        while True:
            got = send(away, "ctx", bit)
            got, stay, _ = lax.optimization_barrier((got, stay, after[0]))
            after = after[1:]
            total = stay.astype(F32) + got.astype(F32)
            bit *= 2
            if bit == nc:
                return total.reshape(rows, cols)
            mine = jnp.bitwise_and(rank // bit, 1)
            view = total.reshape(total.shape[0] // 2, 2, rows, cols)
            away = lax.dynamic_index_in_dim(view, 1 - mine, 1, keepdims=False).astype(BF)
            stay = lax.dynamic_index_in_dim(view, mine, 1, keepdims=False)

    def local(
        inputs, w_qkv, w_out, w_up, w_down, head_bias, up_bias, out_biases,
        norm_gains, norm_shifts, cotangent,
    ):
        tokens, width = inputs.shape[1], inputs.shape[2]
        half_t, half_d = tokens // 2, width // 2
        cols, hidden = w_qkv.shape[2], w_up.shape[1]
        rank = lax.axis_index("ctx")
        far_weight = lax.axis_index("weight") == 1
        far_core = jnp.bitwise_and(lax.axis_index("tensor"), 1) == 1

        def turn_d(a):
            return jnp.where(far_weight, jnp.concatenate([a[:, half_d:], a[:, :half_d]], 1), a)

        def turn_t(a):
            return jnp.where(far_core, jnp.concatenate([a[half_t:], a[:half_t]], 0), a)

        wq = w_qkv[:, 0]
        wkv = w_qkv[:, 1:3].reshape(half_d, 2 * cols)
        wqo = jnp.concatenate([wq, w_out], axis=1)
        wkv_far = send(wkv, "weight")
        wqo_far = send(wqo, "weight")
        piece = lax.dynamic_slice_in_dim(w_down, rank * (half_d // nc), half_d // nc, 0)
        piece = send(piece, "weight")
        up_far = send(w_up, "weight")
        pieces = gather(piece)

        x = turn_t(turn_d(inputs[0]))
        x_own = x[:half_t]
        cot = turn_t(turn_d(cotangent[0]))[:half_t]
        out_b, gains, shifts = turn_d(out_biases), turn_d(norm_gains), turn_d(norm_shifts)
        x_lo, x_hi = x[:, :half_d], x[:, half_d:]

        kv_bias = jnp.concatenate([jnp.zeros((cols,), F32), head_bias[1]])
        kv = (dot(x_lo, wkv, NN) + dot(x_hi, wkv_far, NN) + kv_bias).astype(BF)
        kvs = gather(kv)
        q = dot(x_lo, wq, NN) + dot(x_hi, wqo_far[:, :cols], NN) + head_bias[0]
        q = q.astype(BF) * BF(HD**-0.5)
        qs = gather_few(q)

        part = (shape(half_t, width, F32), shape(half_t, width, BF))
        attended, lse, keep, sent = attend(q, wqo, wqo_far, kvs)
        sent, got = settle(keep, sent)
        mixed_one, normed_one, inverse_one, mixed_own = call(
            norm_one_kernel,
            (part[0], part[0], shape(half_t, 128, F32), part[1]),
            sent, got, x_own, out_b, gains, shifts,
        )
        mixed_got = send(mixed_own, "tensor")
        big = 2 * tokens * width * hidden
        pre_act, act = call(
            up_kernel,
            (shape(tokens, hidden, F32), shape(tokens, hidden, BF)),
            mixed_own, mixed_got, w_up, up_far, up_bias.reshape(1, hidden),
            flops=big,
        )
        down_far, keep, sent = call(
            down_kernel,
            (shape(half_d, hidden, BF),) + part,
            rank.reshape(1), act, w_down, *pieces,
            flops=big, scalars=1,
        )
        sent, got = settle(keep, sent)
        act_mate = send(act, "weight")
        mixed_hi = jnp.concatenate([mixed_own[:, half_d:], mixed_got[:, half_d:]], axis=0)
        bundle = send(jnp.concatenate([mixed_hi, x_hi, attended], axis=1), "weight")
        mixed_mate, x_mate = bundle[:, :half_d], bundle[:, half_d:width]
        attended_mate = bundle[:, width:]

        pair, grad_two, sums_two = call(
            norm_two_kernel,
            (shape(tokens, width, BF), part[0], shape(3, width, F32)),
            sent, got, mixed_one, cot, out_b, gains, shifts,
        )
        pair_got = send(pair, "tensor")
        two_hi = jnp.concatenate([pair[:half_t, half_d:], pair_got[:half_t, half_d:]], axis=0)
        two_mate = send(two_hi, "weight")
        grad_pre, grad_up_b, keep, sent = call(
            back_kernel,
            (shape(tokens, hidden, BF), shape(1, hidden, F32)) + part,
            pair, pair_got, w_down, down_far, pre_act, w_up, up_far,
            flops=2 * big,
        )
        sent, got = settle(keep, sent)
        pre_mate = send(grad_pre, "weight")
        one_own, grad_one, sums_one = call(
            norm_back_kernel,
            (part[1], part[0], shape(3, width, F32)),
            sent, got, grad_two, normed_one, inverse_one, gains,
        )
        one_got = send(one_own, "tensor")
        msg = pack_message(one_own, one_got, wqo, wqo_far, attended, lse)
        msgs = gather(msg)
        two_lo = jnp.concatenate([pair[:half_t, :half_d], pair_got[:half_t, :half_d]], axis=0)
        one = jnp.concatenate([one_own, one_got], axis=0)
        one_mate = send(one[:, half_d:], "weight")
        dq, sums_q = query_grads(q, msg, attended, lse, kvs)
        dq_mate = send(dq, "weight")
        mixed_lo = jnp.concatenate([mixed_own[:, :half_d], mixed_got[:, :half_d]], axis=0)
        dkv, sums_v = key_grads(kv, qs, msgs)

        dkv_mate = send(dkv, "weight")
        keep, sent = call(
            input_kernel, part, dq, dkv, wqo, wqo_far, wkv, wkv_far,
            flops=6 * tokens * width * cols,
        )
        late = [sent] * 8
        grad_w_down = owned([[(two_lo, act), (two_mate, act_mate)]], [msg] + late)
        grad_w_up = owned([[(mixed_lo, grad_pre), (mixed_mate, pre_mate)]], [dq] + late)
        oq_grad = owned(
            [
                [(one[:, :half_d], attended), (one_mate, attended_mate)],
                [(x_lo, dq), (x_mate, dq_mate)],
            ],
            late,
        )
        grad_w_out, grad_wq = oq_grad[:, :cols], oq_grad[:, cols:]
        sent, got = settle(keep, sent)
        grad_wkv = owned([[(x_lo, dkv), (x_mate, dkv_mate)]], late)
        grad_own = (grad_one + (sent.astype(F32) + got.astype(F32))).astype(BF)
        grad_got = send(grad_own, "tensor")
        grad_input = turn_d(turn_t(jnp.concatenate([grad_own, grad_got], axis=0)))
        pair, pair_got, _ = lax.optimization_barrier((pair, pair_got, late[0]))
        layer_out = turn_d(turn_t(jnp.concatenate([pair[half_t:], pair_got[half_t:]], axis=0)))

        rows = jnp.concatenate([sums_one, sums_two], axis=0)
        rows = turn_d(rows + send(rows, "tensor"))
        vector = [rows.reshape(-1), grad_up_b[0], sums_q[0], sums_v[0]]
        vector = jnp.concatenate(vector).reshape(-1, 128)
        vector = vector + send(vector, "weight")
        bit = 1
        while bit < nc:
            vector = vector + send(vector, "ctx", bit)
            bit *= 2
        vector = vector.reshape(-1)
        rows = vector[: 6 * width].reshape(2, 3, width)
        heads_at = 6 * width + hidden
        return (
            layer_out[None],
            grad_input[None],
            jnp.stack([grad_wq, grad_wkv[:, :cols], grad_wkv[:, cols:]], axis=1),
            grad_w_out,
            grad_w_up,
            grad_w_down,
            vector[heads_at:].reshape(2, cols),
            vector[6 * width : heads_at],
            rows[:, 0],
            rows[:, 1],
            rows[:, 2],
        )

    return local


def solution(mesh):
    return jax.shard_map(
        build(mesh.shape["weight"], mesh.shape["ctx"], mesh.shape["tensor"]),
        mesh=mesh,
        in_specs=(
            P("weight", "ctx", None),
            P("weight", None, "tensor"),
            P("weight", "tensor"),
            P("weight", "tensor"),
            P("weight", "tensor"),
            P(None, "tensor"),
            P("tensor"),
            P(),
            P(),
            P(),
            P("weight", "ctx", None),
        ),
        out_specs=(
            P("weight", "ctx", None),
            P("weight", "ctx", None),
            P(("weight", "ctx"), None, "tensor"),
            P(("weight", "ctx"), "tensor"),
            P(("weight", "ctx"), "tensor"),
            P(("weight", "ctx"), "tensor"),
            P(None, "tensor"),
            P("tensor"),
            P(),
            P(),
            P(),
        ),
        check_vma=False,
    )
```

profile of v0, /device:TPU:0, one launch (start us, length us, event | category | flops | bytes accessed | tf_op | source)
XLA Modules:
  0.0 216.0 jit_solution(1572691531000012566)
XLA Ops:
  0.6 1.1 slice_bitcast_fusion
  1.8 3.0 %collective-permute-start.1 = (bf16[512,512]{1,0:T(8,128)(2,1)S(1)}, bf16[512,512]{1,0:T(8,128)(2,1)}, u32[]{:S(2)}, u32[]{:S(2)}) collective-permute-start(bf16[512,512]{1,0:T(8,128)(2,1)S(1)} %bitcast.65), channel_id=1, source_target_pairs={{0,16},{16,0},{1,17},{17,1},{2,18},{18,2},{3,19},{19,3},{4,20},{20... | collective-permute-start | bytes 1572872 | tf_op jit(solution)/shard_map/ppermute | solution.py:438
  6.1 1.9 collective-permute-start.8
  8.8 1.8 fusion.23
  10.6 2.1 maximum_select_fusion
  12.7 1.8 fusion.22
  14.5 1.3 maximum_select_fusion.1
  15.8 1.2 fusion.9
  17.7 1.3 fusion.1.r_3_.r_4_.r_0_
  19.1 3.2 %collective-permute-start.2 = (bf16[256,512]{1,0:T(8,128)(2,1)S(1)}, bf16[256,512]{1,0:T(8,128)(2,1)S(1)}, u32[]{:S(2)}, u32[]{:S(2)}) collective-permute-start(bf16[256,512]{1,0:T(8,128)(2,1)S(1)} %fusion.1.r_3_.r_4_.r_0_), channel_id=1, source_target_pairs={{0,8},{4,12},{8,0},{12,4},{1,9},{5,13},{9,1},{13,5},{2,10},{6,14},... | collective-permute-start | bytes 786440 | tf_op jit(solution)/shard_map/ppermute | solution.py:438
  22.3 1.6 collective-permute-start.3
  23.9 8.8 %collective-permute-done.2.r_4_.r_5_ = bf16[256,512]{1,0:T(8,128)(2,1)S(1)} collective-permute-done((bf16[256,512]{1,0:T(8,128)(2,1)S(1)}, bf16[256,512]{1,0:T(8,128)(2,1)S(1)}, u32[]{:S(2)}, u32[]{:S(2)}) %collective-permute-start.2) | collective-permute-done | bytes 262176 | tf_op jit(solution)/shard_map/ppermute | solution.py:438
  33.4 1.2 fusion.4.r_0_.r_1_
  34.6 5.3 %collective-permute-done.4.r_6_.r_7_ = bf16[256,512]{1,0:T(8,128)(2,1)S(1)} collective-permute-done((bf16[256,512]{1,0:T(8,128)(2,1)S(1)}, bf16[256,512]{1,0:T(8,128)(2,1)S(1)}, u32[]{:S(2)}, u32[]{:S(2)}) %collective-permute-start.4) | collective-permute-done | bytes 262176 | tf_op jit(solution)/shard_map/ppermute | solution.py:438
  39.9 3.4 %attend.1 = (bf16[256,256]{1,0:T(8,128)(2,1)S(1)}, f32[4,256]{1,0:T(4,128)S(1)}, f32[128,1024]{1,0:T(8,128)S(1)}, bf16[128,1024]{1,0:T(8,128)(2,1)S(1)}) custom-call(bf16[256,256]{1,0:T(8,128)(2,1)S(1)} %fusion.4.r_0_.r_1_, bf16[512,512]{1,0:T(8,128)(2,1)S(1)} %pad_maximum_fusion.1.r_1_.r_2_.qo_ref, ...), custom_call_target="tpu_custom_call" | custom-call | flops 1073741824 | bytes 1310720 | tf_op jit(solution)/shard_map/attend/pallas_call | solution.py:111
  45.0 1.6 collective-permute-start.6
  46.6 9.6 %collective-permute-done.9.refs_0_ = bf16[128,1024]{1,0:T(8,128)(2,1)} collective-permute-done((bf16[128,1024]{1,0:T(8,128)(2,1)}, bf16[128,1024]{1,0:T(8,128)(2,1)}, u32[]{:S(2)}, u32[]{:S(2)}) %collective-permute-start.9) | collective-permute-done | bytes 262176 | tf_op jit(solution)/shard_map/ppermute | solution.py:438
  56.2 2.8 %collective-permute-start.10 = (bf16[128,1024]{1,0:T(8,128)(2,1)}, bf16[128,1024]{1,0:T(8,128)(2,1)}, u32[]{:S(2)}, u32[]{:S(2)}) collective-permute-start(bf16[128,1024]{1,0:T(8,128)(2,1)} %collective-permute-done.9.refs_0_), channel_id=1, source_target_pairs={{0,8},{4,12},{8,0},{12,4},{1,9},{5,13},{9,1},{13,5},{2,10},{6,14},... | collective-permute-start | bytes 786440 | tf_op jit(solution)/shard_map/ppermute | solution.py:438
  63.0 1.6 collective-permute-start.11
  64.6 6.0 %collective-permute-done.10.refs_1_ = bf16[128,1024]{1,0:T(8,128)(2,1)} collective-permute-done((bf16[128,1024]{1,0:T(8,128)(2,1)}, bf16[128,1024]{1,0:T(8,128)(2,1)}, u32[]{:S(2)}, u32[]{:S(2)}) %collective-permute-start.10) | collective-permute-done | bytes 262176 | tf_op jit(solution)/shard_map/ppermute | solution.py:438
  71.2 1.1 fusion.20
  72.3 3.5 %collective-permute-start.19 = (bf16[256,256]{1,0:T(8,128)(2,1)S(1)}, bf16[256,256]{1,0:T(8,128)(2,1)S(1)}, u32[]{:S(2)}, u32[]{:S(2)}) collective-permute-start(bf16[256,256]{1,0:T(8,128)(2,1)S(1)} %copy-done.19), channel_id=1, source_target_pairs={{0,8},{4,12},{8,0},{12,4},{1,9},{5,13},{9,1},{13,5},{2,10},{6,14},... | collective-permute-start | bytes 393224 | tf_op jit(solution)/shard_map/ppermute | solution.py:438
  75.8 2.2 %shard_map.195 = (f32[256,1024]{1,0:T(8,128)S(1)}, bf16[256,1024]{1,0:T(8,128)(2,1)S(1)}) custom-call(bf16[128,1024]{1,0:T(8,128)(2,1)} %get-tuple-element.68.own_ref, bf16[128,1024]{1,0:T(8,128)(2,1)} %collective-permute-done.7.got_ref, bf16[512,1024]{1,0:T(8,128)(2,1)S(1)} %copy-done.1, bf16[512,1024]{1,0:T(8,128)(2,1)} %collective-permute-done.8.far_ref.uf_ref, ...), custom_call_target="tpu_custom_call" | custom-call | flops 536870912 | bytes 4198400 | tf_op jit(solution)/shard_map/pallas_call | solution.py:286
  78.0 6.4 %collective-permute-done.12.refs_3_ = bf16[128,1024]{1,0:T(8,128)(2,1)S(1)} collective-permute-done((bf16[128,1024]{1,0:T(8,128)(2,1)}, bf16[128,1024]{1,0:T(8,128)(2,1)S(1)}, u32[]{:S(2)}, u32[]{:S(2)}) %collective-permute-start.12) | collective-permute-done | bytes 262176 | tf_op jit(solution)/shard_map/ppermute | solution.py:438
  84.4 1.8 shard_map.196
  87.9 1.6 collective-permute-start.14
  90.5 1.6 collective-permute-start.39
  93.0 3.3 %collective-permute-done.14.got_ref = bf16[128,1024]{1,0:T(8,128)(2,1)S(1)} collective-permute-done((bf16[128,1024]{1,0:T(8,128)(2,1)S(1)}, bf16[128,1024]{1,0:T(8,128)(2,1)S(1)}, u32[]{:S(2)}, u32[]{:S(2)}) %collective-permute-start.14) | collective-permute-done | bytes 262176 | tf_op jit(solution)/shard_map/ppermute | solution.py:438
  97.0 1.5 collective-permute-start.28
  98.9 2.9 %shard_map.198 = (bf16[256,1024]{1,0:T(8,128)(2,1)S(1)}, f32[1,1024]{1,0:T(1,128)S(1)}, f32[128,1024]{1,0:T(8,128)S(1)}, bf16[128,1024]{1,0:T(8,128)(2,1)S(1)}) custom-call(bf16[256,1024]{1,0:T(8,128)(2,1)S(1)} %get-tuple-element.88.own_ref, bf16[256,1024]{1,0:T(8,128)(2,1)S(1)} %collective-permute-done.15.got_ref, bf16[512,1024]{1,0:T(8,128)(2,1)S(1)} %copy-done, ...), custom_call_target="tpu_custom_call" | custom-call | flops 1073741824 | bytes 7606272 | tf_op jit(solution)/shard_map/pallas_call | solution.py:286
  102.0 1.5 collective-permute-start.38
  103.6 1.3 collective-permute-start.35
  104.9 14.5 %collective-permute-done.28 = bf16[256,1280]{1,0:T(8,128)(2,1)S(1)} collective-permute-done((bf16[256,1280]{1,0:T(8,128)(2,1)S(1)}, bf16[256,1280]{1,0:T(8,128)(2,1)S(1)}, u32[]{:S(2)}, u32[]{:S(2)}) %collective-permute-start.28) | collective-permute-done | bytes 655392 | tf_op jit(solution)/shard_map/ppermute | solution.py:438
  120.0 5.0 %collective-permute-done.38.r_3_ = bf16[256,512]{1,0:T(8,128)(2,1)S(1)} collective-permute-done((bf16[256,512]{1,0:T(8,128)(2,1)S(1)}, bf16[256,512]{1,0:T(8,128)(2,1)S(1)}, u32[]{:S(2)}, u32[]{:S(2)}) %collective-permute-start.38) | collective-permute-done | bytes 262176 | tf_op jit(solution)/shard_map/ppermute | solution.py:438
  125.0 1.4 shard_map.204
  127.2 1.4 collective-permute-start.40
  130.3 4.8 %collective-permute-done.35.r_4_ = bf16[256,1024]{1,0:T(8,128)(2,1)S(1)} collective-permute-done((bf16[256,1024]{1,0:T(8,128)(2,1)S(1)}, bf16[256,1024]{1,0:T(8,128)(2,1)S(1)}, u32[]{:S(2)}, u32[]{:S(2)}) %collective-permute-start.35) | collective-permute-done | bytes 524320 | tf_op jit(solution)/shard_map/ppermute | solution.py:438
  135.1 1.4 shard_map.203
  137.4 1.4 collective-permute-start.36
  139.5 1.7 pack_message.1.r_1_.r_4_
  141.2 2.1 collective-permute-start.21
  143.2 1.4 collective-permute-start.22
  145.4 1.1 fusion.18
  146.5 1.6 collective-permute-start.27
  148.0 1.2 convert_add_fusion
  150.5 2.6 %query_grads.1 = (bf16[256,256]{1,0:T(8,128)(2,1)S(1)}, f32[1,256]{1,0:T(1,128)S(1)}) custom-call(bf16[256,256]{1,0:T(8,128)(2,1)S(1)} %copy-done.20, bf16[288,256]{1,0:T(8,128)(2,1)S(1)} %pack_message.1.r_1_.r_4_, bf16[256,256]{1,0:T(8,128)(2,1)S(1)} %get-tuple-element.82.r_4_.r_2_, f32[4,256]{1,0:T(4,128)S(1)} %copy-done.29, ...), custom_call_target="tpu_custom_call" | custom-call | flops 1610612736 | bytes 1572864 | tf_op jit(solution)/shard_map/query_grads/pallas_call | solution.py:210
  153.0 1.2 collective-permute-done.21.r_5_
  154.2 1.5 collective-permute-start.29
  155.7 4.1 %collective-permute-start.23 = (bf16[288,256]{1,0:T(8,128)(2,1)S(1)}, bf16[288,256]{1,0:T(8,128)(2,1)S(1)}, u32[]{:S(2)}, u32[]{:S(2)}) collective-permute-start(bf16[288,256]{1,0:T(8,128)(2,1)S(1)} %collective-permute-done.21.r_5_), channel_id=1, source_target_pairs={{0,4},{4,0},{8,12},{12,8},{1,5},{5,1},{9,13},{13,9},{2,6},{6,2},{1... | collective-permute-start | bytes 442376 | tf_op jit(solution)/shard_map/ppermute | solution.py:438
  159.9 1.2 convert_add_fusion.1
  162.7 2.9 %collective-permute-start.37 = (bf16[1,128,1024]{2,1,0:T(8,128)(2,1)}, bf16[1,128,1024]{2,1,0:T(8,128)(2,1)}, u32[]{:S(2)}, u32[]{:S(2)}) collective-permute-start(bf16[1,128,1024]{2,1,0:T(8,128)(2,1)} %dynamic-slice_convert_fusion.1), channel_id=1, source_target_pairs={{0,8},{4,12},{8,0},{12,4},{1,9},{5,13},{9,1},{13,5},{2,10},{6,14},... | collective-permute-start | bytes 786440 | tf_op jit(solution)/shard_map/ppermute | solution.py:438
  165.6 1.2 shard_map.201
  168.2 4.0 %key_grads.1 = (bf16[256,512]{1,0:T(8,128)(2,1)S(1)}, f32[1,256]{1,0:T(1,128)S(1)}) custom-call(bf16[256,512]{1,0:T(8,128)(2,1)S(1)} %copy-done.15, bf16[256,256]{1,0:T(8,128)(2,1)S(1)} %copy-done.20, bf16[256,256]{1,0:T(8,128)(2,1)S(1)} %copy-done.22, bf16[512,256]{1,0:T(8,128)(2,1)} %collective-permute-done.20.r_3_, ...), custom_call_target="tpu_custom_call" | custom-call | flops 2147483648 | bytes 1572864 | tf_op jit(solution)/shard_map/key_grads/pallas_call | solution.py:263
  172.2 1.6 collective-permute-start.43
  174.3 2.5 %shard_map.200 = (f32[128,1024]{1,0:T(8,128)S(1)}, bf16[128,1024]{1,0:T(8,128)(2,1)}) custom-call(bf16[256,256]{1,0:T(8,128)(2,1)S(1)} %get-tuple-element.84.dq_ref.r_6_, bf16[256,512]{1,0:T(8,128)(2,1)S(1)} %get-tuple-element.85.dkv_ref.r_2_, bf16[512,512]{1,0:T(8,128)(2,1)S(1)} %pad_maximum_fusion.1.r_1_.r_2_.qo_ref, ...), custom_call_target="tpu_custom_call" | custom-call | flops 402653184 | bytes 3276800 | tf_op jit(solution)/shard_map/pallas_call | solution.py:286
  176.8 3.2 %collective-permute-done.41 = bf16[1,128,1024]{2,1,0:T(8,128)(2,1)S(1)} collective-permute-done((bf16[1,128,1024]{2,1,0:T(8,128)(2,1)S(1)}, bf16[1,128,1024]{2,1,0:T(8,128)(2,1)S(1)}, u32[]{:S(2)}, u32[]{:S(2)}) %collective-permute-start.41) | collective-permute-done | bytes 262176 | tf_op jit(solution)/shard_map/ppermute | solution.py:438
  181.3 3.8 %collective-permute-done.44 = f32[60,128]{1,0:T(8,128)S(1)} collective-permute-done((f32[60,128]{1,0:T(8,128)S(1)}, f32[60,128]{1,0:T(8,128)S(1)}, u32[]{:S(2)}, u32[]{:S(2)}) %collective-permute-start.44) | collective-permute-done | bytes 30752 | tf_op jit(solution)/shard_map/ppermute | solution.py:438
  186.3 3.7 %collective-permute-done.45 = f32[60,128]{1,0:T(8,128)S(1)} collective-permute-done((f32[60,128]{1,0:T(8,128)S(1)}, f32[60,128]{1,0:T(8,128)S(1)}, u32[]{:S(2)}, u32[]{:S(2)}) %collective-permute-start.45) | collective-permute-done | bytes 30752 | tf_op jit(solution)/shard_map/ppermute | solution.py:438
  193.1 1.8 add_bitcast_fusion.1
  196.6 1.9 collective-permute-start.33
  200.0 3.6 %collective-permute-done.31 = bf16[1,128,512]{2,1,0:T(8,128)(2,1)S(1)} collective-permute-done((bf16[1,128,512]{2,1,0:T(8,128)(2,1)S(1)}, bf16[1,128,512]{2,1,0:T(8,128)(2,1)S(1)}, u32[]{:S(2)}, u32[]{:S(2)}) %collective-permute-start.31) | collective-permute-done | bytes 131104 | tf_op jit(solution)/shard_map/ppermute | solution.py:438
  204.3 1.9 collective-permute-done.33
  206.3 1.3 collective-permute-start.34
  207.8 6.1 %collective-permute-done.34 = bf16[1,128,512]{2,1,0:T(8,128)(2,1)S(1)} collective-permute-done((bf16[1,128,512]{2,1,0:T(8,128)(2,1)S(1)}, bf16[1,128,512]{2,1,0:T(8,128)(2,1)S(1)}, u32[]{:S(2)}, u32[]{:S(2)}) %collective-permute-start.34) | collective-permute-done | bytes 131104 | tf_op jit(solution)/shard_map/ppermute | solution.py:438
  (223 shorter events, 36.3 us)
Async XLA Ops:
  1.8 15.9 %collective-permute-start.1 = (bf16[512,512]{1,0:T(8,128)(2,1)S(1)}, bf16[512,512]{1,0:T(8,128)(2,1)}, u32[]{:S(2)}, u32[]{:S(2)}) collective-permute-start(bf16[512,512]{1,0:T(8,128)(2,1)S(1)} %bitcast.65), channel_id=1, source_target_pairs={{0,16},{16,0},{1,17},{17,1},{2,18},{18,2},{3,19},{19,3},{4,20},{20... | collective-permute-start | bytes 1572872 | tf_op jit(solution)/shard_map/ppermute | solution.py:438
  5.9 27.5 %collective-permute-start = (bf16[512,512]{1,0:T(8,128)(2,1)S(1)}, bf16[512,512]{1,0:T(8,128)(2,1)}, u32[]{:S(2)}, u32[]{:S(2)}) collective-permute-start(bf16[512,512]{1,0:T(8,128)(2,1)S(1)} %pad_maximum_fusion.1.r_1_.r_2_.qo_ref), channel_id=1, source_target_pairs={{0,16},{16,0},{1,17},{17,1},{2,18},{18,2},{3,19},{19,3},{4,20},{20... | collective-permute-start | bytes 1572872 | tf_op jit(solution)/shard_map/ppermute | solution.py:438
  6.1 69.7 %collective-permute-start.8 = (bf16[512,1024]{1,0:T(8,128)(2,1)S(1)}, bf16[512,1024]{1,0:T(8,128)(2,1)}, u32[]{:S(2)}, u32[]{:S(2)}) collective-permute-start(bf16[512,1024]{1,0:T(8,128)(2,1)S(1)} %copy-done.1), channel_id=1, source_target_pairs={{0,16},{16,0},{1,17},{17,1},{2,18},{18,2},{3,19},{19,3},{4,20},{20... | collective-permute-start | bytes 3145736 | tf_op jit(solution)/shard_map/ppermute | solution.py:438
  8.7 47.5 %collective-permute-start.9 = (bf16[128,1024]{1,0:T(8,128)(2,1)}, bf16[128,1024]{1,0:T(8,128)(2,1)}, u32[]{:S(2)}, u32[]{:S(2)}) collective-permute-start(bf16[128,1024]{1,0:T(8,128)(2,1)} %constant_dynamic-slice_fusion.4), channel_id=1, source_target_pairs={{0,16},{16,0},{1,17},{17,1},{2,18},{18,2},{3,19},{19,3},{4,20},{20... | collective-permute-start | bytes 786440 | tf_op jit(solution)/shard_map/ppermute | solution.py:438
  17.3 16.0 %copy-start.41 = (f32[2,1024]{1,0:T(2,128)S(1)}, f32[2,1024]{1,0:T(2,128)}, u32[]{:S(2)}) copy-start(f32[2,1024]{1,0:T(2,128)} %param.18) | copy-start | bytes 24580
  19.1 24.2 %copy-start.14 = (bf16[256,512]{1,0:T(8,128)(2,1)}, bf16[256,512]{1,0:T(8,128)(2,1)S(1)}, u32[]{:S(2)}) copy-start(bf16[256,512]{1,0:T(8,128)(2,1)S(1)} %fusion.1.r_3_.r_4_.r_0_) | copy-start | bytes 786436
  19.1 13.7 %collective-permute-start.2 = (bf16[256,512]{1,0:T(8,128)(2,1)S(1)}, bf16[256,512]{1,0:T(8,128)(2,1)S(1)}, u32[]{:S(2)}, u32[]{:S(2)}) collective-permute-start(bf16[256,512]{1,0:T(8,128)(2,1)S(1)} %fusion.1.r_3_.r_4_.r_0_), channel_id=1, source_target_pairs={{0,8},{4,12},{8,0},{12,4},{1,9},{5,13},{9,1},{13,5},{2,10},{6,14},... | collective-permute-start | bytes 786440 | tf_op jit(solution)/shard_map/ppermute | solution.py:438
  22.3 12.3 %collective-permute-start.3 = (bf16[256,512]{1,0:T(8,128)(2,1)S(1)}, bf16[256,512]{1,0:T(8,128)(2,1)S(1)}, u32[]{:S(2)}, u32[]{:S(2)}) collective-permute-start(bf16[256,512]{1,0:T(8,128)(2,1)S(1)} %fusion.1.r_3_.r_4_.r_0_), channel_id=1, source_target_pairs={{0,4},{4,0},{8,12},{12,8},{1,5},{5,1},{9,13},{13,9},{2,6},{6,2},{1... | collective-permute-start | bytes 786440 | tf_op jit(solution)/shard_map/ppermute | solution.py:438
  32.8 10.5 %copy-start.30 = (bf16[256,512]{1,0:T(8,128)(2,1)}, bf16[256,512]{1,0:T(8,128)(2,1)S(1)}, u32[]{:S(2)}) copy-start(bf16[256,512]{1,0:T(8,128)(2,1)S(1)} %collective-permute-done.2.r_4_.r_5_) | copy-start | bytes 786436
  32.8 7.1 %collective-permute-start.4 = (bf16[256,512]{1,0:T(8,128)(2,1)S(1)}, bf16[256,512]{1,0:T(8,128)(2,1)S(1)}, u32[]{:S(2)}, u32[]{:S(2)}) collective-permute-start(bf16[256,512]{1,0:T(8,128)(2,1)S(1)} %collective-permute-done.2.r_4_.r_5_), channel_id=1, source_target_pairs={{0,4},{4,0},{8,12},{12,8},{1,5},{5,1},{9,13},{13,9},{2,6},{6,2},{1... | collective-permute-start | bytes 786440 | tf_op jit(solution)/shard_map/ppermute | solution.py:438
  34.6 8.7 %copy-start.18 = (bf16[256,256]{1,0:T(8,128)(2,1)}, bf16[256,256]{1,0:T(8,128)(2,1)S(1)}, u32[]{:S(2)}) copy-start(bf16[256,256]{1,0:T(8,128)(2,1)S(1)} %fusion.4.r_0_.r_1_) | copy-start | bytes 393220
  34.6 8.7 %copy-start.32 = (bf16[256,512]{1,0:T(8,128)(2,1)}, bf16[256,512]{1,0:T(8,128)(2,1)S(1)}, u32[]{:S(2)}) copy-start(bf16[256,512]{1,0:T(8,128)(2,1)S(1)} %collective-permute-done.3.r_5_.r_6_) | copy-start | bytes 786436
  43.3 1.6 collective-permute-start.5
  45.0 14.1 %collective-permute-start.6 = (bf16[128,1024]{1,0:T(8,128)(2,1)S(1)}, bf16[128,1024]{1,0:T(8,128)(2,1)S(1)}, u32[]{:S(2)}, u32[]{:S(2)}) collective-permute-start(bf16[128,1024]{1,0:T(8,128)(2,1)S(1)} %add_convert_fusion.4.sent_ref), channel_id=1, source_target_pairs={{0,2},{1,3},{2,0},{3,1},{4,6},{5,7},{6,4},{7,5},{8,10},{9,11},{10,... | collective-permute-start | bytes 786440 | tf_op jit(solution)/shard_map/ppermute | solution.py:438
  56.2 14.4 %collective-permute-start.10 = (bf16[128,1024]{1,0:T(8,128)(2,1)}, bf16[128,1024]{1,0:T(8,128)(2,1)}, u32[]{:S(2)}, u32[]{:S(2)}) collective-permute-start(bf16[128,1024]{1,0:T(8,128)(2,1)} %collective-permute-done.9.refs_0_), channel_id=1, source_target_pairs={{0,8},{4,12},{8,0},{12,4},{1,9},{5,13},{9,1},{13,5},{2,10},{6,14},... | collective-permute-start | bytes 786440 | tf_op jit(solution)/shard_map/ppermute | solution.py:438
  62.3 13.5 %collective-permute-start.7 = (bf16[128,1024]{1,0:T(8,128)(2,1)}, bf16[128,1024]{1,0:T(8,128)(2,1)}, u32[]{:S(2)}, u32[]{:S(2)}) collective-permute-start(bf16[128,1024]{1,0:T(8,128)(2,1)} %get-tuple-element.68.own_ref), channel_id=1, source_target_pairs={{0,1},{1,0},{2,3},{3,2},{4,5},{5,4},{6,7},{7,6},{8,9},{9,8},{10,11... | collective-permute-start | bytes 786440 | tf_op jit(solution)/shard_map/ppermute | solution.py:438
  63.0 9.2 %copy-start.19 = (bf16[256,256]{1,0:T(8,128)(2,1)S(1)}, bf16[256,256]{1,0:T(8,128)(2,1)}, u32[]{:S(2)}) copy-start(bf16[256,256]{1,0:T(8,128)(2,1)} %copy-done.18) | copy-start | bytes 393220
  63.0 12.7 %copy-start.27 = (f32[1024]{0:T(1024)S(1)}, f32[1024]{0:T(1024)}, u32[]{:S(2)}) copy-start(f32[1024]{0:T(1024)} %param.17) | copy-start | bytes 12292
  63.0 14.9 %collective-permute-start.11 = (bf16[128,1024]{1,0:T(8,128)(2,1)}, bf16[128,1024]{1,0:T(8,128)(2,1)S(1)}, u32[]{:S(2)}, u32[]{:S(2)}) collective-permute-start(bf16[128,1024]{1,0:T(8,128)(2,1)} %collective-permute-done.9.refs_0_), channel_id=1, source_target_pairs={{0,4},{4,0},{8,12},{12,8},{1,5},{5,1},{9,13},{13,9},{2,6},{6,2},{1... | collective-permute-start | bytes 786440 | tf_op jit(solution)/shard_map/ppermute | solution.py:438
  70.6 13.8 %collective-permute-start.12 = (bf16[128,1024]{1,0:T(8,128)(2,1)}, bf16[128,1024]{1,0:T(8,128)(2,1)S(1)}, u32[]{:S(2)}, u32[]{:S(2)}) collective-permute-start(bf16[128,1024]{1,0:T(8,128)(2,1)} %collective-permute-done.10.refs_1_), channel_id=1, source_target_pairs={{0,4},{4,0},{8,12},{12,8},{1,5},{5,1},{9,13},{13,9},{2,6},{6,2},{1... | collective-permute-start | bytes 786440 | tf_op jit(solution)/shard_map/ppermute | solution.py:438
  72.3 14.2 %collective-permute-start.19 = (bf16[256,256]{1,0:T(8,128)(2,1)S(1)}, bf16[256,256]{1,0:T(8,128)(2,1)S(1)}, u32[]{:S(2)}, u32[]{:S(2)}) collective-permute-start(bf16[256,256]{1,0:T(8,128)(2,1)S(1)} %copy-done.19), channel_id=1, source_target_pairs={{0,8},{4,12},{8,0},{12,4},{1,9},{5,13},{9,1},{13,5},{2,10},{6,14},... | collective-permute-start | bytes 393224 | tf_op jit(solution)/shard_map/ppermute | solution.py:438
  86.2 1.6 collective-permute-start.13
  87.2 80.3 %collective-permute-start.20 = (bf16[512,256]{1,0:T(8,128)(2,1)}, bf16[512,256]{1,0:T(8,128)(2,1)}, u32[]{:S(2)}, u32[]{:S(2)}) collective-permute-start(bf16[512,256]{1,0:T(8,128)(2,1)} %pad_maximum_fusion.4), channel_id=1, source_target_pairs={{0,4},{4,0},{8,12},{12,8},{1,5},{5,1},{9,13},{13,9},{2,6},{6,2},{1... | collective-permute-start | bytes 786440 | tf_op jit(solution)/shard_map/ppermute | solution.py:438
  87.8 8.5 %copy-start.9 = (f32[128,1024]{1,0:T(8,128)S(1)}, f32[128,1024]{1,0:T(8,128)}, u32[]{:S(2)}) copy-start(f32[128,1024]{1,0:T(8,128)} %copy-done.8) | copy-start | bytes 1572868
  87.8 8.5 %copy-start.24 = (f32[2,1024]{1,0:T(2,128)S(1)}, f32[2,1024]{1,0:T(2,128)}, u32[]{:S(2)}) copy-start(f32[2,1024]{1,0:T(2,128)} %copy-done.23) | copy-start | bytes 24580
  87.9 8.4 %collective-permute-start.14 = (bf16[128,1024]{1,0:T(8,128)(2,1)S(1)}, bf16[128,1024]{1,0:T(8,128)(2,1)S(1)}, u32[]{:S(2)}, u32[]{:S(2)}) collective-permute-start(bf16[128,1024]{1,0:T(8,128)(2,1)S(1)} %add_convert_fusion.3.sent_ref), channel_id=1, source_target_pairs={{0,2},{1,3},{2,0},{3,1},{4,6},{5,7},{6,4},{7,5},{8,10},{9,11},{10,... | collective-permute-start | bytes 786440 | tf_op jit(solution)/shard_map/ppermute | solution.py:438
  90.5 6.5 %copy-start.38 = (bf16[256,512]{1,0:T(8,128)(2,1)S(1)}, bf16[256,512]{1,0:T(8,128)(2,1)}, u32[]{:S(2)}) copy-start(bf16[256,512]{1,0:T(8,128)(2,1)} %get-tuple-element.129) | copy-start | bytes 786436
  90.5 29.6 %collective-permute-start.39 = (bf16[256,1024]{1,0:T(8,128)(2,1)S(1)}, bf16[256,1024]{1,0:T(8,128)(2,1)S(1)}, u32[]{:S(2)}, u32[]{:S(2)}) collective-permute-start(bf16[256,1024]{1,0:T(8,128)(2,1)S(1)} %get-tuple-element.69.act_ref.r_2_), channel_id=1, source_target_pairs={{0,16},{16,0},{1,17},{17,1},{2,18},{18,2},{3,19},{19,3},{4,20},{20... | collective-permute-start | bytes 1572872 | tf_op jit(solution)/shard_map/ppermute | solution.py:438
  96.9 2.0 collective-permute-start.15
  97.0 22.4 %collective-permute-start.28 = (bf16[256,1280]{1,0:T(8,128)(2,1)S(1)}, bf16[256,1280]{1,0:T(8,128)(2,1)S(1)}, u32[]{:S(2)}, u32[]{:S(2)}) collective-permute-start(bf16[256,1280]{1,0:T(8,128)(2,1)S(1)} %pad_maximum_fusion), channel_id=1, source_target_pairs={{0,16},{16,0},{1,17},{17,1},{2,18},{18,2},{3,19},{19,3},{4,20},{20... | collective-permute-start | bytes 1966088 | tf_op jit(solution)/shard_map/ppermute | solution.py:438
  101.8 1.8 collective-permute-start.16
  102.0 23.0 %collective-permute-start.38 = (bf16[256,512]{1,0:T(8,128)(2,1)S(1)}, bf16[256,512]{1,0:T(8,128)(2,1)S(1)}, u32[]{:S(2)}, u32[]{:S(2)}) collective-permute-start(bf16[256,512]{1,0:T(8,128)(2,1)S(1)} %pad_maximum_fusion.7), channel_id=1, source_target_pairs={{0,16},{16,0},{1,17},{17,1},{2,18},{18,2},{3,19},{19,3},{4,20},{20... | collective-permute-start | bytes 786440 | tf_op jit(solution)/shard_map/ppermute | solution.py:438
  103.6 31.6 %collective-permute-start.35 = (bf16[256,1024]{1,0:T(8,128)(2,1)S(1)}, bf16[256,1024]{1,0:T(8,128)(2,1)S(1)}, u32[]{:S(2)}, u32[]{:S(2)}) collective-permute-start(bf16[256,1024]{1,0:T(8,128)(2,1)S(1)} %get-tuple-element.103.r_2_), channel_id=1, source_target_pairs={{0,16},{16,0},{1,17},{17,1},{2,18},{18,2},{3,19},{19,3},{4,20},{20... | collective-permute-start | bytes 1572872 | tf_op jit(solution)/shard_map/ppermute | solution.py:438
  119.4 9.2 %collective-permute-start.17 = (bf16[128,1024]{1,0:T(8,128)(2,1)S(1)}, bf16[128,1024]{1,0:T(8,128)(2,1)S(1)}, u32[]{:S(2)}, u32[]{:S(2)}) collective-permute-start(bf16[128,1024]{1,0:T(8,128)(2,1)S(1)} %add_convert_fusion.2.sent_ref), channel_id=1, source_target_pairs={{0,2},{1,3},{2,0},{3,1},{4,6},{5,7},{6,4},{7,5},{8,10},{9,11},{10,... | collective-permute-start | bytes 786440 | tf_op jit(solution)/shard_map/ppermute | solution.py:438
  120.0 8.6 %copy-start.7 = (f32[128,1024]{1,0:T(8,128)S(1)}, f32[128,1024]{1,0:T(8,128)}, u32[]{:S(2)}) copy-start(f32[128,1024]{1,0:T(8,128)} %copy-done.6) | copy-start | bytes 1572868
  120.0 8.6 %copy-start.26 = (f32[128,128]{1,0:T(8,128)S(1)}, f32[128,128]{1,0:T(8,128)}, u32[]{:S(2)}) copy-start(f32[128,128]{1,0:T(8,128)} %copy-done.25) | copy-start | bytes 196612
  127.2 17.4 %collective-permute-start.40 = (bf16[2,128,1024]{2,1,0:T(8,128)(2,1)}, bf16[2,128,1024]{2,1,0:T(8,128)(2,1)}, u32[]{:S(2)}, u32[]{:S(2)}) collective-permute-start(bf16[2,128,1024]{2,1,0:T(8,128)(2,1)} %get-tuple-element.110), channel_id=1, source_target_pairs={{0,4},{4,0},{8,12},{12,8},{1,5},{5,1},{9,13},{13,9},{2,6},{6,2},{1... | collective-permute-start | bytes 1572872 | tf_op jit(solution)/shard_map/ppermute | solution.py:438
  129.0 9.7 %collective-permute-start.42 = (f32[6,1024]{1,0:T(8,128)S(1)}, f32[6,1024]{1,0:T(8,128)S(1)}, u32[]{:S(2)}, u32[]{:S(2)}) collective-permute-start(f32[6,1024]{1,0:T(8,128)S(1)} %pad_maximum_fusion.8), channel_id=1, source_target_pairs={{0,1},{1,0},{2,3},{3,2},{4,5},{5,4},{6,7},{7,6},{8,9},{9,8},{10,11... | collective-permute-start | bytes 73736 | tf_op jit(solution)/shard_map/ppermute | solution.py:438
  129.1 10.3 %collective-permute-start.18 = (bf16[128,1024]{1,0:T(8,128)(2,1)S(1)}, bf16[128,1024]{1,0:T(8,128)(2,1)S(1)}, u32[]{:S(2)}, u32[]{:S(2)}) collective-permute-start(bf16[128,1024]{1,0:T(8,128)(2,1)S(1)} %get-tuple-element.81.r_0_), channel_id=1, source_target_pairs={{0,1},{1,0},{2,3},{3,2},{4,5},{5,4},{6,7},{7,6},{8,9},{9,8},{10,11... | collective-permute-start | bytes 786440 | tf_op jit(solution)/shard_map/ppermute | solution.py:438
  137.4 18.4 %collective-permute-start.36 = (bf16[2,128,1024]{2,1,0:T(8,128)(2,1)}, bf16[2,128,1024]{2,1,0:T(8,128)(2,1)}, u32[]{:S(2)}, u32[]{:S(2)}) collective-permute-start(bf16[2,128,1024]{2,1,0:T(8,128)(2,1)} %get-tuple-element.104), channel_id=1, source_target_pairs={{0,4},{4,0},{8,12},{12,8},{1,5},{5,1},{9,13},{13,9},{2,6},{6,2},{1... | collective-permute-start | bytes 1572872 | tf_op jit(solution)/shard_map/ppermute | solution.py:438
  141.2 6.9 %copy-start.11 = (bf16[2,128,1024]{2,1,0:T(8,128)(2,1)S(1)}, bf16[2,128,1024]{2,1,0:T(8,128)(2,1)}, u32[]{:S(2)}) copy-start(bf16[2,128,1024]{2,1,0:T(8,128)(2,1)} %copy-done.10) | copy-start | bytes 1572868
  141.2 13.1 %collective-permute-start.21 = (bf16[288,256]{1,0:T(8,128)(2,1)S(1)}, bf16[288,256]{1,0:T(8,128)(2,1)S(1)}, u32[]{:S(2)}, u32[]{:S(2)}) collective-permute-start(bf16[288,256]{1,0:T(8,128)(2,1)S(1)} %pack_message.1.r_1_.r_4_), channel_id=1, source_target_pairs={{0,8},{4,12},{8,0},{12,4},{1,9},{5,13},{9,1},{13,5},{2,10},{6,14},... | collective-permute-start | bytes 442376 | tf_op jit(solution)/shard_map/ppermute | solution.py:438
  143.2 24.9 %collective-permute-start.22 = (bf16[288,256]{1,0:T(8,128)(2,1)S(1)}, bf16[288,256]{1,0:T(8,128)(2,1)S(1)}, u32[]{:S(2)}, u32[]{:S(2)}) collective-permute-start(bf16[288,256]{1,0:T(8,128)(2,1)S(1)} %pack_message.1.r_1_.r_4_), channel_id=1, source_target_pairs={{0,4},{4,0},{8,12},{12,8},{1,5},{5,1},{9,13},{13,9},{2,6},{6,2},{1... | collective-permute-start | bytes 442376 | tf_op jit(solution)/shard_map/ppermute | solution.py:438
  146.5 16.2 %collective-permute-start.27 = (bf16[256,512]{1,0:T(8,128)(2,1)S(1)}, bf16[256,512]{1,0:T(8,128)(2,1)S(1)}, u32[]{:S(2)}, u32[]{:S(2)}) collective-permute-start(bf16[256,512]{1,0:T(8,128)(2,1)S(1)} %get-tuple-element.127), channel_id=1, source_target_pairs={{0,16},{16,0},{1,17},{17,1},{2,18},{18,2},{3,19},{19,3},{4,20},{20... | collective-permute-start | bytes 786440 | tf_op jit(solution)/shard_map/ppermute | solution.py:438
  150.5 9.4 %copy-start.13 = (bf16[2,128,1024]{2,1,0:T(8,128)(2,1)S(1)}, bf16[2,128,1024]{2,1,0:T(8,128)(2,1)}, u32[]{:S(2)}) copy-start(bf16[2,128,1024]{2,1,0:T(8,128)(2,1)} %copy-done.12) | copy-start | bytes 1572868
  154.2 8.5 %collective-permute-start.29 = (bf16[256,256]{1,0:T(8,128)(2,1)S(1)}, bf16[256,256]{1,0:T(8,128)(2,1)S(1)}, u32[]{:S(2)}, u32[]{:S(2)}) collective-permute-start(bf16[256,256]{1,0:T(8,128)(2,1)S(1)} %get-tuple-element.84.dq_ref.r_6_), channel_id=1, source_target_pairs={{0,16},{16,0},{1,17},{17,1},{2,18},{18,2},{3,19},{19,3},{4,20},{20... | collective-permute-start | bytes 393224 | tf_op jit(solution)/shard_map/ppermute | solution.py:438
  155.7 12.5 %collective-permute-start.23 = (bf16[288,256]{1,0:T(8,128)(2,1)S(1)}, bf16[288,256]{1,0:T(8,128)(2,1)S(1)}, u32[]{:S(2)}, u32[]{:S(2)}) collective-permute-start(bf16[288,256]{1,0:T(8,128)(2,1)S(1)} %collective-permute-done.21.r_5_), channel_id=1, source_target_pairs={{0,4},{4,0},{8,12},{12,8},{1,5},{5,1},{9,13},{13,9},{2,6},{6,2},{1... | collective-permute-start | bytes 442376 | tf_op jit(solution)/shard_map/ppermute | solution.py:438
  162.7 17.3 %collective-permute-start.41 = (bf16[1,128,1024]{2,1,0:T(8,128)(2,1)S(1)}, bf16[1,128,1024]{2,1,0:T(8,128)(2,1)S(1)}, u32[]{:S(2)}, u32[]{:S(2)}) collective-permute-start(bf16[1,128,1024]{2,1,0:T(8,128)(2,1)S(1)} %dynamic-slice_convert_fusion), channel_id=1, source_target_pairs={{0,8},{4,12},{8,0},{12,4},{1,9},{5,13},{9,1},{13,5},{2,10},{6,14},... | collective-permute-start | bytes 786440 | tf_op jit(solution)/shard_map/ppermute | solution.py:438
  162.7 30.4 %collective-permute-start.37 = (bf16[1,128,1024]{2,1,0:T(8,128)(2,1)}, bf16[1,128,1024]{2,1,0:T(8,128)(2,1)}, u32[]{:S(2)}, u32[]{:S(2)}) collective-permute-start(bf16[1,128,1024]{2,1,0:T(8,128)(2,1)} %dynamic-slice_convert_fusion.1), channel_id=1, source_target_pairs={{0,8},{4,12},{8,0},{12,4},{1,9},{5,13},{9,1},{13,5},{2,10},{6,14},... | collective-permute-start | bytes 786440 | tf_op jit(solution)/shard_map/ppermute | solution.py:438
  167.5 27.4 %collective-permute-start.30 = (bf16[2,128,512]{2,1,0:T(8,128)(2,1)}, bf16[2,128,512]{2,1,0:T(8,128)(2,1)}, u32[]{:S(2)}, u32[]{:S(2)}) collective-permute-start(bf16[2,128,512]{2,1,0:T(8,128)(2,1)} %get-tuple-element.91), channel_id=1, source_target_pairs={{0,4},{4,0},{8,12},{12,8},{1,5},{5,1},{9,13},{13,9},{2,6},{6,2},{1... | collective-permute-start | bytes 786440 | tf_op jit(solution)/shard_map/ppermute | solution.py:438
  172.2 8.9 %collective-permute-start.43 = (f32[60,128]{1,0:T(8,128)S(1)}, f32[60,128]{1,0:T(8,128)S(1)}, u32[]{:S(2)}, u32[]{:S(2)}) collective-permute-start(f32[60,128]{1,0:T(8,128)S(1)} %maximum_bitcast_fusion), channel_id=1, source_target_pairs={{0,16},{16,0},{1,17},{17,1},{2,18},{18,2},{3,19},{19,3},{4,20},{20... | collective-permute-start | bytes 92168 | tf_op jit(solution)/shard_map/ppermute | solution.py:438
  173.7 6.3 %copy-start.5 = (bf16[256,1024]{1,0:T(8,128)(2,1)S(1)}, bf16[256,1024]{1,0:T(8,128)(2,1)}, u32[]{:S(2)}) copy-start(bf16[256,1024]{1,0:T(8,128)(2,1)} %copy-done.4) | copy-start | bytes 1572868
  173.8 6.3 %copy-start.3 = (bf16[256,1024]{1,0:T(8,128)(2,1)S(1)}, bf16[256,1024]{1,0:T(8,128)(2,1)}, u32[]{:S(2)}) copy-start(bf16[256,1024]{1,0:T(8,128)(2,1)} %copy-done.2) | copy-start | bytes 1572868
  173.8 22.3 %collective-permute-start.32 = (bf16[256,512]{1,0:T(8,128)(2,1)S(1)}, bf16[256,512]{1,0:T(8,128)(2,1)S(1)}, u32[]{:S(2)}, u32[]{:S(2)}) collective-permute-start(bf16[256,512]{1,0:T(8,128)(2,1)S(1)} %get-tuple-element.85.dkv_ref.r_2_), channel_id=1, source_target_pairs={{0,16},{16,0},{1,17},{17,1},{2,18},{18,2},{3,19},{19,3},{4,20},{20... | collective-permute-start | bytes 786440 | tf_op jit(solution)/shard_map/ppermute | solution.py:438
  180.0 18.5 %collective-permute-start.24 = (bf16[128,1024]{1,0:T(8,128)(2,1)}, bf16[128,1024]{1,0:T(8,128)(2,1)}, u32[]{:S(2)}, u32[]{:S(2)}) collective-permute-start(bf16[128,1024]{1,0:T(8,128)(2,1)} %get-tuple-element.86), channel_id=1, source_target_pairs={{0,1},{1,0},{2,3},{3,2},{4,5},{5,4},{6,7},{7,6},{8,9},{9,8},{10,11... | collective-permute-start | bytes 786440 | tf_op jit(solution)/shard_map/ppermute | solution.py:438
  181.2 4.0 %collective-permute-start.44 = (f32[60,128]{1,0:T(8,128)S(1)}, f32[60,128]{1,0:T(8,128)S(1)}, u32[]{:S(2)}, u32[]{:S(2)}) collective-permute-start(f32[60,128]{1,0:T(8,128)S(1)} %fusion.8), channel_id=1, source_target_pairs={{0,4},{4,0},{8,12},{12,8},{1,5},{5,1},{9,13},{13,9},{2,6},{6,2},{1... | collective-permute-start | bytes 92168 | tf_op jit(solution)/shard_map/ppermute | solution.py:438
  181.3 11.8 %copy-start.37 = (f32[1,128,1024]{2,1,0:T(8,128)S(1)}, f32[1,128,1024]{2,1,0:T(8,128)}, u32[]{:S(2)}) copy-start(f32[1,128,1024]{2,1,0:T(8,128)} %constant_dynamic-slice_fusion.1) | copy-start | bytes 1572868
  185.2 4.9 %collective-permute-start.45 = (f32[60,128]{1,0:T(8,128)S(1)}, f32[60,128]{1,0:T(8,128)S(1)}, u32[]{:S(2)}, u32[]{:S(2)}) collective-permute-start(f32[60,128]{1,0:T(8,128)S(1)} %fusion.35), channel_id=1, source_target_pairs={{0,8},{4,12},{8,0},{12,4},{1,9},{5,13},{9,1},{13,5},{2,10},{6,14},... | collective-permute-start | bytes 92168 | tf_op jit(solution)/shard_map/ppermute | solution.py:438
  186.3 8.6 %copy-start.17 = (bf16[2,128,512]{2,1,0:T(8,128)(2,1)S(1)}, bf16[2,128,512]{2,1,0:T(8,128)(2,1)}, u32[]{:S(2)}) copy-start(bf16[2,128,512]{2,1,0:T(8,128)(2,1)} %copy-done.16) | copy-start | bytes 786436
  196.0 7.7 %collective-permute-start.31 = (bf16[1,128,512]{2,1,0:T(8,128)(2,1)S(1)}, bf16[1,128,512]{2,1,0:T(8,128)(2,1)S(1)}, u32[]{:S(2)}, u32[]{:S(2)}) collective-permute-start(bf16[1,128,512]{2,1,0:T(8,128)(2,1)S(1)} %dynamic-slice_convert_fusion.3), channel_id=1, source_target_pairs={{0,8},{4,12},{8,0},{12,4},{1,9},{5,13},{9,1},{13,5},{2,10},{6,14},... | collective-permute-start | bytes 393224 | tf_op jit(solution)/shard_map/ppermute | solution.py:438
  196.6 9.6 %collective-permute-start.33 = (bf16[2,128,512]{2,1,0:T(8,128)(2,1)S(1)}, bf16[2,128,512]{2,1,0:T(8,128)(2,1)S(1)}, u32[]{:S(2)}, u32[]{:S(2)}) collective-permute-start(bf16[2,128,512]{2,1,0:T(8,128)(2,1)S(1)} %get-tuple-element.97), channel_id=1, source_target_pairs={{0,4},{4,0},{8,12},{12,8},{1,5},{5,1},{9,13},{13,9},{2,6},{6,2},{1... | collective-permute-start | bytes 786440 | tf_op jit(solution)/shard_map/ppermute | solution.py:438
  199.5 8.2 %collective-permute-start.25 = (bf16[128,1024]{1,0:T(8,128)(2,1)S(1)}, bf16[128,1024]{1,0:T(8,128)(2,1)S(1)}, u32[]{:S(2)}, u32[]{:S(2)}) collective-permute-start(bf16[128,1024]{1,0:T(8,128)(2,1)S(1)} %add_convert_fusion.1), channel_id=1, source_target_pairs={{0,2},{1,3},{2,0},{3,1},{4,6},{5,7},{6,4},{7,5},{8,10},{9,11},{10,... | collective-permute-start | bytes 786440 | tf_op jit(solution)/shard_map/ppermute | solution.py:438
  206.3 7.6 %collective-permute-start.34 = (bf16[1,128,512]{2,1,0:T(8,128)(2,1)S(1)}, bf16[1,128,512]{2,1,0:T(8,128)(2,1)S(1)}, u32[]{:S(2)}, u32[]{:S(2)}) collective-permute-start(bf16[1,128,512]{2,1,0:T(8,128)(2,1)S(1)} %dynamic-slice_convert_fusion.2), channel_id=1, source_target_pairs={{0,8},{4,12},{8,0},{12,4},{1,9},{5,13},{9,1},{13,5},{2,10},{6,14},... | collective-permute-start | bytes 393224 | tf_op jit(solution)/shard_map/ppermute | solution.py:438
  207.7 7.0 %collective-permute-start.26 = (bf16[128,1024]{1,0:T(8,128)(2,1)S(1)}, bf16[128,1024]{1,0:T(8,128)(2,1)S(1)}, u32[]{:S(2)}, u32[]{:S(2)}) collective-permute-start(bf16[128,1024]{1,0:T(8,128)(2,1)S(1)} %add_convert_fusion), channel_id=1, source_target_pairs={{0,1},{1,0},{2,3},{3,2},{4,5},{5,4},{6,7},{7,6},{8,9},{9,8},{10,11... | collective-permute-start | bytes 786440 | tf_op jit(solution)/shard_map/ppermute | solution.py:438
  (27 other events, 71.6 us)
where the time goes:
time: 217 us; the launch traced here: 216 us
  waiting for transfers between devices  88.9 us (41%)
  starting transfers between devices  53.1 us (24%)
  Pallas kernels  27.5 us (13%)
  local copies, waits for them, and re-layouts  24.9 us (11%)
  other arithmetic  16.1 us (7%)
  matrix products  4 us (2%)
    ppermute x46, waiting for transfers between devices, send(): return lax.ppermute(a, axis, [(i, i ^ bit) for i in range(sizes[axis])])  88.9 us
    ppermute x46, starting transfers between devices, send(): return lax.ppermute(a, axis, [(i, i ^ bit) for i in range(sizes[axis])])  53.1 us
    pallas_call x11, Pallas kernels, call(): pl.pallas_call(kernel, out_shape=outs, in_specs=[pl.BlockSpec(memory_spac...  15.9 us
    unnamed x95, local copies, waits for them, and re-layouts  9.41 us
    select_n x7, other arithmetic, turn_d(): jnp.where(far_weight, jnp.concatenate([a[:, half_d:], a[:, :half_d]], 1), a)  5.21 us
  transfers between devices with their start and end apart: 46, of which 20 were waited for; matrix products, arithmetic and copies ran while one was open for 17% of the time, Pallas kernels for 13%

commit v1 on v0

--- a/solution.py
+++ b/solution.py
@@ -67,16 +67,11 @@
     return tile.T[:rows]
 
 
-def halves(refs):
-    cols = refs[0].shape[1] // 2
-    return [r.at[:, pl.ds(0, cols)] for r in refs], [r.at[:, pl.ds(cols, cols)] for r in refs]
-
-
 def attend_kernel(n, heads, *refs):
-    q_ref, near_ref, far_ref, kv_refs = refs[0], refs[1], refs[2], refs[3 : 3 + n]
-    out_ref, lse_ref, keep_ref, sent_ref = refs[3 + n :]
+    q_ref, near_ref, far_ref = refs[:3]
+    k_refs, v_refs = refs[3 : 3 + n], refs[3 + n : 3 + 2 * n]
+    out_ref, lse_ref, keep_ref, sent_ref = refs[3 + 2 * n :]
     q = q_ref[...]
-    k_refs, v_refs = halves(kv_refs)
     out = jnp.zeros(q.shape, F32)
     lses = []
     for h in range(heads):
@@ -103,8 +98,8 @@
     out_kernel(out_ref, near_ref.at[:, weight], far_ref.at[:, weight], keep_ref, sent_ref)
 
 
-def attend(q, near, far, kvs):
-    n, (tokens, cols) = len(kvs), q.shape
+def attend(q, near, far, ks, vs):
+    n, (tokens, cols) = len(ks), q.shape
     width = 2 * near.shape[0]
     heads = cols // HD
     keys = n * tokens
@@ -123,7 +118,7 @@
         ),
         name="attend",
         compiler_params=ROOM,
-    )(q, near, far, *kvs)
+    )(q, near, far, *ks, *vs)
 
 
 def split_rows(rows):
@@ -138,9 +133,10 @@
     return tokens + -(-6 * heads // 16) * 16
 
 
-def pack_kernel(heads, own_ref, got_ref, near_ref, far_ref, at_ref, lse_ref, msg_ref):
+def pack_kernel(heads, own_ref, got_ref, near_ref, far_ref, at_ref, lse_ref, msg_ref, high_ref):
     half = near_ref.shape[0]
     one = jnp.concatenate([own_ref[...], got_ref[...]], axis=0)
+    high_ref[...] = one[:, half:]
     cols = at_ref.shape[1]
     out = pl.ds(near_ref.shape[1] - cols, cols)
     da = dot(one[:, :half], near_ref[:, out], NN) + dot(one[:, half:], far_ref[:, out], NN)
@@ -166,7 +162,10 @@
         raise ValueError("message shape")
     return pl.pallas_call(
         lambda *r: pack_kernel(heads, *r),
-        out_shape=jax.ShapeDtypeStruct((message_rows(tokens, heads), cols), BF),
+        out_shape=(
+            jax.ShapeDtypeStruct((message_rows(tokens, heads), cols), BF),
+            jax.ShapeDtypeStruct((tokens, own.shape[1] // 2), BF),
+        ),
         cost_estimate=pl.CostEstimate(
             flops=2 * tokens * own.shape[1] * cols,
             bytes_accessed=2 * (2 * own.size + near.size + far.size + 2 * attended.size),
@@ -179,8 +178,8 @@
 
 def query_kernel(n, heads, *refs):
     q_ref, da_ref, at_ref, lse_ref = refs[:4]
-    k_refs, v_refs = halves(refs[4 : 4 + n])
-    dq_ref, sum_ref = refs[4 + n :]
+    k_refs, v_refs = refs[4 : 4 + n], refs[4 + n : 4 + 2 * n]
+    dq_ref, sum_ref = refs[4 + 2 * n :]
     q = q_ref[...]
     tokens = q.shape[0]
     da = da_ref[:tokens, :]
@@ -204,9 +203,9 @@
     sum_ref[...] = jnp.sum(out, axis=0, keepdims=True)
 
 
-def query_grads(q, msg, attended, lse, kvs):
-    n, (tokens, cols) = len(kvs), q.shape
-    heads, keys = cols // HD, len(kvs) * q.shape[0]
+def query_grads(q, msg, attended, lse, ks, vs):
+    n, (tokens, cols) = len(ks), q.shape
+    heads, keys = cols // HD, len(ks) * q.shape[0]
     return pl.pallas_call(
         lambda *r: query_kernel(n, heads, *r),
         out_shape=(
@@ -220,20 +219,20 @@
         ),
         name="query_grads",
         compiler_params=ROOM,
-    )(q, msg, attended, lse, *kvs)
+    )(q, msg, attended, lse, *ks, *vs)
 
 
 def key_kernel(m, n, heads, *refs):
-    kv_ref = refs[0]
-    tokens, cols = kv_ref.shape[0], kv_ref.shape[1] // 2
+    k_ref, v_ref = refs[:2]
+    tokens, cols = k_ref.shape
     qs = [
         r.at[pl.ds(i * tokens, tokens)]
-        for r in refs[1 : 1 + m]
+        for r in refs[2 : 2 + m]
         for i in range(r.shape[0] // tokens)
     ]
-    msgs = refs[1 + m : 1 + m + n]
-    out_ref, sum_ref = refs[1 + m + n :]
-    k, v = kv_ref[:, :cols], kv_ref[:, cols:]
+    msgs = refs[2 + m : 2 + m + n]
+    out_ref, sum_ref = refs[2 + m + n :]
+    k, v = k_ref[...], v_ref[...]
     stats = []
     for msg in msgs:
         rows = msg[tokens:, :].astype(F32)
@@ -257,8 +256,8 @@
     sum_ref[...] = jnp.sum(dv, axis=0, keepdims=True)
 
 
-def key_grads(kv, qs, msgs):
-    m, n, tokens, cols = len(qs), len(msgs), kv.shape[0], kv.shape[1] // 2
+def key_grads(k, v, qs, msgs):
+    m, n, (tokens, cols) = len(qs), len(msgs), k.shape
     heads, rows = cols // HD, n * tokens
     return pl.pallas_call(
         lambda *r: key_kernel(m, n, heads, *r),
@@ -273,10 +272,10 @@
         ),
         name="key_grads",
         compiler_params=ROOM,
-    )(kv, *qs, *msgs)
-
-
-def shape(rows, cols, dtype):
+    )(k, v, *qs, *msgs)
+
+
+def arr(rows, cols, dtype):
     return jax.ShapeDtypeStruct((rows, cols), dtype)
 
 
@@ -327,10 +326,14 @@
     own_ref[...] = mixed.astype(BF)
 
 
-def up_kernel(own_ref, got_ref, near_ref, far_ref, bias_ref, pre_ref, act_ref):
+def up_kernel(own_ref, got_ref, x_ref, at_ref, near_ref, far_ref, bias_ref, *outs):
+    pre_ref, act_ref, bundle_ref = outs
     half = near_ref.shape[0]
     mixed = jnp.concatenate([own_ref[...], got_ref[...]], axis=0)
     low, high = mixed[:, :half], mixed[:, half:]
+    bundle_ref[:, :half] = high
+    bundle_ref[:, pl.ds(half, half)] = x_ref[:, pl.ds(half, half)]
+    bundle_ref[:, pl.ds(2 * half, at_ref.shape[1])] = at_ref[...]
     for block in column_blocks(near_ref.shape[1]):
         pre = dot(low, near_ref[:, block], NN) + dot(high, far_ref[:, block], NN)
         pre = pre + bias_ref[:, block]
@@ -385,24 +388,51 @@
     out_kernel(grad_ref, un_ref, uf_ref, keep_ref, sent_ref)
 
 
-def norm_back_kernel(sent_ref, got_ref, two_ref, normed_ref, inverse_ref, gain_ref, *outs):
+def norm_back_kernel(
+    sent_ref, got_ref, two_ref, normed_ref, inverse_ref, gain_ref, sums_ref, *outs
+):
     own_ref, grad_ref, sum_ref = outs
     normed = normed_ref[...]
     mixed = two_ref[...] + (sent_ref[...].astype(F32) + got_ref[...].astype(F32))
     grad = layer_back(mixed * gain_ref[0:1, :], normed, inverse_ref[:, 0:1])
     own_ref[...] = grad.astype(BF)
     grad_ref[...] = grad
-    sum_ref[0:1, :] = jnp.sum(grad, axis=0, keepdims=True)
-    sum_ref[1:2, :] = jnp.sum(mixed * normed, axis=0, keepdims=True)
-    sum_ref[2:3, :] = jnp.sum(mixed, axis=0, keepdims=True)
-
-
-def input_kernel(dq_ref, dkv_ref, qo_ref, qo_far_ref, kv_ref, kv_far_ref, keep_ref, sent_ref):
-    dq, dkv = dq_ref[...], dkv_ref[...]
-    cols, half = dq.shape[1], qo_ref.shape[0]
-    for start, q_ref, k_ref in ((0, qo_ref, kv_ref), (half, qo_far_ref, kv_far_ref)):
+    for i, value in enumerate((grad, mixed * normed, mixed)):
+        sum_ref[2 * i : 2 * i + 1, :] = jnp.sum(value, axis=0, keepdims=True)
+        sum_ref[2 * i + 1 : 2 * i + 2, :] = sums_ref[i : i + 1, :]
+
+
+def sums_kernel(flag_ref, own_ref, got_ref, up_ref, q_ref, v_ref, out_ref):
+    half, cols = own_ref.shape[1] // 2, q_ref.shape[1]
+    rows = own_ref[...] + got_ref[...]
+    turned = jnp.concatenate([rows[:, half:], rows[:, :half]], axis=1)
+    out_ref[0:6, :] = jnp.where(flag_ref[0] == 1, turned, rows)
+    out_ref[6:7, :] = up_ref[...]
+    out_ref[7:8, :] = jnp.zeros((1, 2 * half), F32)
+    out_ref[7:8, pl.ds(0, cols)] = q_ref[...]
+    out_ref[7:8, pl.ds(cols, cols)] = v_ref[...]
+
+
+def unpack_kernel(a_ref, b_ref, head_ref, up_ref, bias_ref, gain_ref, shift_ref):
+    total = a_ref[...] + b_ref[...]
+    cols = head_ref.shape[1]
+    bias_ref[...] = total[0:2]
+    gain_ref[...] = total[2:4]
+    shift_ref[...] = total[4:6]
+    up_ref[...] = total[6:7]
+    head_ref[0:1, :] = total[7:8, :cols]
+    head_ref[1:2, :] = total[7:8, cols : 2 * cols]
+
+
+def input_kernel(dq_ref, dkv_ref, *refs):
+    near, far, (keep_ref, sent_ref) = refs[:3], refs[3:6], refs[6:]
+    dq = dq_ref[...]
+    cols, half = dq.shape[1], near[0].shape[0]
+    dk, dv = dkv_ref[:, :cols], dkv_ref[:, cols:]
+    for start, (q_ref, k_ref, v_ref) in ((0, near), (half, far)):
         for rows in column_blocks(half):
-            value = dot(dq, q_ref[rows, pl.ds(0, cols)], NT) + dot(dkv, k_ref[rows, :], NT)
+            value = dot(dq, q_ref[rows, pl.ds(0, cols)], NT)
+            value = value + dot(dk, k_ref[rows, :], NT) + dot(dv, v_ref[rows, :], NT)
             put_partial(pl.ds(start + rows.start, rows.size), value, keep_ref, sent_ref)
 
 
@@ -412,14 +442,16 @@
     mine = mine_ref[0]
     for i in range(n // 2):
         for out, side in ((away_ref, 1 - mine), (stay_ref, mine)):
-            at = pl.multiple_of((2 * i + side) * rows, rows)
-            col, k = 0, 0
-            for count in terms:
+            at = (2 * i + side) * rows
+            col = 0
+            for group in terms:
                 value = None
-                for _ in range(count):
-                    a, b = ins[k], ins[k + 1]
-                    k += 2
-                    term = dot(a[:, pl.ds(at, rows)], b[...], TN)
+                for pieces, low, b in group:
+                    block = pl.ds(pl.multiple_of(at + low, 128), rows)
+                    a = [ins[k][pl.ds(0, count), block] for k, count in pieces]
+                    a = a[0] if len(a) == 1 else jnp.concatenate(a, axis=0)
+                    where, first, cols = b
+                    term = dot(a, ins[where][:, pl.ds(first, cols)], TN)
                     value = term if value is None else value + term
                 out[i, :, pl.ds(col, value.shape[1])] = value.astype(BF)
                 col += value.shape[1]
@@ -462,28 +494,38 @@
             bit //= 2
         return held
 
-    def owned(products, after):
-        rank = lax.axis_index("ctx")
-        rows = products[0][0][0].shape[1] // nc
-        cols = sum(p[0][1].shape[1] for p in products)
-        mine = jnp.bitwise_and(rank, 1)
+    def owned(products, after, bits, mines):
+        rows = products[0][0][3] // nc
+        cols = sum(p[0][2][2] for p in products)
         if rows % 128 == 0:
-            flat = [m for p in products for term in p for m in term]
-            terms = [len(p) for p in products]
+            flat, terms, flops = [], [], 0
+            for group in products:
+                terms.append([])
+                for stack, low, (b, first, wide), high in group:
+                    pieces = [(len(flat) + i, count) for i, (_, count) in enumerate(stack)]
+                    flat += [ref for ref, _ in stack] + [b]
+                    terms[-1].append((pieces, low, (len(flat) - 1, first, wide)))
+                    flops += 2 * b.shape[0] * high * wide
             part = jax.ShapeDtypeStruct((nc // 2, rows, cols), BF)
             away, stay = call(
                 lambda *r: weight_kernel(nc, terms, *r),
                 (part, part),
-                mine.reshape(1),
+                mines,
                 *flat,
-                flops=sum(2 * m.shape[0] * m.shape[1] * rows * nc for m in flat[1::2]),
+                flops=flops,
                 scalars=1,
             )
         else:
-            grad = [sum(dot(a_, b_, TN) for a_, b_ in p).astype(BF) for p in products]
+            grad = []
+            for group in products:
+                value = 0.0
+                for stack, low, (b, first, wide), high in group:
+                    lhs = jnp.concatenate([r[:c, low : low + high] for r, c in stack], axis=0)
+                    value = value + dot(lhs, b[:, first : first + wide], TN)
+                grad.append(value.astype(BF))
             view = jnp.concatenate(grad, axis=1).reshape(nc // 2, 2, rows, cols)
-            away = lax.dynamic_index_in_dim(view, 1 - mine, 1, keepdims=False)
-            stay = lax.dynamic_index_in_dim(view, mine, 1, keepdims=False)
+            away = jnp.where(bits[0], view[:, 0], view[:, 1])
+            stay = jnp.where(bits[0], view[:, 1], view[:, 0])
         bit = 1
         while True:
             got = send(away, "ctx", bit)
@@ -493,10 +535,10 @@
             bit *= 2
             if bit == nc:
                 return total.reshape(rows, cols)
-            mine = jnp.bitwise_and(rank // bit, 1)
             view = total.reshape(total.shape[0] // 2, 2, rows, cols)
-            away = lax.dynamic_index_in_dim(view, 1 - mine, 1, keepdims=False).astype(BF)
-            stay = lax.dynamic_index_in_dim(view, mine, 1, keepdims=False)
+            upper = bits[bit.bit_length() - 1]
+            away = jnp.where(upper, view[:, 0], view[:, 1]).astype(BF)
+            stay = jnp.where(upper, view[:, 1], view[:, 0])
 
     def local(
         inputs, w_qkv, w_out, w_up, w_down, head_bias, up_bias, out_biases,
@@ -506,8 +548,19 @@
         half_t, half_d = tokens // 2, width // 2
         cols, hidden = w_qkv.shape[2], w_up.shape[1]
         rank = lax.axis_index("ctx")
+        bits = [jnp.bitwise_and(rank, bit) != 0 for bit in reversed(levels(nc))]
+        piece_at = rank * (half_d // nc)
         far_weight = lax.axis_index("weight") == 1
         far_core = jnp.bitwise_and(lax.axis_index("tensor"), 1) == 1
+        ranks = rank.reshape(1)
+        mines = jnp.bitwise_and(ranks, 1)
+        flags = far_weight.astype(jnp.int32).reshape(1)
+        early = (piece_at, far_weight, far_core, ranks, mines, flags, *bits)
+        (inputs, w_qkv, w_out, w_up, w_down, cotangent), early = lax.optimization_barrier(
+            ((inputs, w_qkv, w_out, w_up, w_down, cotangent), early)
+        )
+        piece_at, far_weight, far_core, ranks, mines, flags = early[:6]
+        bits = early[6:]
 
         def turn_d(a):
             return jnp.where(far_weight, jnp.concatenate([a[:, half_d:], a[:, :half_d]], 1), a)
@@ -515,12 +568,12 @@
         def turn_t(a):
             return jnp.where(far_core, jnp.concatenate([a[half_t:], a[:half_t]], 0), a)
 
-        wq = w_qkv[:, 0]
-        wkv = w_qkv[:, 1:3].reshape(half_d, 2 * cols)
+        wq, wk, wv = w_qkv[:, 0], w_qkv[:, 1], w_qkv[:, 2]
         wqo = jnp.concatenate([wq, w_out], axis=1)
-        wkv_far = send(wkv, "weight")
+        wk_far = send(wk, "weight")
+        wv_far = send(wv, "weight")
         wqo_far = send(wqo, "weight")
-        piece = lax.dynamic_slice_in_dim(w_down, rank * (half_d // nc), half_d // nc, 0)
+        piece = lax.dynamic_slice_in_dim(w_down, piece_at, half_d // nc, 0)
         piece = send(piece, "weight")
         up_far = send(w_up, "weight")
         pieces = gather(piece)
@@ -531,45 +584,42 @@
         out_b, gains, shifts = turn_d(out_biases), turn_d(norm_gains), turn_d(norm_shifts)
         x_lo, x_hi = x[:, :half_d], x[:, half_d:]
 
-        kv_bias = jnp.concatenate([jnp.zeros((cols,), F32), head_bias[1]])
-        kv = (dot(x_lo, wkv, NN) + dot(x_hi, wkv_far, NN) + kv_bias).astype(BF)
-        kvs = gather(kv)
+        k = (dot(x_lo, wk, NN) + dot(x_hi, wk_far, NN)).astype(BF)
+        ks = gather(k)
+        v = (dot(x_lo, wv, NN) + dot(x_hi, wv_far, NN) + head_bias[1]).astype(BF)
+        vs = gather(v)
         q = dot(x_lo, wq, NN) + dot(x_hi, wqo_far[:, :cols], NN) + head_bias[0]
         q = q.astype(BF) * BF(HD**-0.5)
         qs = gather_few(q)
 
-        part = (shape(half_t, width, F32), shape(half_t, width, BF))
-        attended, lse, keep, sent = attend(q, wqo, wqo_far, kvs)
+        part = (arr(half_t, width, F32), arr(half_t, width, BF))
+        attended, lse, keep, sent = attend(q, wqo, wqo_far, ks, vs)
         sent, got = settle(keep, sent)
         mixed_one, normed_one, inverse_one, mixed_own = call(
             norm_one_kernel,
-            (part[0], part[0], shape(half_t, 128, F32), part[1]),
+            (part[0], part[0], arr(half_t, 128, F32), part[1]),
             sent, got, x_own, out_b, gains, shifts,
         )
         mixed_got = send(mixed_own, "tensor")
         big = 2 * tokens * width * hidden
-        pre_act, act = call(
+        pre_act, act, bundle = call(
             up_kernel,
-            (shape(tokens, hidden, F32), shape(tokens, hidden, BF)),
-            mixed_own, mixed_got, w_up, up_far, up_bias.reshape(1, hidden),
+            (arr(tokens, hidden, F32), arr(tokens, hidden, BF), arr(tokens, width + cols, BF)),
+            mixed_own, mixed_got, x, attended, w_up, up_far, up_bias.reshape(1, hidden),
             flops=big,
         )
+        bundle = send(bundle, "weight")
         down_far, keep, sent = call(
             down_kernel,
-            (shape(half_d, hidden, BF),) + part,
-            rank.reshape(1), act, w_down, *pieces,
+            (arr(half_d, hidden, BF),) + part,
+            ranks, act, w_down, *pieces,
             flops=big, scalars=1,
         )
         sent, got = settle(keep, sent)
         act_mate = send(act, "weight")
-        mixed_hi = jnp.concatenate([mixed_own[:, half_d:], mixed_got[:, half_d:]], axis=0)
-        bundle = send(jnp.concatenate([mixed_hi, x_hi, attended], axis=1), "weight")
-        mixed_mate, x_mate = bundle[:, :half_d], bundle[:, half_d:width]
-        attended_mate = bundle[:, width:]
-
         pair, grad_two, sums_two = call(
             norm_two_kernel,
-            (shape(tokens, width, BF), part[0], shape(3, width, F32)),
+            (arr(tokens, width, BF), part[0], arr(3, width, F32)),
             sent, got, mixed_one, cot, out_b, gains, shifts,
         )
         pair_got = send(pair, "tensor")
@@ -577,7 +627,7 @@
         two_mate = send(two_hi, "weight")
         grad_pre, grad_up_b, keep, sent = call(
             back_kernel,
-            (shape(tokens, hidden, BF), shape(1, hidden, F32)) + part,
+            (arr(tokens, hidden, BF), arr(1, hidden, F32)) + part,
             pair, pair_got, w_down, down_far, pre_act, w_up, up_far,
             flops=2 * big,
         )
@@ -585,56 +635,87 @@
         pre_mate = send(grad_pre, "weight")
         one_own, grad_one, sums_one = call(
             norm_back_kernel,
-            (part[1], part[0], shape(3, width, F32)),
-            sent, got, grad_two, normed_one, inverse_one, gains,
+            (part[1], part[0], arr(6, width, F32)),
+            sent, got, grad_two, normed_one, inverse_one, gains, sums_two,
         )
         one_got = send(one_own, "tensor")
-        msg = pack_message(one_own, one_got, wqo, wqo_far, attended, lse)
+        msg, one_hi = pack_message(one_own, one_got, wqo, wqo_far, attended, lse)
         msgs = gather(msg)
-        two_lo = jnp.concatenate([pair[:half_t, :half_d], pair_got[:half_t, :half_d]], axis=0)
-        one = jnp.concatenate([one_own, one_got], axis=0)
-        one_mate = send(one[:, half_d:], "weight")
-        dq, sums_q = query_grads(q, msg, attended, lse, kvs)
+        one_mate = send(one_hi, "weight")
+        dq, sums_q = query_grads(q, msg, attended, lse, ks, vs)
         dq_mate = send(dq, "weight")
-        mixed_lo = jnp.concatenate([mixed_own[:, :half_d], mixed_got[:, :half_d]], axis=0)
-        dkv, sums_v = key_grads(kv, qs, msgs)
+        dkv, sums_v = key_grads(k, v, qs, msgs)
 
         dkv_mate = send(dkv, "weight")
         keep, sent = call(
-            input_kernel, part, dq, dkv, wqo, wqo_far, wkv, wkv_far,
+            input_kernel, part, dq, dkv, wqo, wk, wv, wqo_far, wk_far, wv_far,
             flops=6 * tokens * width * cols,
         )
         late = [sent] * 8
-        grad_w_down = owned([[(two_lo, act), (two_mate, act_mate)]], [msg] + late)
-        grad_w_up = owned([[(mixed_lo, grad_pre), (mixed_mate, pre_mate)]], [dq] + late)
+
+        def term(stack, b, low=0, first=0, wide=None):
+            return ([(r, r.shape[0] if c is None else c) for r, c in stack], low,
+                    (b, first, b.shape[1] if wide is None else wide), half_d)
+
+        grad_w_down = owned(
+            [[term([(pair, half_t), (pair_got, half_t)], act), term([(two_mate, None)], act_mate)]],
+            [dq] + late,
+            bits,
+            mines,
+        )
+        grad_w_up = owned(
+            [[
+                term([(mixed_own, None), (mixed_got, None)], grad_pre),
+                term([(bundle, None)], pre_mate),
+            ]],
+            late,
+            bits,
+            mines,
+        )
         oq_grad = owned(
             [
-                [(one[:, :half_d], attended), (one_mate, attended_mate)],
-                [(x_lo, dq), (x_mate, dq_mate)],
+                [
+                    term([(one_own, None), (one_got, None)], attended),
+                    term([(one_mate, None)], bundle, first=width, wide=cols),
+                ],
+                [term([(x, None)], dq), term([(bundle, None)], dq_mate, low=half_d)],
             ],
             late,
+            bits,
+            mines,
         )
         grad_w_out, grad_wq = oq_grad[:, :cols], oq_grad[:, cols:]
         sent, got = settle(keep, sent)
-        grad_wkv = owned([[(x_lo, dkv), (x_mate, dkv_mate)]], late)
+        grad_wkv = owned(
+            [[term([(x, None)], dkv), term([(bundle, None)], dkv_mate, low=half_d)]],
+            late,
+            bits,
+            mines,
+        )
         grad_own = (grad_one + (sent.astype(F32) + got.astype(F32))).astype(BF)
         grad_got = send(grad_own, "tensor")
         grad_input = turn_d(turn_t(jnp.concatenate([grad_own, grad_got], axis=0)))
         pair, pair_got, _ = lax.optimization_barrier((pair, pair_got, late[0]))
         layer_out = turn_d(turn_t(jnp.concatenate([pair[half_t:], pair_got[half_t:]], axis=0)))
 
-        rows = jnp.concatenate([sums_one, sums_two], axis=0)
-        rows = turn_d(rows + send(rows, "tensor"))
-        vector = [rows.reshape(-1), grad_up_b[0], sums_q[0], sums_v[0]]
-        vector = jnp.concatenate(vector).reshape(-1, 128)
-        vector = vector + send(vector, "weight")
+        if hidden != width or 2 * cols > width:
+            raise ValueError("vector shape")
+        sums_got = send(sums_one, "tensor")
+        vector = call(
+            sums_kernel, arr(8, width, F32),
+            flags, sums_one, sums_got, grad_up_b, sums_q, sums_v, scalars=1,
+        )
+        got = send(vector, "weight")
         bit = 1
         while bit < nc:
-            vector = vector + send(vector, "ctx", bit)
+            vector = vector + got
+            got = send(vector, "ctx", bit)
             bit *= 2
-        vector = vector.reshape(-1)
-        rows = vector[: 6 * width].reshape(2, 3, width)
-        heads_at = 6 * width + hidden
+        head, up_row, bias, gain, shift = call(
+            unpack_kernel,
+            (arr(2, cols, F32), arr(1, hidden, F32)) + (arr(2, width, F32),) * 3,
+            vector, got,
+        )
         return (
             layer_out[None],
             grad_input[None],
@@ -642,11 +723,11 @@
             grad_w_out,
             grad_w_up,
             grad_w_down,
-            vector[heads_at:].reshape(2, cols),
-            vector[6 * width : heads_at],
-            rows[:, 0],
-            rows[:, 1],
-            rows[:, 2],
+            head,
+            up_row[0],
+            bias,
+            gain,
+            shift,
         )
 
     return local

time: 217 us -> 240 us (1.11)
  waiting for transfers between devices: 88.9 us -> 135 us
  local copies, waits for them, and re-layouts: 24.9 us -> 3.57 us
  starting transfers between devices: 53.1 us -> 65.1 us
  other arithmetic: 16.1 us -> 6.41 us
  Pallas kernels: 27.5 us -> 24.5 us
    ppermute x46 -> x50, waiting for transfers between devices: 88.9 us -> 135 us  [send(): return lax.ppermute(a, axis, [(i, i ^ bit) for i in range(sizes[axis])])]
    ppermute x46 -> x50, starting transfers between devices: 53.1 us -> 65.1 us  [send(): return lax.ppermute(a, axis, [(i, i ^ bit) for i in range(sizes[axis])])]
    unnamed x95 -> x36, local copies, waits for them, and re-layouts: 9.41 us -> 1.19 us
    slice x11 -> x1, local copies, waits for them, and re-layouts: 4.45 us -> 0.01 us  [local(): v = (dot(x_lo, wv, NN) + dot(x_hi, wv_far, NN) + head_bias[1]).astype(BF)]
    pallas_call x11 -> x13, Pallas kernels: 15.9 us -> 11.6 us  [call(): pl.pallas_call(kernel, out_shape=outs, in_specs=[pl.BlockSpec(memory_spac...]
    add x8 -> x2, other arithmetic: 3.54 us -> 0.01 us  [local(): vector = vector + got]
    slice x2, local copies, waits for them, and re-layouts: 2.83 us -> 0.07 us  [turn_t(): return jnp.where(far_core, jnp.concatenate([a[half_t:], a[:half_t]], 0), a)]
    select_n x7, other arithmetic: 5.21 us -> 2.47 us  [turn_d(): jnp.where(far_weight, jnp.concatenate([a[:, half_d:], a[:, :half_d]], 1), a)]
  transfers between devices with their start and end apart: 46 -> 50, of which waited for: 20 -> 23; matrix products, arithmetic and copies ran while one was open for 17% -> 4% of each run, Pallas kernels for 13% -> 9%
where the time goes in v1:
time: 240 us; the launch traced here: 239 us
  waiting for transfers between devices  135 us (56%)
  starting transfers between devices  65.1 us (27%)
  Pallas kernels  24.5 us (10%)
  other arithmetic  6.41 us (3%)
  matrix products  3.69 us (2%)
  local copies, waits for them, and re-layouts  3.57 us (1%)
    ppermute x50, waiting for transfers between devices, send(): return lax.ppermute(a, axis, [(i, i ^ bit) for i in range(sizes[axis])])  135 us
    ppermute x50, starting transfers between devices, send(): return lax.ppermute(a, axis, [(i, i ^ bit) for i in range(sizes[axis])])  65.1 us
    pallas_call x13, Pallas kernels, call(): pl.pallas_call(kernel, out_shape=outs, in_specs=[pl.BlockSpec(memory_spac...  11.6 us
  transfers between devices with their start and end apart: 50, of which 23 were waited for; matrix products, arithmetic and copies ran while one was open for 4% of the time, Pallas kernels for 9%

profile of v1, /device:TPU:0, one launch (start us, length us, event | category | flops | bytes accessed | tf_op | source)
XLA Modules:
  0.0 239.2 jit_solution(15313779244244764937)
XLA Ops:
  0.7 1.3 slice_bitcast_fusion.4
  2.0 3.0 %collective-permute-start.5 = (bf16[512,256]{1,0:T(8,128)(2,1)S(1)}, bf16[512,256]{1,0:T(8,128)(2,1)S(1)}, u32[]{:S(2)}, u32[]{:S(2)}) collective-permute-start(bf16[512,256]{1,0:T(8,128)(2,1)S(1)} %get-tuple-element.163.refs_2_), channel_id=1, source_target_pairs={{0,16},{16,0},{1,17},{17,1},{2,18},{18,2},{3,19},{19,3},{4,20},{20... | collective-permute-start | bytes 786440 | tf_op jit(solution)/shard_map/ppermute | solution.py:470
  5.1 2.0 collective-permute-start
  7.7 0.9 copy-done.9
  9.1 0.9 fusion.17
  10.1 2.1 collective-permute-done.5.refs_5_
  13.0 3.1 %collective-permute-start.6 = (bf16[256,256]{1,0:T(8,128)(2,1)}, bf16[256,256]{1,0:T(8,128)(2,1)}, u32[]{:S(2)}, u32[]{:S(2)}) collective-permute-start(bf16[256,256]{1,0:T(8,128)(2,1)} %fusion.4.r_7_.r_8_.r_1_), channel_id=1, source_target_pairs={{0,8},{4,12},{8,0},{12,4},{1,9},{5,13},{9,1},{13,5},{2,10},{6,14},... | collective-permute-start | bytes 393224 | tf_op jit(solution)/shard_map/ppermute | solution.py:470
  16.2 1.6 collective-permute-done.1.refs_4_
  18.0 3.2 %collective-permute-start.2 = (bf16[256,256]{1,0:T(8,128)(2,1)S(1)}, bf16[256,256]{1,0:T(8,128)(2,1)}, u32[]{:S(2)}, u32[]{:S(2)}) collective-permute-start(bf16[256,256]{1,0:T(8,128)(2,1)S(1)} %fusion.3.r_3_.r_4_.r_0_), channel_id=1, source_target_pairs={{0,8},{4,12},{8,0},{12,4},{1,9},{5,13},{9,1},{13,5},{2,10},{6,14},... | collective-permute-start | bytes 393224 | tf_op jit(solution)/shard_map/ppermute | solution.py:470
  21.3 1.6 collective-permute-start.7
  22.9 1.5 collective-permute-start.3
  24.5 1.6 collective-permute-done.2.r_4_.r_5_
  26.1 1.3 collective-permute-start.8
  27.4 1.7 collective-permute-done.r_2_.r_3_.refs_3_
  29.1 2.1 collective-permute-start.4
  31.2 1.2 fusion.5.r_0_.r_2_
  32.4 1.6 collective-permute-start.13
  34.0 1.6 collective-permute-done.4.r_6_.r_7_
  35.6 3.5 %attend.1 = (bf16[256,256]{1,0:T(8,128)(2,1)S(1)}, f32[4,256]{1,0:T(4,128)S(1)}, f32[128,1024]{1,0:T(8,128)S(1)}, bf16[128,1024]{1,0:T(8,128)(2,1)S(1)}) custom-call(bf16[256,256]{1,0:T(8,128)(2,1)S(1)} %fusion.5.r_0_.r_2_, bf16[512,512]{1,0:T(8,128)(2,1)S(1)} %pad_maximum_fusion.r_1_.r_2_.refs_0_, bf16[512,512]{1,0:T(8,128)(2,1)} %collective-permute-done.r_2_.r_3_.refs_3_, ...), custom_call_target="tpu_custom_call" | custom-call | flops 1073741824 | bytes 1310720 | tf_op jit(solution)/shard_map/attend/pallas_call | solution.py:106
  39.2 1.5 collective-permute-done.9
  40.7 1.9 collective-permute-start.10
  42.6 13.6 %collective-permute-done.13.refs_0_ = bf16[128,1024]{1,0:T(8,128)(2,1)S(1)} collective-permute-done((bf16[128,1024]{1,0:T(8,128)(2,1)S(1)}, bf16[128,1024]{1,0:T(8,128)(2,1)S(1)}, u32[]{:S(2)}, u32[]{:S(2)}) %collective-permute-start.13) | collective-permute-done | bytes 262176 | tf_op jit(solution)/shard_map/ppermute | solution.py:470
  56.2 2.8 %collective-permute-start.14 = (bf16[128,1024]{1,0:T(8,128)(2,1)S(1)}, bf16[128,1024]{1,0:T(8,128)(2,1)S(1)}, u32[]{:S(2)}, u32[]{:S(2)}) collective-permute-start(bf16[128,1024]{1,0:T(8,128)(2,1)S(1)} %collective-permute-done.13.refs_0_), channel_id=1, source_target_pairs={{0,8},{4,12},{8,0},{12,4},{1,9},{5,13},{9,1},{13,5},{2,10},{6,14},... | collective-permute-start | bytes 786440 | tf_op jit(solution)/shard_map/ppermute | solution.py:470
  59.5 1.6 collective-permute-start.15
  61.1 9.2 %collective-permute-done.14.refs_1_ = bf16[128,1024]{1,0:T(8,128)(2,1)S(1)} collective-permute-done((bf16[128,1024]{1,0:T(8,128)(2,1)S(1)}, bf16[128,1024]{1,0:T(8,128)(2,1)S(1)}, u32[]{:S(2)}, u32[]{:S(2)}) %collective-permute-start.14) | collective-permute-done | bytes 262176 | tf_op jit(solution)/shard_map/ppermute | solution.py:470
  70.9 2.1 shard_map.195
  73.3 5.1 %collective-permute-done.16.refs_3_ = bf16[128,1024]{1,0:T(8,128)(2,1)S(1)} collective-permute-done((bf16[128,1024]{1,0:T(8,128)(2,1)S(1)}, bf16[128,1024]{1,0:T(8,128)(2,1)S(1)}, u32[]{:S(2)}, u32[]{:S(2)}) %collective-permute-start.16) | collective-permute-done | bytes 262176 | tf_op jit(solution)/shard_map/ppermute | solution.py:470
  79.6 1.1 collective-permute-done.17
  80.8 1.6 collective-permute-start.18
  82.5 6.7 %collective-permute-done.18.got_ref = bf16[128,1024]{1,0:T(8,128)(2,1)S(1)} collective-permute-done((bf16[128,1024]{1,0:T(8,128)(2,1)S(1)}, bf16[128,1024]{1,0:T(8,128)(2,1)S(1)}, u32[]{:S(2)}, u32[]{:S(2)}) %collective-permute-start.18) | collective-permute-done | bytes 262176 | tf_op jit(solution)/shard_map/ppermute | solution.py:470
  89.8 1.9 collective-permute-done.19.got_ref.r_2_
  91.7 2.7 %shard_map.198 = (bf16[256,1024]{1,0:T(8,128)(2,1)S(1)}, f32[1,1024]{1,0:T(1,128)S(1)}, f32[128,1024]{1,0:T(8,128)S(1)}, bf16[128,1024]{1,0:T(8,128)(2,1)S(1)}) custom-call(bf16[256,1024]{1,0:T(8,128)(2,1)S(1)} %get-tuple-element.121.own_ref.r_1_, bf16[256,1024]{1,0:T(8,128)(2,1)S(1)} %collective-permute-done.19.got_ref.r_2_, bf16[512,1024]{1,0:T(8,128)(2,1)S(1)} %copy-done, ...), custom_call_target="tpu_custom_call" | custom-call | flops 1073741824 | bytes 7606272 | tf_op jit(solution)/shard_map/pallas_call | solution.py:285
  94.7 1.5 collective-permute-start.43
  96.7 1.5 collective-permute-start.39
  99.0 1.6 collective-permute-start.21
  100.5 8.9 %collective-permute-done.43.r_5_ = bf16[256,1024]{1,0:T(8,128)(2,1)S(1)} collective-permute-done((bf16[256,1024]{1,0:T(8,128)(2,1)S(1)}, bf16[256,1024]{1,0:T(8,128)(2,1)S(1)}, u32[]{:S(2)}, u32[]{:S(2)}) %collective-permute-start.43) | collective-permute-done | bytes 524320 | tf_op jit(solution)/shard_map/ppermute | solution.py:470
  109.5 30.3 %collective-permute-done.42.r_4_ = bf16[256,512]{1,0:T(8,128)(2,1)S(1)} collective-permute-done((bf16[256,512]{1,0:T(8,128)(2,1)S(1)}, bf16[256,512]{1,0:T(8,128)(2,1)S(1)}, u32[]{:S(2)}, u32[]{:S(2)}) %collective-permute-start.42) | collective-permute-done | bytes 262176 | tf_op jit(solution)/shard_map/ppermute | solution.py:470
  141.4 3.4 %collective-permute-start.23 = (bf16[256,256]{1,0:T(8,128)(2,1)S(1)}, bf16[256,256]{1,0:T(8,128)(2,1)S(1)}, u32[]{:S(2)}, u32[]{:S(2)}) collective-permute-start(bf16[256,256]{1,0:T(8,128)(2,1)S(1)} %fusion.5.r_0_.r_2_), channel_id=1, source_target_pairs={{0,8},{4,12},{8,0},{12,4},{1,9},{5,13},{9,1},{13,5},{2,10},{6,14},... | collective-permute-start | bytes 393224 | tf_op jit(solution)/shard_map/ppermute | solution.py:470
  145.3 9.8 %collective-permute-done.23.r_3_ = bf16[256,256]{1,0:T(8,128)(2,1)S(1)} collective-permute-done((bf16[256,256]{1,0:T(8,128)(2,1)S(1)}, bf16[256,256]{1,0:T(8,128)(2,1)S(1)}, u32[]{:S(2)}, u32[]{:S(2)}) %collective-permute-start.23) | collective-permute-done | bytes 131104 | tf_op jit(solution)/shard_map/ppermute | solution.py:470
  155.1 4.2 %collective-permute-start.24 = (bf16[512,256]{1,0:T(8,128)(2,1)S(1)}, bf16[512,256]{1,0:T(8,128)(2,1)S(1)}, u32[]{:S(2)}, u32[]{:S(2)}) collective-permute-start(bf16[512,256]{1,0:T(8,128)(2,1)S(1)} %pad_maximum_fusion.3), channel_id=1, source_target_pairs={{0,4},{4,0},{8,12},{12,8},{1,5},{5,1},{9,13},{13,9},{2,6},{6,2},{1... | collective-permute-start | bytes 786440 | tf_op jit(solution)/shard_map/ppermute | solution.py:470
  160.1 1.7 pack_message.1
  161.8 1.3 collective-permute-start.25
  163.1 3.7 %query_grads.1 = (bf16[256,256]{1,0:T(8,128)(2,1)S(1)}, f32[1,256]{1,0:T(1,128)S(1)}) custom-call(bf16[256,256]{1,0:T(8,128)(2,1)S(1)} %fusion.5.r_0_.r_2_, bf16[288,256]{1,0:T(8,128)(2,1)S(1)} %get-tuple-element.116.r_1_.r_5_, bf16[256,256]{1,0:T(8,128)(2,1)S(1)} %get-tuple-element.96.at_ref.r_4_.r_2_.r_3_, f32[4,256]{1,0:T(4,128)S(1)} %get-tuple-element.115.r_5_.r_3_, ...), custom_call_target="tpu_custom_call" | custom-call | flops 1610612736 | bytes 1572864 | tf_op jit(solution)/shard_map/query_grads/pallas_call | solution.py:209
  166.8 1.6 collective-permute-start.33
  169.1 3.5 %collective-permute-done.33.r_9_ = bf16[256,256]{1,0:T(8,128)(2,1)S(1)} collective-permute-done((bf16[256,256]{1,0:T(8,128)(2,1)S(1)}, bf16[256,256]{1,0:T(8,128)(2,1)S(1)}, u32[]{:S(2)}, u32[]{:S(2)}) %collective-permute-start.33) | collective-permute-done | bytes 131104 | tf_op jit(solution)/shard_map/ppermute | solution.py:470
  172.6 1.1 collective-permute-start.26
  173.7 6.7 %collective-permute-done.25.r_6_ = bf16[288,256]{1,0:T(8,128)(2,1)S(1)} collective-permute-done((bf16[288,256]{1,0:T(8,128)(2,1)S(1)}, bf16[288,256]{1,0:T(8,128)(2,1)S(1)}, u32[]{:S(2)}, u32[]{:S(2)}) %collective-permute-start.25) | collective-permute-done | bytes 147488 | tf_op jit(solution)/shard_map/ppermute | solution.py:470
  181.8 2.7 %collective-permute-start.45 = (bf16[1,128,1024]{2,1,0:T(8,128)(2,1)S(1)}, bf16[1,128,1024]{2,1,0:T(8,128)(2,1)S(1)}, u32[]{:S(2)}, u32[]{:S(2)}) collective-permute-start(bf16[1,128,1024]{2,1,0:T(8,128)(2,1)S(1)} %fusion.7), channel_id=1, source_target_pairs={{0,8},{4,12},{8,0},{12,4},{1,9},{5,13},{9,1},{13,5},{2,10},{6,14},... | collective-permute-start | bytes 786440 | tf_op jit(solution)/shard_map/ppermute | solution.py:470
  184.5 2.0 collective-permute-start.34
  186.5 4.0 %key_grads.1 = (bf16[256,512]{1,0:T(8,128)(2,1)S(1)}, f32[1,256]{1,0:T(1,128)S(1)}) custom-call(bf16[256,256]{1,0:T(8,128)(2,1)S(1)} %fusion.3.r_3_.r_4_.r_0_, bf16[256,256]{1,0:T(8,128)(2,1)} %fusion.4.r_7_.r_8_.r_1_, bf16[256,256]{1,0:T(8,128)(2,1)S(1)} %fusion.5.r_0_.r_2_, bf16[256,256]{1,0:T(8,128)(2,1)S(1)} %collective-permute-done.23.r_3_, ...), custom_call_target="tpu_custom_call" | custom-call | flops 2147483648 | bytes 1572864 | tf_op jit(solution)/shard_map/key_grads/pallas_call | solution.py:262
  190.6 1.6 collective-permute-start.47
  192.2 1.6 shard_map.200
  194.9 3.8 %collective-permute-done.48 = f32[8,1024]{1,0:T(8,128)S(1)} collective-permute-done((f32[8,1024]{1,0:T(8,128)S(1)}, f32[8,1024]{1,0:T(8,128)S(1)}, u32[]{:S(2)}, u32[]{:S(2)}) %collective-permute-start.48) | collective-permute-done | bytes 32800 | tf_op jit(solution)/shard_map/ppermute | solution.py:470
  198.8 3.5 %collective-permute-start.49 = (f32[8,1024]{1,0:T(8,128)S(1)}, f32[8,1024]{1,0:T(8,128)S(1)}, u32[]{:S(2)}, u32[]{:S(2)}) collective-permute-start(f32[8,1024]{1,0:T(8,128)S(1)} %add.105.a_ref), channel_id=1, source_target_pairs={{0,8},{4,12},{8,0},{12,4},{1,9},{5,13},{9,1},{13,5},{2,10},{6,14},... | collective-permute-start | bytes 98312 | tf_op jit(solution)/shard_map/ppermute | solution.py:470
  202.4 1.8 collective-permute-done.49.b_ref
  204.9 3.4 %collective-permute-start.35 = (bf16[1,128,512]{2,1,0:T(8,128)(2,1)S(1)}, bf16[1,128,512]{2,1,0:T(8,128)(2,1)S(1)}, u32[]{:S(2)}, u32[]{:S(2)}) collective-permute-start(bf16[1,128,512]{2,1,0:T(8,128)(2,1)S(1)} %fusion.19), channel_id=1, source_target_pairs={{0,8},{4,12},{8,0},{12,4},{1,9},{5,13},{9,1},{13,5},{2,10},{6,14},... | collective-permute-start | bytes 393224 | tf_op jit(solution)/shard_map/ppermute | solution.py:470
  208.3 9.3 %collective-permute-done.41 = bf16[1,128,1024]{2,1,0:T(8,128)(2,1)S(1)} collective-permute-done((bf16[1,128,1024]{2,1,0:T(8,128)(2,1)S(1)}, bf16[1,128,1024]{2,1,0:T(8,128)(2,1)S(1)}, u32[]{:S(2)}, u32[]{:S(2)}) %collective-permute-start.41) | collective-permute-done | bytes 262176 | tf_op jit(solution)/shard_map/ppermute | solution.py:470
  218.1 1.2 collective-permute-start.37
  219.4 1.6 collective-permute-start.29
  221.0 1.1 add_bitcast_fusion.2
  222.9 4.5 %collective-permute-done.37 = bf16[2,128,512]{2,1,0:T(8,128)(2,1)S(1)} collective-permute-done((bf16[2,128,512]{2,1,0:T(8,128)(2,1)S(1)}, bf16[2,128,512]{2,1,0:T(8,128)(2,1)S(1)}, u32[]{:S(2)}, u32[]{:S(2)}) %collective-permute-start.37) | collective-permute-done | bytes 262176 | tf_op jit(solution)/shard_map/ppermute | solution.py:470
  227.8 7.8 %collective-permute-done.38 = bf16[1,128,512]{2,1,0:T(8,128)(2,1)S(1)} collective-permute-done((bf16[1,128,512]{2,1,0:T(8,128)(2,1)S(1)}, bf16[1,128,512]{2,1,0:T(8,128)(2,1)S(1)}, u32[]{:S(2)}, u32[]{:S(2)}) %collective-permute-start.38) | collective-permute-done | bytes 131104 | tf_op jit(solution)/shard_map/ppermute | solution.py:470
  237.1 1.1 maximum_select_fusion.7
  238.1 1.1 maximum_select_fusion.4
  (150 shorter events, 17.4 us)
Async XLA Ops:
  0.7 4.4 %copy-start.13 = (bf16[512,256]{1,0:T(8,128)(2,1)S(1)}, bf16[512,256]{1,0:T(8,128)(2,1)}, u32[]{:S(2)}) copy-start(bf16[512,256]{1,0:T(8,128)(2,1)} %param.13) | copy-start | bytes 786436
  0.7 6.5 %copy-start.1 = (bf16[512,1024]{1,0:T(8,128)(2,1)S(1)}, bf16[512,1024]{1,0:T(8,128)(2,1)}, u32[]{:S(2)}) copy-start(bf16[512,1024]{1,0:T(8,128)(2,1)} %un_ref) | copy-start | bytes 3145732
  1.9 3.2 %copy-start.2 = (bf16[512,256]{1,0:T(8,128)(2,1)}, bf16[512,256]{1,0:T(8,128)(2,1)S(1)}, u32[]{:S(2)}) copy-start(bf16[512,256]{1,0:T(8,128)(2,1)S(1)} %get-tuple-element.163.refs_2_) | copy-start | bytes 786436
  2.0 3.2 %copy-start.4 = (bf16[512,256]{1,0:T(8,128)(2,1)}, bf16[512,256]{1,0:T(8,128)(2,1)S(1)}, u32[]{:S(2)}) copy-start(bf16[512,256]{1,0:T(8,128)(2,1)S(1)} %get-tuple-element.164.refs_1_) | copy-start | bytes 786436
  2.0 10.2 %collective-permute-start.5 = (bf16[512,256]{1,0:T(8,128)(2,1)S(1)}, bf16[512,256]{1,0:T(8,128)(2,1)S(1)}, u32[]{:S(2)}, u32[]{:S(2)}) collective-permute-start(bf16[512,256]{1,0:T(8,128)(2,1)S(1)} %get-tuple-element.163.refs_2_), channel_id=1, source_target_pairs={{0,16},{16,0},{1,17},{17,1},{2,18},{18,2},{3,19},{19,3},{4,20},{20... | collective-permute-start | bytes 786440 | tf_op jit(solution)/shard_map/ppermute | solution.py:470
  5.0 12.8 %collective-permute-start.1 = (bf16[512,256]{1,0:T(8,128)(2,1)S(1)}, bf16[512,256]{1,0:T(8,128)(2,1)S(1)}, u32[]{:S(2)}, u32[]{:S(2)}) collective-permute-start(bf16[512,256]{1,0:T(8,128)(2,1)S(1)} %get-tuple-element.164.refs_1_), channel_id=1, source_target_pairs={{0,16},{16,0},{1,17},{17,1},{2,18},{18,2},{3,19},{19,3},{4,20},{20... | collective-permute-start | bytes 786440 | tf_op jit(solution)/shard_map/ppermute | solution.py:470
  5.1 2.2 copy-start.10
  5.1 24.0 %collective-permute-start = (bf16[512,512]{1,0:T(8,128)(2,1)S(1)}, bf16[512,512]{1,0:T(8,128)(2,1)}, u32[]{:S(2)}, u32[]{:S(2)}) collective-permute-start(bf16[512,512]{1,0:T(8,128)(2,1)S(1)} %pad_maximum_fusion.r_1_.r_2_.refs_0_), channel_id=1, source_target_pairs={{0,16},{16,0},{1,17},{17,1},{2,18},{18,2},{3,19},{19,3},{4,20},{20... | collective-permute-start | bytes 1572872 | tf_op jit(solution)/shard_map/ppermute | solution.py:470
  7.2 63.8 %collective-permute-start.12 = (bf16[512,1024]{1,0:T(8,128)(2,1)S(1)}, bf16[512,1024]{1,0:T(8,128)(2,1)}, u32[]{:S(2)}, u32[]{:S(2)}) collective-permute-start(bf16[512,1024]{1,0:T(8,128)(2,1)S(1)} %copy-done.1), channel_id=1, source_target_pairs={{0,16},{16,0},{1,17},{17,1},{2,18},{18,2},{3,19},{19,3},{4,20},{20... | collective-permute-start | bytes 3145736 | tf_op jit(solution)/shard_map/ppermute | solution.py:470
  7.5 1.1 copy-start.9
  10.1 11.1 %copy-start = (bf16[512,1024]{1,0:T(8,128)(2,1)S(1)}, bf16[512,1024]{1,0:T(8,128)(2,1)}, u32[]{:S(2)}) copy-start(bf16[512,1024]{1,0:T(8,128)(2,1)} %dn_ref) | copy-start | bytes 3145732
  13.0 9.9 %collective-permute-start.6 = (bf16[256,256]{1,0:T(8,128)(2,1)}, bf16[256,256]{1,0:T(8,128)(2,1)}, u32[]{:S(2)}, u32[]{:S(2)}) collective-permute-start(bf16[256,256]{1,0:T(8,128)(2,1)} %fusion.4.r_7_.r_8_.r_1_), channel_id=1, source_target_pairs={{0,8},{4,12},{8,0},{12,4},{1,9},{5,13},{9,1},{13,5},{2,10},{6,14},... | collective-permute-start | bytes 393224 | tf_op jit(solution)/shard_map/ppermute | solution.py:470
  18.0 8.1 %collective-permute-start.2 = (bf16[256,256]{1,0:T(8,128)(2,1)S(1)}, bf16[256,256]{1,0:T(8,128)(2,1)}, u32[]{:S(2)}, u32[]{:S(2)}) collective-permute-start(bf16[256,256]{1,0:T(8,128)(2,1)S(1)} %fusion.3.r_3_.r_4_.r_0_), channel_id=1, source_target_pairs={{0,8},{4,12},{8,0},{12,4},{1,9},{5,13},{9,1},{13,5},{2,10},{6,14},... | collective-permute-start | bytes 393224 | tf_op jit(solution)/shard_map/ppermute | solution.py:470
  21.2 10.0 %copy-start.12 = (f32[256,256]{1,0:T(8,128)S(1)}, f32[256,256]{1,0:T(8,128)}, u32[]{:S(2)}) copy-start(f32[256,256]{1,0:T(8,128)} %fusion.17) | copy-start | bytes 786436
  21.3 11.1 %collective-permute-start.7 = (bf16[256,256]{1,0:T(8,128)(2,1)}, bf16[256,256]{1,0:T(8,128)(2,1)S(1)}, u32[]{:S(2)}, u32[]{:S(2)}) collective-permute-start(bf16[256,256]{1,0:T(8,128)(2,1)} %fusion.4.r_7_.r_8_.r_1_), channel_id=1, source_target_pairs={{0,4},{4,0},{8,12},{12,8},{1,5},{5,1},{9,13},{13,9},{2,6},{6,2},{1... | collective-permute-start | bytes 393224 | tf_op jit(solution)/shard_map/ppermute | solution.py:470
  22.9 11.0 %collective-permute-start.3 = (bf16[256,256]{1,0:T(8,128)(2,1)S(1)}, bf16[256,256]{1,0:T(8,128)(2,1)S(1)}, u32[]{:S(2)}, u32[]{:S(2)}) collective-permute-start(bf16[256,256]{1,0:T(8,128)(2,1)S(1)} %fusion.3.r_3_.r_4_.r_0_), channel_id=1, source_target_pairs={{0,4},{4,0},{8,12},{12,8},{1,5},{5,1},{9,13},{13,9},{2,6},{6,2},{1... | collective-permute-start | bytes 393224 | tf_op jit(solution)/shard_map/ppermute | solution.py:470
  26.1 7.9 %collective-permute-start.8 = (bf16[256,256]{1,0:T(8,128)(2,1)}, bf16[256,256]{1,0:T(8,128)(2,1)S(1)}, u32[]{:S(2)}, u32[]{:S(2)}) collective-permute-start(bf16[256,256]{1,0:T(8,128)(2,1)} %collective-permute-done.6.r_8_.r_9_), channel_id=1, source_target_pairs={{0,4},{4,0},{8,12},{12,8},{1,5},{5,1},{9,13},{13,9},{2,6},{6,2},{1... | collective-permute-start | bytes 393224 | tf_op jit(solution)/shard_map/ppermute | solution.py:470
  29.1 6.5 %collective-permute-start.4 = (bf16[256,256]{1,0:T(8,128)(2,1)}, bf16[256,256]{1,0:T(8,128)(2,1)S(1)}, u32[]{:S(2)}, u32[]{:S(2)}) collective-permute-start(bf16[256,256]{1,0:T(8,128)(2,1)} %collective-permute-done.2.r_4_.r_5_), channel_id=1, source_target_pairs={{0,4},{4,0},{8,12},{12,8},{1,5},{5,1},{9,13},{13,9},{2,6},{6,2},{1... | collective-permute-start | bytes 393224 | tf_op jit(solution)/shard_map/ppermute | solution.py:470
  32.4 6.7 %copy-start.15 = (f32[2,1024]{1,0:T(2,128)S(1)}, f32[2,1024]{1,0:T(2,128)}, u32[]{:S(2)}) copy-start(f32[2,1024]{1,0:T(2,128)} %param.20) | copy-start | bytes 24580
  32.4 23.8 %collective-permute-start.13 = (bf16[128,1024]{1,0:T(8,128)(2,1)S(1)}, bf16[128,1024]{1,0:T(8,128)(2,1)S(1)}, u32[]{:S(2)}, u32[]{:S(2)}) collective-permute-start(bf16[128,1024]{1,0:T(8,128)(2,1)S(1)} %constant_dynamic-slice_fusion), channel_id=1, source_target_pairs={{0,16},{16,0},{1,17},{17,1},{2,18},{18,2},{3,19},{19,3},{4,20},{20... | collective-permute-start | bytes 786440 | tf_op jit(solution)/shard_map/ppermute | solution.py:470
  39.1 1.6 collective-permute-start.9
  40.7 1.9 copy-start.16
  40.7 18.3 %collective-permute-start.10 = (bf16[128,1024]{1,0:T(8,128)(2,1)S(1)}, bf16[128,1024]{1,0:T(8,128)(2,1)S(1)}, u32[]{:S(2)}, u32[]{:S(2)}) collective-permute-start(bf16[128,1024]{1,0:T(8,128)(2,1)S(1)} %add_convert_fusion.4.sent_ref), channel_id=1, source_target_pairs={{0,2},{1,3},{2,0},{3,1},{4,6},{5,7},{6,4},{7,5},{8,10},{9,11},{10,... | collective-permute-start | bytes 786440 | tf_op jit(solution)/shard_map/ppermute | solution.py:470
  56.2 14.1 %collective-permute-start.14 = (bf16[128,1024]{1,0:T(8,128)(2,1)S(1)}, bf16[128,1024]{1,0:T(8,128)(2,1)S(1)}, u32[]{:S(2)}, u32[]{:S(2)}) collective-permute-start(bf16[128,1024]{1,0:T(8,128)(2,1)S(1)} %collective-permute-done.13.refs_0_), channel_id=1, source_target_pairs={{0,8},{4,12},{8,0},{12,4},{1,9},{5,13},{9,1},{13,5},{2,10},{6,14},... | collective-permute-start | bytes 786440 | tf_op jit(solution)/shard_map/ppermute | solution.py:470
  59.4 11.5 %copy-start.8 = (f32[1024]{0:T(1024)S(1)}, f32[1024]{0:T(1024)}, u32[]{:S(2)}) copy-start(f32[1024]{0:T(1024)} %param.17) | copy-start | bytes 12292
  59.4 11.5 %collective-permute-start.11 = (bf16[128,1024]{1,0:T(8,128)(2,1)S(1)}, bf16[128,1024]{1,0:T(8,128)(2,1)S(1)}, u32[]{:S(2)}, u32[]{:S(2)}) collective-permute-start(bf16[128,1024]{1,0:T(8,128)(2,1)S(1)} %get-tuple-element.95.own_ref.r_1_), channel_id=1, source_target_pairs={{0,1},{1,0},{2,3},{3,2},{4,5},{5,4},{6,7},{7,6},{8,9},{9,8},{10,11... | collective-permute-start | bytes 786440 | tf_op jit(solution)/shard_map/ppermute | solution.py:470
  59.5 13.8 %collective-permute-start.15 = (bf16[128,1024]{1,0:T(8,128)(2,1)S(1)}, bf16[128,1024]{1,0:T(8,128)(2,1)S(1)}, u32[]{:S(2)}, u32[]{:S(2)}) collective-permute-start(bf16[128,1024]{1,0:T(8,128)(2,1)S(1)} %collective-permute-done.13.refs_0_), channel_id=1, source_target_pairs={{0,4},{4,0},{8,12},{12,8},{1,5},{5,1},{9,13},{13,9},{2,6},{6,2},{1... | collective-permute-start | bytes 786440 | tf_op jit(solution)/shard_map/ppermute | solution.py:470
  70.3 8.0 %collective-permute-start.16 = (bf16[128,1024]{1,0:T(8,128)(2,1)S(1)}, bf16[128,1024]{1,0:T(8,128)(2,1)S(1)}, u32[]{:S(2)}, u32[]{:S(2)}) collective-permute-start(bf16[128,1024]{1,0:T(8,128)(2,1)S(1)} %collective-permute-done.14.refs_1_), channel_id=1, source_target_pairs={{0,4},{4,0},{8,12},{12,8},{1,5},{5,1},{9,13},{13,9},{2,6},{6,2},{1... | collective-permute-start | bytes 786440 | tf_op jit(solution)/shard_map/ppermute | solution.py:470
  79.1 1.6 collective-permute-start.17
  80.8 8.4 %collective-permute-start.18 = (bf16[128,1024]{1,0:T(8,128)(2,1)S(1)}, bf16[128,1024]{1,0:T(8,128)(2,1)S(1)}, u32[]{:S(2)}, u32[]{:S(2)}) collective-permute-start(bf16[128,1024]{1,0:T(8,128)(2,1)S(1)} %add_convert_fusion.3.sent_ref), channel_id=1, source_target_pairs={{0,2},{1,3},{2,0},{3,1},{4,6},{5,7},{6,4},{7,5},{8,10},{9,11},{10,... | collective-permute-start | bytes 786440 | tf_op jit(solution)/shard_map/ppermute | solution.py:470
  89.8 2.0 collective-permute-start.19
  94.5 4.4 %collective-permute-start.20 = (bf16[128,1024]{1,0:T(8,128)(2,1)S(1)}, bf16[128,1024]{1,0:T(8,128)(2,1)S(1)}, u32[]{:S(2)}, u32[]{:S(2)}) collective-permute-start(bf16[128,1024]{1,0:T(8,128)(2,1)S(1)} %get-tuple-element.109), channel_id=1, source_target_pairs={{0,1},{1,0},{2,3},{3,2},{4,5},{5,4},{6,7},{7,6},{8,9},{9,8},{10,11... | collective-permute-start | bytes 786440 | tf_op jit(solution)/shard_map/ppermute | solution.py:470
  94.7 14.8 %collective-permute-start.43 = (bf16[256,1024]{1,0:T(8,128)(2,1)S(1)}, bf16[256,1024]{1,0:T(8,128)(2,1)S(1)}, u32[]{:S(2)}, u32[]{:S(2)}) collective-permute-start(bf16[256,1024]{1,0:T(8,128)(2,1)S(1)} %get-tuple-element.98.act_ref.r_3_), channel_id=1, source_target_pairs={{0,16},{16,0},{1,17},{17,1},{2,18},{18,2},{3,19},{19,3},{4,20},{20... | collective-permute-start | bytes 1572872 | tf_op jit(solution)/shard_map/ppermute | solution.py:470
  96.1 63.1 %collective-permute-start.32 = (bf16[256,1280]{1,0:T(8,128)(2,1)S(1)}, bf16[256,1280]{1,0:T(8,128)(2,1)S(1)}, u32[]{:S(2)}, u32[]{:S(2)}) collective-permute-start(bf16[256,1280]{1,0:T(8,128)(2,1)S(1)} %get-tuple-element.127), channel_id=1, source_target_pairs={{0,16},{16,0},{1,17},{17,1},{2,18},{18,2},{3,19},{19,3},{4,20},{20... | collective-permute-start | bytes 1966088 | tf_op jit(solution)/shard_map/ppermute | solution.py:470
  96.7 62.6 %collective-permute-start.39 = (bf16[256,1024]{1,0:T(8,128)(2,1)S(1)}, bf16[256,1024]{1,0:T(8,128)(2,1)S(1)}, u32[]{:S(2)}, u32[]{:S(2)}) collective-permute-start(bf16[256,1024]{1,0:T(8,128)(2,1)S(1)} %get-tuple-element.140.r_3_), channel_id=1, source_target_pairs={{0,16},{16,0},{1,17},{17,1},{2,18},{18,2},{3,19},{19,3},{4,20},{20... | collective-permute-start | bytes 1572872 | tf_op jit(solution)/shard_map/ppermute | solution.py:470
  98.3 41.5 %collective-permute-start.42 = (bf16[256,512]{1,0:T(8,128)(2,1)S(1)}, bf16[256,512]{1,0:T(8,128)(2,1)S(1)}, u32[]{:S(2)}, u32[]{:S(2)}) collective-permute-start(bf16[256,512]{1,0:T(8,128)(2,1)S(1)} %pad_maximum_fusion.4), channel_id=1, source_target_pairs={{0,16},{16,0},{1,17},{17,1},{2,18},{18,2},{3,19},{19,3},{4,20},{20... | collective-permute-start | bytes 786440 | tf_op jit(solution)/shard_map/ppermute | solution.py:470
  99.0 45.8 %collective-permute-start.21 = (bf16[128,1024]{1,0:T(8,128)(2,1)S(1)}, bf16[128,1024]{1,0:T(8,128)(2,1)S(1)}, u32[]{:S(2)}, u32[]{:S(2)}) collective-permute-start(bf16[128,1024]{1,0:T(8,128)(2,1)S(1)} %add_convert_fusion.2.sent_ref), channel_id=1, source_target_pairs={{0,2},{1,3},{2,0},{3,1},{4,6},{5,7},{6,4},{7,5},{8,10},{9,11},{10,... | collective-permute-start | bytes 786440 | tf_op jit(solution)/shard_map/ppermute | solution.py:470
  140.5 27.8 %collective-permute-start.44 = (bf16[2,128,1024]{2,1,0:T(8,128)(2,1)S(1)}, bf16[2,128,1024]{2,1,0:T(8,128)(2,1)S(1)}, u32[]{:S(2)}, u32[]{:S(2)}) collective-permute-start(bf16[2,128,1024]{2,1,0:T(8,128)(2,1)S(1)} %get-tuple-element.147), channel_id=1, source_target_pairs={{0,4},{4,0},{8,12},{12,8},{1,5},{5,1},{9,13},{13,9},{2,6},{6,2},{1... | collective-permute-start | bytes 1572872 | tf_op jit(solution)/shard_map/ppermute | solution.py:470
  141.4 13.7 %collective-permute-start.23 = (bf16[256,256]{1,0:T(8,128)(2,1)S(1)}, bf16[256,256]{1,0:T(8,128)(2,1)S(1)}, u32[]{:S(2)}, u32[]{:S(2)}) collective-permute-start(bf16[256,256]{1,0:T(8,128)(2,1)S(1)} %fusion.5.r_0_.r_2_), channel_id=1, source_target_pairs={{0,8},{4,12},{8,0},{12,4},{1,9},{5,13},{9,1},{13,5},{2,10},{6,14},... | collective-permute-start | bytes 393224 | tf_op jit(solution)/shard_map/ppermute | solution.py:470
  145.2 14.9 %collective-permute-start.22 = (bf16[128,1024]{1,0:T(8,128)(2,1)S(1)}, bf16[128,1024]{1,0:T(8,128)(2,1)S(1)}, u32[]{:S(2)}, u32[]{:S(2)}) collective-permute-start(bf16[128,1024]{1,0:T(8,128)(2,1)S(1)} %get-tuple-element.114.r_0_.r_1_), channel_id=1, source_target_pairs={{0,1},{1,0},{2,3},{3,2},{4,5},{5,4},{6,7},{7,6},{8,9},{9,8},{10,11... | collective-permute-start | bytes 786440 | tf_op jit(solution)/shard_map/ppermute | solution.py:470
  155.1 26.8 %collective-permute-start.24 = (bf16[512,256]{1,0:T(8,128)(2,1)S(1)}, bf16[512,256]{1,0:T(8,128)(2,1)S(1)}, u32[]{:S(2)}, u32[]{:S(2)}) collective-permute-start(bf16[512,256]{1,0:T(8,128)(2,1)S(1)} %pad_maximum_fusion.3), channel_id=1, source_target_pairs={{0,4},{4,0},{8,12},{12,8},{1,5},{5,1},{9,13},{13,9},{2,6},{6,2},{1... | collective-permute-start | bytes 786440 | tf_op jit(solution)/shard_map/ppermute | solution.py:470
  160.0 33.8 %collective-permute-start.40 = (bf16[2,128,1024]{2,1,0:T(8,128)(2,1)S(1)}, bf16[2,128,1024]{2,1,0:T(8,128)(2,1)S(1)}, u32[]{:S(2)}, u32[]{:S(2)}) collective-permute-start(bf16[2,128,1024]{2,1,0:T(8,128)(2,1)S(1)} %get-tuple-element.141), channel_id=1, source_target_pairs={{0,4},{4,0},{8,12},{12,8},{1,5},{5,1},{9,13},{13,9},{2,6},{6,2},{1... | collective-permute-start | bytes 1572872 | tf_op jit(solution)/shard_map/ppermute | solution.py:470
  161.8 18.5 %collective-permute-start.25 = (bf16[288,256]{1,0:T(8,128)(2,1)S(1)}, bf16[288,256]{1,0:T(8,128)(2,1)S(1)}, u32[]{:S(2)}, u32[]{:S(2)}) collective-permute-start(bf16[288,256]{1,0:T(8,128)(2,1)S(1)} %get-tuple-element.116.r_1_.r_5_), channel_id=1, source_target_pairs={{0,8},{4,12},{8,0},{12,4},{1,9},{5,13},{9,1},{13,5},{2,10},{6,14},... | collective-permute-start | bytes 442376 | tf_op jit(solution)/shard_map/ppermute | solution.py:470
  166.8 5.8 %collective-permute-start.33 = (bf16[256,256]{1,0:T(8,128)(2,1)S(1)}, bf16[256,256]{1,0:T(8,128)(2,1)S(1)}, u32[]{:S(2)}, u32[]{:S(2)}) collective-permute-start(bf16[256,256]{1,0:T(8,128)(2,1)S(1)} %get-tuple-element.117.dq_ref.r_7_), channel_id=1, source_target_pairs={{0,16},{16,0},{1,17},{17,1},{2,18},{18,2},{3,19},{19,3},{4,20},{20... | collective-permute-start | bytes 393224 | tf_op jit(solution)/shard_map/ppermute | solution.py:470
  168.4 12.8 %collective-permute-start.31 = (bf16[256,512]{1,0:T(8,128)(2,1)S(1)}, bf16[256,512]{1,0:T(8,128)(2,1)S(1)}, u32[]{:S(2)}, u32[]{:S(2)}) collective-permute-start(bf16[256,512]{1,0:T(8,128)(2,1)S(1)} %get-tuple-element.126), channel_id=1, source_target_pairs={{0,16},{16,0},{1,17},{17,1},{2,18},{18,2},{3,19},{19,3},{4,20},{20... | collective-permute-start | bytes 786440 | tf_op jit(solution)/shard_map/ppermute | solution.py:470
  172.6 11.9 %collective-permute-start.26 = (bf16[288,256]{1,0:T(8,128)(2,1)S(1)}, bf16[288,256]{1,0:T(8,128)(2,1)S(1)}, u32[]{:S(2)}, u32[]{:S(2)}) collective-permute-start(bf16[288,256]{1,0:T(8,128)(2,1)S(1)} %get-tuple-element.116.r_1_.r_5_), channel_id=1, source_target_pairs={{0,4},{4,0},{8,12},{12,8},{1,5},{5,1},{9,13},{13,9},{2,6},{6,2},{1... | collective-permute-start | bytes 442376 | tf_op jit(solution)/shard_map/ppermute | solution.py:470
  180.4 6.2 %collective-permute-start.27 = (bf16[288,256]{1,0:T(8,128)(2,1)S(1)}, bf16[288,256]{1,0:T(8,128)(2,1)S(1)}, u32[]{:S(2)}, u32[]{:S(2)}) collective-permute-start(bf16[288,256]{1,0:T(8,128)(2,1)S(1)} %collective-permute-done.25.r_6_), channel_id=1, source_target_pairs={{0,4},{4,0},{8,12},{12,8},{1,5},{5,1},{9,13},{13,9},{2,6},{6,2},{1... | collective-permute-start | bytes 442376 | tf_op jit(solution)/shard_map/ppermute | solution.py:470
  181.2 9.4 %collective-permute-start.46 = (f32[6,1024]{1,0:T(8,128)S(1)}, f32[6,1024]{1,0:T(8,128)S(1)}, u32[]{:S(2)}, u32[]{:S(2)}) collective-permute-start(f32[6,1024]{1,0:T(8,128)S(1)} %get-tuple-element.154.own_ref), channel_id=1, source_target_pairs={{0,1},{1,0},{2,3},{3,2},{4,5},{5,4},{6,7},{7,6},{8,9},{9,8},{10,11... | collective-permute-start | bytes 73736 | tf_op jit(solution)/shard_map/ppermute | solution.py:470
  181.8 20.5 %collective-permute-start.45 = (bf16[1,128,1024]{2,1,0:T(8,128)(2,1)S(1)}, bf16[1,128,1024]{2,1,0:T(8,128)(2,1)S(1)}, u32[]{:S(2)}, u32[]{:S(2)}) collective-permute-start(bf16[1,128,1024]{2,1,0:T(8,128)(2,1)S(1)} %fusion.7), channel_id=1, source_target_pairs={{0,8},{4,12},{8,0},{12,4},{1,9},{5,13},{9,1},{13,5},{2,10},{6,14},... | collective-permute-start | bytes 786440 | tf_op jit(solution)/shard_map/ppermute | solution.py:470
  184.5 20.3 %collective-permute-start.34 = (bf16[2,128,512]{2,1,0:T(8,128)(2,1)S(1)}, bf16[2,128,512]{2,1,0:T(8,128)(2,1)S(1)}, u32[]{:S(2)}, u32[]{:S(2)}) collective-permute-start(bf16[2,128,512]{2,1,0:T(8,128)(2,1)S(1)} %get-tuple-element.128), channel_id=1, source_target_pairs={{0,4},{4,0},{8,12},{12,8},{1,5},{5,1},{9,13},{13,9},{2,6},{6,2},{1... | collective-permute-start | bytes 786440 | tf_op jit(solution)/shard_map/ppermute | solution.py:470
  186.5 5.7 %copy-start.3 = (bf16[512,256]{1,0:T(8,128)(2,1)S(1)}, bf16[512,256]{1,0:T(8,128)(2,1)}, u32[]{:S(2)}) copy-start(bf16[512,256]{1,0:T(8,128)(2,1)} %copy-done.2) | copy-start | bytes 786436
  186.5 5.7 %copy-start.5 = (bf16[512,256]{1,0:T(8,128)(2,1)S(1)}, bf16[512,256]{1,0:T(8,128)(2,1)}, u32[]{:S(2)}) copy-start(bf16[512,256]{1,0:T(8,128)(2,1)} %copy-done.4) | copy-start | bytes 786436
  186.5 5.7 %copy-start.7 = (bf16[512,256]{1,0:T(8,128)(2,1)S(1)}, bf16[512,256]{1,0:T(8,128)(2,1)}, u32[]{:S(2)}) copy-start(bf16[512,256]{1,0:T(8,128)(2,1)} %copy-done.6) | copy-start | bytes 786436
  190.6 4.1 %collective-permute-start.47 = (f32[8,1024]{1,0:T(8,128)S(1)}, f32[8,1024]{1,0:T(8,128)S(1)}, u32[]{:S(2)}, u32[]{:S(2)}) collective-permute-start(f32[8,1024]{1,0:T(8,128)S(1)} %shard_map.205), channel_id=1, source_target_pairs={{0,16},{16,0},{1,17},{17,1},{2,18},{18,2},{3,19},{19,3},{4,20},{20... | collective-permute-start | bytes 98312 | tf_op jit(solution)/shard_map/ppermute | solution.py:470
  194.2 23.5 %collective-permute-start.36 = (bf16[256,512]{1,0:T(8,128)(2,1)S(1)}, bf16[256,512]{1,0:T(8,128)(2,1)S(1)}, u32[]{:S(2)}, u32[]{:S(2)}) collective-permute-start(bf16[256,512]{1,0:T(8,128)(2,1)S(1)} %get-tuple-element.118.dkv_ref.r_2_), channel_id=1, source_target_pairs={{0,16},{16,0},{1,17},{17,1},{2,18},{18,2},{3,19},{19,3},{4,20},{20... | collective-permute-start | bytes 786440 | tf_op jit(solution)/shard_map/ppermute | solution.py:470
  194.8 24.6 %collective-permute-start.28 = (bf16[128,1024]{1,0:T(8,128)(2,1)S(1)}, bf16[128,1024]{1,0:T(8,128)(2,1)S(1)}, u32[]{:S(2)}, u32[]{:S(2)}) collective-permute-start(bf16[128,1024]{1,0:T(8,128)(2,1)S(1)} %get-tuple-element.119), channel_id=1, source_target_pairs={{0,1},{1,0},{2,3},{3,2},{4,5},{5,4},{6,7},{7,6},{8,9},{9,8},{10,11... | collective-permute-start | bytes 786440 | tf_op jit(solution)/shard_map/ppermute | solution.py:470
  194.8 4.0 %collective-permute-start.48 = (f32[8,1024]{1,0:T(8,128)S(1)}, f32[8,1024]{1,0:T(8,128)S(1)}, u32[]{:S(2)}, u32[]{:S(2)}) collective-permute-start(f32[8,1024]{1,0:T(8,128)S(1)} %add.104), channel_id=1, source_target_pairs={{0,4},{4,0},{8,12},{12,8},{1,5},{5,1},{9,13},{13,9},{2,6},{6,2},{1... | collective-permute-start | bytes 98312 | tf_op jit(solution)/shard_map/ppermute | solution.py:470
  198.8 5.4 %collective-permute-start.49 = (f32[8,1024]{1,0:T(8,128)S(1)}, f32[8,1024]{1,0:T(8,128)S(1)}, u32[]{:S(2)}, u32[]{:S(2)}) collective-permute-start(f32[8,1024]{1,0:T(8,128)S(1)} %add.105.a_ref), channel_id=1, source_target_pairs={{0,8},{4,12},{8,0},{12,4},{1,9},{5,13},{9,1},{13,5},{2,10},{6,14},... | collective-permute-start | bytes 98312 | tf_op jit(solution)/shard_map/ppermute | solution.py:470
  202.3 15.3 %collective-permute-start.41 = (bf16[1,128,1024]{2,1,0:T(8,128)(2,1)S(1)}, bf16[1,128,1024]{2,1,0:T(8,128)(2,1)S(1)}, u32[]{:S(2)}, u32[]{:S(2)}) collective-permute-start(bf16[1,128,1024]{2,1,0:T(8,128)(2,1)S(1)} %fusion.6), channel_id=1, source_target_pairs={{0,8},{4,12},{8,0},{12,4},{1,9},{5,13},{9,1},{13,5},{2,10},{6,14},... | collective-permute-start | bytes 786440 | tf_op jit(solution)/shard_map/ppermute | solution.py:470
  204.9 17.2 %collective-permute-start.35 = (bf16[1,128,512]{2,1,0:T(8,128)(2,1)S(1)}, bf16[1,128,512]{2,1,0:T(8,128)(2,1)S(1)}, u32[]{:S(2)}, u32[]{:S(2)}) collective-permute-start(bf16[1,128,512]{2,1,0:T(8,128)(2,1)S(1)} %fusion.19), channel_id=1, source_target_pairs={{0,8},{4,12},{8,0},{12,4},{1,9},{5,13},{9,1},{13,5},{2,10},{6,14},... | collective-permute-start | bytes 393224 | tf_op jit(solution)/shard_map/ppermute | solution.py:470
  218.1 9.2 %collective-permute-start.37 = (bf16[2,128,512]{2,1,0:T(8,128)(2,1)S(1)}, bf16[2,128,512]{2,1,0:T(8,128)(2,1)S(1)}, u32[]{:S(2)}, u32[]{:S(2)}) collective-permute-start(bf16[2,128,512]{2,1,0:T(8,128)(2,1)S(1)} %get-tuple-element.134), channel_id=1, source_target_pairs={{0,4},{4,0},{8,12},{12,8},{1,5},{5,1},{9,13},{13,9},{2,6},{6,2},{1... | collective-permute-start | bytes 786440 | tf_op jit(solution)/shard_map/ppermute | solution.py:470
  219.4 8.1 %collective-permute-start.29 = (bf16[128,1024]{1,0:T(8,128)(2,1)S(1)}, bf16[128,1024]{1,0:T(8,128)(2,1)S(1)}, u32[]{:S(2)}, u32[]{:S(2)}) collective-permute-start(bf16[128,1024]{1,0:T(8,128)(2,1)S(1)} %add_convert_fusion.1), channel_id=1, source_target_pairs={{0,2},{1,3},{2,0},{3,1},{4,6},{5,7},{6,4},{7,5},{8,10},{9,11},{10,... | collective-permute-start | bytes 786440 | tf_op jit(solution)/shard_map/ppermute | solution.py:470
  227.5 8.2 %collective-permute-start.38 = (bf16[1,128,512]{2,1,0:T(8,128)(2,1)S(1)}, bf16[1,128,512]{2,1,0:T(8,128)(2,1)S(1)}, u32[]{:S(2)}, u32[]{:S(2)}) collective-permute-start(bf16[1,128,512]{2,1,0:T(8,128)(2,1)S(1)} %fusion.20), channel_id=1, source_target_pairs={{0,8},{4,12},{8,0},{12,4},{1,9},{5,13},{9,1},{13,5},{2,10},{6,14},... | collective-permute-start | bytes 393224 | tf_op jit(solution)/shard_map/ppermute | solution.py:470
  227.7 8.8 %collective-permute-start.30 = (bf16[128,1024]{1,0:T(8,128)(2,1)S(1)}, bf16[128,1024]{1,0:T(8,128)(2,1)S(1)}, u32[]{:S(2)}, u32[]{:S(2)}) collective-permute-start(bf16[128,1024]{1,0:T(8,128)(2,1)S(1)} %add_convert_fusion), channel_id=1, source_target_pairs={{0,1},{1,0},{2,3},{3,2},{4,5},{5,4},{6,7},{7,6},{8,9},{9,8},{10,11... | collective-permute-start | bytes 786440 | tf_op jit(solution)/shard_map/ppermute | solution.py:470
  (4 other events, 3.8 us)

commit v2 on v1

--- a/solution.py
+++ b/solution.py
@@ -129,57 +129,92 @@
     return [high, middle, low]
 
 
+def join_rows(parts, count):
+    wide = parts.astype(F32)
+    return wide[:count] + wide[count : 2 * count] + wide[2 * count : 3 * count]
+
+
+def stack_rows(parts, rows):
+    parts = [p.astype(F32) for p in parts]
+    spare = rows - sum(p.shape[0] for p in parts)
+    if spare:
+        parts.append(jnp.zeros((spare, parts[0].shape[1]), F32))
+    return jnp.concatenate(parts, axis=0).astype(BF)
+
+
+def folded(rows, cols):
+    return jnp.concatenate([rows[:, i : i + cols] for i in range(0, rows.shape[1], cols)], axis=0)
+
+
+def unfolded(rows, count):
+    return jnp.concatenate(
+        [rows[i : i + count] for i in range(0, rows.shape[0], count)], axis=1
+    )
+
+
+def settled_rows(rows):
+    high, middle, low = split_rows(rows)
+    return high.astype(F32) + middle.astype(F32) + low.astype(F32)
+
+
 def message_rows(tokens, heads):
     return tokens + -(-6 * heads // 16) * 16
 
 
-def pack_kernel(heads, own_ref, got_ref, near_ref, far_ref, at_ref, lse_ref, msg_ref, high_ref):
+def pack_kernel(
+    heads, flag_ref, own_ref, got_ref, near_ref, far_ref, at_ref, lse_ref, x_ref, up_ref, *outs
+):
+    msg_ref, bundle_ref, vector_ref = outs
     half = near_ref.shape[0]
-    one = jnp.concatenate([own_ref[...], got_ref[...]], axis=0)
-    high_ref[...] = one[:, half:]
-    cols = at_ref.shape[1]
+    tokens, cols = at_ref.shape
+    part = tokens // 2
+    one = jnp.concatenate([own_ref[:part, :], got_ref[:part, :]], axis=0)
+    bundle_ref[:tokens, :half] = one[:, half:]
+    bundle_ref[:tokens, pl.ds(half, half)] = x_ref[:, pl.ds(half, half)]
+    bundle_ref[:tokens, pl.ds(2 * half, cols)] = at_ref[...]
     out = pl.ds(near_ref.shape[1] - cols, cols)
     da = dot(one[:, :half], near_ref[:, out], NN) + dot(one[:, half:], far_ref[:, out], NN)
     da = da.astype(BF)
-    tokens = da.shape[0]
+    rows = join_rows(own_ref[part:, :], 6) + join_rows(got_ref[part:, :], 6)
+    turned = jnp.concatenate([rows[:, half:], rows[:, :half]], axis=1)
+    vector_ref[0:6, :] = jnp.where(flag_ref[0] == 1, turned, rows)
+    vector_ref[6:7, :] = up_ref[...]
+    vector_ref[7:8, :] = jnp.zeros((1, 2 * half), F32)
+    vector_ref[7:8, pl.ds(cols, cols)] = jnp.sum(da.astype(F32), axis=0, keepdims=True)
+    extra = bundle_ref.shape[0] - tokens
+    bundle_ref[tokens:, : 2 * half] = stack_rows(split_rows(vector_ref[...]), extra)
+    bundle_ref[tokens:, pl.ds(2 * half, cols)] = jnp.zeros((extra, cols), BF)
     prod = da.astype(F32) * at_ref[...].astype(F32)
     deltas = []
     for h in range(heads):
         mask = head_mask(da.shape, h)
         deltas.append(jnp.sum(jnp.where(mask, prod, 0.0), axis=1, keepdims=True))
     rows = split_rows(lse_ref[...]) + split_rows(as_rows(deltas, heads))
-    spare = msg_ref.shape[0] - tokens - 6 * heads
-    if spare:
-        rows.append(jnp.zeros((spare, tokens), BF))
     msg_ref[:tokens, :] = da
-    msg_ref[tokens:, :] = jnp.concatenate([r.astype(F32) for r in rows], axis=0).astype(BF)
-
-
-def pack_message(own, got, near, far, attended, lse):
+    msg_ref[tokens:, :] = stack_rows(rows, msg_ref.shape[0] - tokens)
+
+
+def pack_message(flags, own, got, near, far, attended, lse, x, up_row):
     tokens, cols = attended.shape
-    heads = cols // HD
-    if tokens != cols:
+    width, heads = own.shape[1], cols // HD
+    if tokens != cols or up_row.shape[1] != width or 2 * cols > width:
         raise ValueError("message shape")
-    return pl.pallas_call(
+    return call(
         lambda *r: pack_kernel(heads, *r),
-        out_shape=(
-            jax.ShapeDtypeStruct((message_rows(tokens, heads), cols), BF),
-            jax.ShapeDtypeStruct((tokens, own.shape[1] // 2), BF),
+        (
+            arr(message_rows(tokens, heads), cols, BF),
+            arr(tokens + 32, width + cols, BF),
+            arr(8, width, F32),
         ),
-        cost_estimate=pl.CostEstimate(
-            flops=2 * tokens * own.shape[1] * cols,
-            bytes_accessed=2 * (2 * own.size + near.size + far.size + 2 * attended.size),
-            transcendentals=0,
-        ),
-        name="pack_message",
-        compiler_params=ROOM,
-    )(own, got, near, far, attended, lse)
+        flags, own, got, near, far, attended, lse, x, up_row,
+        flops=2 * tokens * width * cols, scalars=1,
+    )
 
 
 def query_kernel(n, heads, *refs):
     q_ref, da_ref, at_ref, lse_ref = refs[:4]
     k_refs, v_refs = refs[4 : 4 + n], refs[4 + n : 4 + 2 * n]
-    dq_ref, sum_ref = refs[4 + 2 * n :]
+    dq_ref = refs[4 + 2 * n]
     q = q_ref[...]
     tokens = q.shape[0]
     da = da_ref[:tokens, :]
@@ -199,8 +234,9 @@
             acc = acc + dot(ds, k[...], NN)
         out = jnp.where(mask, acc, out)
     out = out * (HD**-0.5)
-    dq_ref[...] = out.astype(BF)
-    sum_ref[...] = jnp.sum(out, axis=0, keepdims=True)
+    dq_ref[:tokens, :] = out.astype(BF)
+    sums = jnp.sum(out, axis=0, keepdims=True)
+    dq_ref[tokens:, :] = stack_rows(split_rows(sums), dq_ref.shape[0] - tokens)
 
 
 def query_grads(q, msg, attended, lse, ks, vs):
@@ -208,10 +244,7 @@
     heads, keys = cols // HD, len(ks) * q.shape[0]
     return pl.pallas_call(
         lambda *r: query_kernel(n, heads, *r),
-        out_shape=(
-            jax.ShapeDtypeStruct((tokens, cols), BF),
-            jax.ShapeDtypeStruct((1, cols), F32),
-        ),
+        out_shape=jax.ShapeDtypeStruct((tokens + 16, cols), BF),
         cost_estimate=pl.CostEstimate(
             flops=6 * tokens * keys * cols * heads,
             bytes_accessed=2 * (2 * keys + 4 * tokens) * cols,
@@ -231,7 +264,7 @@
         for i in range(r.shape[0] // tokens)
     ]
     msgs = refs[2 + m : 2 + m + n]
-    out_ref, sum_ref = refs[2 + m + n :]
+    out_ref = refs[2 + m + n]
     k, v = k_ref[...], v_ref[...]
     stats = []
     for msg in msgs:
@@ -253,7 +286,6 @@
         dk, dv = jnp.where(mask, dk_acc, dk), jnp.where(mask, dv_acc, dv)
     out_ref[:, :cols] = dk.astype(BF)
     out_ref[:, cols:] = dv.astype(BF)
-    sum_ref[...] = jnp.sum(dv, axis=0, keepdims=True)
 
 
 def key_grads(k, v, qs, msgs):
@@ -261,10 +293,7 @@
     heads, rows = cols // HD, n * tokens
     return pl.pallas_call(
         lambda *r: key_kernel(m, n, heads, *r),
-        out_shape=(
-            jax.ShapeDtypeStruct((tokens, 2 * cols), BF),
-            jax.ShapeDtypeStruct((1, cols), F32),
-        ),
+        out_shape=jax.ShapeDtypeStruct((tokens, 2 * cols), BF),
         cost_estimate=pl.CostEstimate(
             flops=8 * tokens * rows * cols * heads,
             bytes_accessed=2 * (2 * rows + 4 * tokens) * cols,
@@ -326,14 +355,11 @@
     own_ref[...] = mixed.astype(BF)
 
 
-def up_kernel(own_ref, got_ref, x_ref, at_ref, near_ref, far_ref, bias_ref, *outs):
-    pre_ref, act_ref, bundle_ref = outs
+def up_kernel(own_ref, got_ref, near_ref, far_ref, bias_ref, pre_ref, act_ref, high_ref):
     half = near_ref.shape[0]
     mixed = jnp.concatenate([own_ref[...], got_ref[...]], axis=0)
     low, high = mixed[:, :half], mixed[:, half:]
-    bundle_ref[:, :half] = high
-    bundle_ref[:, pl.ds(half, half)] = x_ref[:, pl.ds(half, half)]
-    bundle_ref[:, pl.ds(2 * half, at_ref.shape[1])] = at_ref[...]
+    high_ref[...] = high
     for block in column_blocks(near_ref.shape[1]):
         pre = dot(low, near_ref[:, block], NN) + dot(high, far_ref[:, block], NN)
         pre = pre + bias_ref[:, block]
@@ -391,42 +417,23 @@
 def norm_back_kernel(
     sent_ref, got_ref, two_ref, normed_ref, inverse_ref, gain_ref, sums_ref, *outs
 ):
-    own_ref, grad_ref, sum_ref = outs
+    own_ref, grad_ref = outs
     normed = normed_ref[...]
     mixed = two_ref[...] + (sent_ref[...].astype(F32) + got_ref[...].astype(F32))
     grad = layer_back(mixed * gain_ref[0:1, :], normed, inverse_ref[:, 0:1])
-    own_ref[...] = grad.astype(BF)
+    tokens = grad.shape[0]
+    own_ref[:tokens, :] = grad.astype(BF)
     grad_ref[...] = grad
+    sums = []
     for i, value in enumerate((grad, mixed * normed, mixed)):
-        sum_ref[2 * i : 2 * i + 1, :] = jnp.sum(value, axis=0, keepdims=True)
-        sum_ref[2 * i + 1 : 2 * i + 2, :] = sums_ref[i : i + 1, :]
-
-
-def sums_kernel(flag_ref, own_ref, got_ref, up_ref, q_ref, v_ref, out_ref):
-    half, cols = own_ref.shape[1] // 2, q_ref.shape[1]
-    rows = own_ref[...] + got_ref[...]
-    turned = jnp.concatenate([rows[:, half:], rows[:, :half]], axis=1)
-    out_ref[0:6, :] = jnp.where(flag_ref[0] == 1, turned, rows)
-    out_ref[6:7, :] = up_ref[...]
-    out_ref[7:8, :] = jnp.zeros((1, 2 * half), F32)
-    out_ref[7:8, pl.ds(0, cols)] = q_ref[...]
-    out_ref[7:8, pl.ds(cols, cols)] = v_ref[...]
-
-
-def unpack_kernel(a_ref, b_ref, head_ref, up_ref, bias_ref, gain_ref, shift_ref):
-    total = a_ref[...] + b_ref[...]
-    cols = head_ref.shape[1]
-    bias_ref[...] = total[0:2]
-    gain_ref[...] = total[2:4]
-    shift_ref[...] = total[4:6]
-    up_ref[...] = total[6:7]
-    head_ref[0:1, :] = total[7:8, :cols]
-    head_ref[1:2, :] = total[7:8, cols : 2 * cols]
+        sums += [jnp.sum(value, axis=0, keepdims=True), sums_ref[i : i + 1, :]]
+    rows = own_ref.shape[0] - tokens
+    own_ref[tokens:, :] = stack_rows(split_rows(jnp.concatenate(sums, axis=0)), rows)
 
 
 def input_kernel(dq_ref, dkv_ref, *refs):
     near, far, (keep_ref, sent_ref) = refs[:3], refs[3:6], refs[6:]
-    dq = dq_ref[...]
+    dq = dq_ref[: dkv_ref.shape[0], :]
     cols, half = dq.shape[1], near[0].shape[0]
     dk, dv = dkv_ref[:, :cols], dkv_ref[:, cols:]
     for start, (q_ref, k_ref, v_ref) in ((0, near), (half, far)):
@@ -436,9 +443,10 @@
             put_partial(pl.ds(start + rows.start, rows.size), value, keep_ref, sent_ref)
 
 
-def weight_kernel(n, terms, mine_ref, *refs):
-    ins, (away_ref, stay_ref) = refs[:-2], refs[-2:]
-    rows = away_ref.shape[1]
+def weight_kernel(n, terms, rows, ride, mine_ref, *refs):
+    count = 3 if ride else 2
+    ins, outs = refs[:-count], refs[-count:]
+    away_ref, stay_ref = outs[:2]
     mine = mine_ref[0]
     for i in range(n // 2):
         for out, side in ((away_ref, 1 - mine), (stay_ref, mine)):
@@ -448,13 +456,74 @@
                 value = None
                 for pieces, low, b in group:
                     block = pl.ds(pl.multiple_of(at + low, 128), rows)
-                    a = [ins[k][pl.ds(0, count), block] for k, count in pieces]
+                    a = [ins[k][pl.ds(0, tall), block] for k, tall in pieces]
                     a = a[0] if len(a) == 1 else jnp.concatenate(a, axis=0)
                     where, first, cols = b
-                    term = dot(a, ins[where][:, pl.ds(first, cols)], TN)
+                    b = ins[where][pl.ds(0, a.shape[0]), pl.ds(first, cols)]
+                    term = dot(a, b, TN)
                     value = term if value is None else value + term
-                out[i, :, pl.ds(col, value.shape[1])] = value.astype(BF)
+                out[pl.ds(i * rows, rows), pl.ds(col, value.shape[1])] = value.astype(BF)
                 col += value.shape[1]
+    if ride:
+        tokens, vector, bundle, dq, dq_mate = ride
+        width = ins[vector].shape[1]
+        rows_x = settled_rows(ins[vector][...])
+        outs[2][...] = rows_x + join_rows(ins[bundle][tokens:, :width], 8)
+        sums = join_rows(ins[dq][tokens:, :], 1) + join_rows(ins[dq_mate][tokens:, :], 1)
+        outs[2][7:8, pl.ds(0, sums.shape[1])] = sums
+        put_vector(outs[2][...], away_ref, n // 2 * rows)
+
+
+def put_vector(vector, away_ref, first):
+    cols = away_ref.shape[1]
+    parts = [folded(p.astype(F32), cols).astype(BF) for p in split_rows(vector)]
+    away_ref[first:, :] = stack_rows(parts, away_ref.shape[0] - first)
+
+
+def take_vector(got_ref, first, width):
+    cols = got_ref.shape[1]
+    return unfolded(join_rows(got_ref[first:, :], 8 * width // cols), 8)
+
+
+def middle_kernel(blocks, rows, mine_ref, stay_ref, got_ref, *refs):
+    mine = mine_ref[0]
+    ride = len(refs) == 4
+    away_ref, kept_ref = refs[1:3] if ride else refs
+    for i in range(blocks // 2):
+        for out, side in ((away_ref, 1 - mine), (kept_ref, mine)):
+            at = pl.ds(pl.multiple_of((2 * i + side) * rows, rows), rows)
+            value = stay_ref[at, :].astype(F32) + got_ref[at, :].astype(F32)
+            out[pl.ds(i * rows, rows), :] = value.astype(out.dtype)
+    if ride:
+        vector_ref, total_ref = refs[0], refs[3]
+        came = take_vector(got_ref, blocks * rows, vector_ref.shape[1])
+        total_ref[...] = settled_rows(vector_ref[...]) + came
+        put_vector(total_ref[...], away_ref, blocks // 2 * rows)
+
+
+def finish_kernel(*refs):
+    vector_ref, refs = refs[0], refs[1:]
+    down_ref, up_ref, out_ref, qkv_ref = refs[8:12]
+    head_ref, bias_up_ref, bias_ref, gain_ref, shift_ref = refs[12:]
+    rows, cols = out_ref.shape
+    down, up, oq, kv = (
+        refs[2 * i][...].astype(F32) + refs[2 * i + 1][:rows, :].astype(F32) for i in range(4)
+    )
+    down_ref[...] = down
+    up_ref[...] = up
+    out_ref[...] = oq[:, :cols]
+    qkv_ref[0] = oq[:, cols:]
+    qkv_ref[1] = kv[:, :cols]
+    qkv_ref[2] = kv[:, cols:]
+    total = vector_ref[...]
+    if refs[5].shape[0] > rows:
+        total = settled_rows(total) + take_vector(refs[5], rows, total.shape[1])
+    bias_ref[...] = total[0:2]
+    gain_ref[...] = total[2:4]
+    shift_ref[...] = total[4:6]
+    bias_up_ref[...] = total[6:7]
+    head_ref[0:1, :] = total[7:8, :cols]
+    head_ref[1:2, :] = total[7:8, cols : 2 * cols]
 
 
 def levels(n):
@@ -494,9 +563,10 @@
             bit //= 2
         return held
 
-    def owned(products, after, bits, mines):
+    def owned(products, after, mines, ride=None):
         rows = products[0][0][3] // nc
         cols = sum(p[0][2][2] for p in products)
+        blocks, extra, vector = nc // 2, 0, None
         if rows % 128 == 0:
             flat, terms, flops = [], [], 0
             for group in products:
@@ -506,39 +576,52 @@
                     flat += [ref for ref, _ in stack] + [b]
                     terms[-1].append((pieces, low, (len(flat) - 1, first, wide)))
                     flops += 2 * b.shape[0] * high * wide
-            part = jax.ShapeDtypeStruct((nc // 2, rows, cols), BF)
-            away, stay = call(
-                lambda *r: weight_kernel(nc, terms, *r),
-                (part, part),
-                mines,
+            spec, outs = None, ()
+            if ride:
+                tokens, *carried = ride
+                spec = (tokens, *range(len(flat), len(flat) + 4))
+                flat += carried
+                extra = 24 * carried[0].shape[1] // cols
+                outs = (arr(*carried[0].shape, F32),)
+            away, stay, *rest = call(
+                lambda *r: weight_kernel(nc, terms, rows, spec, *r),
+                (arr(blocks * rows + extra, cols, BF), arr(blocks * rows, cols, BF)) + outs,
+                mines[0],
                 *flat,
                 flops=flops,
                 scalars=1,
             )
+            vector = rest[0] if ride else None
         else:
             grad = []
             for group in products:
                 value = 0.0
                 for stack, low, (b, first, wide), high in group:
                     lhs = jnp.concatenate([r[:c, low : low + high] for r, c in stack], axis=0)
-                    value = value + dot(lhs, b[:, first : first + wide], TN)
+                    value = value + dot(lhs, b[: lhs.shape[0], first : first + wide], TN)
                 grad.append(value.astype(BF))
-            view = jnp.concatenate(grad, axis=1).reshape(nc // 2, 2, rows, cols)
-            away = jnp.where(bits[0], view[:, 0], view[:, 1])
-            stay = jnp.where(bits[0], view[:, 1], view[:, 0])
-        bit = 1
+            view = jnp.concatenate(grad, axis=1).reshape(blocks, 2, rows, cols)
+            upper = mines[0][0] == 1
+            away = jnp.where(upper, view[:, 0], view[:, 1]).reshape(blocks * rows, cols)
+            stay = jnp.where(upper, view[:, 1], view[:, 0]).reshape(blocks * rows, cols)
+        bit, level = 1, 1
         while True:
             got = send(away, "ctx", bit)
             got, stay, _ = lax.optimization_barrier((got, stay, after[0]))
             after = after[1:]
-            total = stay.astype(F32) + got.astype(F32)
             bit *= 2
             if bit == nc:
-                return total.reshape(rows, cols)
-            view = total.reshape(total.shape[0] // 2, 2, rows, cols)
-            upper = bits[bit.bit_length() - 1]
-            away = jnp.where(upper, view[:, 0], view[:, 1]).astype(BF)
-            stay = jnp.where(upper, view[:, 1], view[:, 0])
+                return stay, got, vector
+            carried = (vector,) if extra else ()
+            away, stay, *rest = call(
+                lambda *r, blocks=blocks: middle_kernel(blocks, rows, *r),
+                (arr(blocks // 2 * rows + extra, cols, BF), arr(blocks // 2 * rows, cols, F32))
+                + tuple(arr(*v.shape, F32) for v in carried),
+                mines[level], stay, got, *carried,
+                scalars=1,
+            )
+            vector = rest[0] if extra else vector
+            blocks, level = blocks // 2, level + 1
 
     def local(
         inputs, w_qkv, w_out, w_up, w_down, head_bias, up_bias, out_biases,
@@ -548,19 +631,17 @@
         half_t, half_d = tokens // 2, width // 2
         cols, hidden = w_qkv.shape[2], w_up.shape[1]
         rank = lax.axis_index("ctx")
-        bits = [jnp.bitwise_and(rank, bit) != 0 for bit in reversed(levels(nc))]
         piece_at = rank * (half_d // nc)
         far_weight = lax.axis_index("weight") == 1
         far_core = jnp.bitwise_and(lax.axis_index("tensor"), 1) == 1
         ranks = rank.reshape(1)
-        mines = jnp.bitwise_and(ranks, 1)
+        mines = [jnp.bitwise_and(ranks // bit, 1) for bit in reversed(levels(nc))]
         flags = far_weight.astype(jnp.int32).reshape(1)
-        early = (piece_at, far_weight, far_core, ranks, mines, flags, *bits)
+        early = (piece_at, far_weight, far_core, ranks, flags, mines)
         (inputs, w_qkv, w_out, w_up, w_down, cotangent), early = lax.optimization_barrier(
             ((inputs, w_qkv, w_out, w_up, w_down, cotangent), early)
         )
-        piece_at, far_weight, far_core, ranks, mines, flags = early[:6]
-        bits = early[6:]
+        piece_at, far_weight, far_core, ranks, flags, mines = early
 
         def turn_d(a):
             return jnp.where(far_weight, jnp.concatenate([a[:, half_d:], a[:, :half_d]], 1), a)
@@ -568,11 +649,8 @@
         def turn_t(a):
             return jnp.where(far_core, jnp.concatenate([a[half_t:], a[:half_t]], 0), a)
 
-        wq, wk, wv = w_qkv[:, 0], w_qkv[:, 1], w_qkv[:, 2]
-        wqo = jnp.concatenate([wq, w_out], axis=1)
+        wk = w_qkv[:, 1]
         wk_far = send(wk, "weight")
-        wv_far = send(wv, "weight")
-        wqo_far = send(wqo, "weight")
         piece = lax.dynamic_slice_in_dim(w_down, piece_at, half_d // nc, 0)
         piece = send(piece, "weight")
         up_far = send(w_up, "weight")
@@ -580,6 +658,11 @@
 
         x = turn_t(turn_d(inputs[0]))
         x_own = x[:half_t]
+        w_qkv, x = lax.optimization_barrier((w_qkv, x))
+        wq, wv = w_qkv[:, 0], w_qkv[:, 2]
+        wv_far = send(wv, "weight")
+        wqo = jnp.concatenate([wq, w_out], axis=1)
+        wqo_far = send(wqo, "weight")
         cot = turn_t(turn_d(cotangent[0]))[:half_t]
         out_b, gains, shifts = turn_d(out_biases), turn_d(norm_gains), turn_d(norm_shifts)
         x_lo, x_hi = x[:, :half_d], x[:, half_d:]
@@ -602,13 +685,13 @@
         )
         mixed_got = send(mixed_own, "tensor")
         big = 2 * tokens * width * hidden
-        pre_act, act, bundle = call(
+        pre_act, act, mixed_hi = call(
             up_kernel,
-            (arr(tokens, hidden, F32), arr(tokens, hidden, BF), arr(tokens, width + cols, BF)),
-            mixed_own, mixed_got, x, attended, w_up, up_far, up_bias.reshape(1, hidden),
+            (arr(tokens, hidden, F32), arr(tokens, hidden, BF), arr(tokens, half_d, BF)),
+            mixed_own, mixed_got, w_up, up_far, up_bias.reshape(1, hidden),
             flops=big,
         )
-        bundle = send(bundle, "weight")
+        mixed_mate = send(mixed_hi, "weight")
         down_far, keep, sent = call(
             down_kernel,
             (arr(half_d, hidden, BF),) + part,
@@ -633,18 +716,20 @@
         )
         sent, got = settle(keep, sent)
         pre_mate = send(grad_pre, "weight")
-        one_own, grad_one, sums_one = call(
+        one_own, grad_one = call(
             norm_back_kernel,
-            (part[1], part[0], arr(6, width, F32)),
+            (arr(half_t + 32, width, BF), part[0]),
             sent, got, grad_two, normed_one, inverse_one, gains, sums_two,
         )
         one_got = send(one_own, "tensor")
-        msg, one_hi = pack_message(one_own, one_got, wqo, wqo_far, attended, lse)
+        msg, bundle_own, vector = pack_message(
+            flags, one_own, one_got, wqo, wqo_far, attended, lse, x, grad_up_b
+        )
         msgs = gather(msg)
-        one_mate = send(one_hi, "weight")
-        dq, sums_q = query_grads(q, msg, attended, lse, ks, vs)
+        bundle = send(bundle_own, "weight")
+        dq = query_grads(q, msg, attended, lse, ks, vs)
         dq_mate = send(dq, "weight")
-        dkv, sums_v = key_grads(k, v, qs, msgs)
+        dkv = key_grads(k, v, qs, msgs)
 
         dkv_mate = send(dkv, "weight")
         keep, sent = call(
@@ -660,37 +745,31 @@
         grad_w_down = owned(
             [[term([(pair, half_t), (pair_got, half_t)], act), term([(two_mate, None)], act_mate)]],
             [dq] + late,
-            bits,
             mines,
         )
         grad_w_up = owned(
             [[
                 term([(mixed_own, None), (mixed_got, None)], grad_pre),
-                term([(bundle, None)], pre_mate),
+                term([(mixed_mate, None)], pre_mate),
             ]],
             late,
-            bits,
             mines,
         )
         oq_grad = owned(
             [
                 [
-                    term([(one_own, None), (one_got, None)], attended),
-                    term([(one_mate, None)], bundle, first=width, wide=cols),
+                    term([(one_own, half_t), (one_got, half_t)], attended),
+                    term([(bundle, tokens)], bundle, first=width, wide=cols),
                 ],
-                [term([(x, None)], dq), term([(bundle, None)], dq_mate, low=half_d)],
+                [term([(x, None)], dq), term([(bundle, tokens)], dq_mate, low=half_d)],
             ],
             late,
-            bits,
             mines,
-        )
-        grad_w_out, grad_wq = oq_grad[:, :cols], oq_grad[:, cols:]
+            (tokens, vector, bundle, dq, dq_mate),
+        )
         sent, got = settle(keep, sent)
         grad_wkv = owned(
-            [[term([(x, None)], dkv), term([(bundle, None)], dkv_mate, low=half_d)]],
-            late,
-            bits,
-            mines,
+            [[term([(x, None)], dkv), term([(bundle, tokens)], dkv_mate, low=half_d)]], late, mines
         )
         grad_own = (grad_one + (sent.astype(F32) + got.astype(F32))).astype(BF)
         grad_got = send(grad_own, "tensor")
@@ -698,31 +777,35 @@
         pair, pair_got, _ = lax.optimization_barrier((pair, pair_got, late[0]))
         layer_out = turn_d(turn_t(jnp.concatenate([pair[half_t:], pair_got[half_t:]], axis=0)))
 
-        if hidden != width or 2 * cols > width:
-            raise ValueError("vector shape")
-        sums_got = send(sums_one, "tensor")
-        vector = call(
-            sums_kernel, arr(8, width, F32),
-            flags, sums_one, sums_got, grad_up_b, sums_q, sums_v, scalars=1,
-        )
-        got = send(vector, "weight")
-        bit = 1
-        while bit < nc:
-            vector = vector + got
-            got = send(vector, "ctx", bit)
-            bit *= 2
-        head, up_row, bias, gain, shift = call(
-            unpack_kernel,
-            (arr(2, cols, F32), arr(1, hidden, F32)) + (arr(2, width, F32),) * 3,
-            vector, got,
+        if half_d // nc % 128:
+            rows = join_rows(bundle[tokens:, :width], 8) + vector
+            sums = join_rows(dq[tokens:], 1) + join_rows(dq_mate[tokens:], 1)
+            vector = jnp.concatenate(
+                [rows[:7], jnp.concatenate([sums, rows[7:, cols:]], axis=1)], axis=0
+            )
+            bit = 1
+            while bit < nc:
+                vector = vector + send(vector, "ctx", bit)
+                bit *= 2
+        else:
+            vector = oq_grad[2]
+        terms = [a_ for triple in (grad_w_down, grad_w_up, oq_grad, grad_wkv) for a_ in triple[:2]]
+        terms, layer_out, grad_input = lax.optimization_barrier((terms, layer_out, grad_input))
+        block = half_d // nc
+        down_grad, up_grad, out_grad, qkv_grad, head, up_row, bias, gain, shift = call(
+            finish_kernel,
+            (arr(block, hidden, F32), arr(block, hidden, F32), arr(block, cols, F32),
+             jax.ShapeDtypeStruct((3, block, cols), F32), arr(2, cols, F32), arr(1, hidden, F32))
+            + (arr(2, width, F32),) * 3,
+            vector, *terms,
         )
         return (
             layer_out[None],
             grad_input[None],
-            jnp.stack([grad_wq, grad_wkv[:, :cols], grad_wkv[:, cols:]], axis=1),
-            grad_w_out,
-            grad_w_up,
-            grad_w_down,
+            jnp.transpose(qkv_grad, (1, 0, 2)),
+            out_grad,
+            up_grad,
+            down_grad,
             head,
             up_row[0],
             bias,

time: 240 us -> 207 us (0.86)
  waiting for transfers between devices: 135 us -> 112 us
  starting transfers between devices: 65.1 us -> 56.1 us
  other arithmetic: 6.41 us -> 3.22 us
    ppermute x50 -> x46, waiting for transfers between devices: 135 us -> 112 us  [send(): return lax.ppermute(a, axis, [(i, i ^ bit) for i in range(sizes[axis])])]
    ppermute x50 -> x46, starting transfers between devices: 65.1 us -> 56.1 us  [send(): return lax.ppermute(a, axis, [(i, i ^ bit) for i in range(sizes[axis])])]
    pallas_call x13 -> x17, Pallas kernels: 11.6 us -> 14.4 us  [call(): pl.pallas_call(kernel, out_shape=outs, in_specs=[pl.BlockSpec(memory_spac...]
    pallas_call x3 -> x2, Pallas kernels: 9.43 us -> 7.78 us  [the longest x1 3.98 us: key_grads(): pl.pallas_call(lambda *r: key_kernel(m, n, heads, *r), out_shape=jax.Shap...]
  transfers between devices with their start and end apart: 50 -> 46, of which waited for: 23 -> 28; matrix products, arithmetic and copies ran while one was open for 4% -> 4% of each run, Pallas kernels for 9% -> 10%
where the time goes in v2:
time: 207 us; the launch traced here: 206 us
  waiting for transfers between devices  112 us (54%)
  starting transfers between devices  56.1 us (27%)
  Pallas kernels  25.6 us (12%)
  local copies, waits for them, and re-layouts  4.87 us (2%)
  matrix products  3.68 us (2%)
  other arithmetic  3.22 us (2%)
    ppermute x46, waiting for transfers between devices, send(): return lax.ppermute(a, axis, [(i, i ^ bit) for i in range(sizes[axis])])  112 us
    ppermute x46, starting transfers between devices, send(): return lax.ppermute(a, axis, [(i, i ^ bit) for i in range(sizes[axis])])  56.1 us
    pallas_call x17, Pallas kernels, call(): pl.pallas_call(kernel, out_shape=outs, in_specs=[pl.BlockSpec(memory_spac...  14.4 us
  transfers between devices with their start and end apart: 46, of which 28 were waited for; matrix products, arithmetic and copies ran while one was open for 4% of the time, Pallas kernels for 10%

profile of v2, /device:TPU:0, one launch (start us, length us, event | category | flops | bytes accessed | tf_op | source)
XLA Modules:
  0.0 206.3 jit_solution(8121277466760847004)
XLA Ops:
  0.7 1.1 fusion.22
  3.3 3.0 %collective-permute-start.5 = (bf16[512,256]{1,0:T(8,128)(2,1)S(1)}, bf16[512,256]{1,0:T(8,128)(2,1)S(1)}, u32[]{:S(2)}, u32[]{:S(2)}) collective-permute-start(bf16[512,256]{1,0:T(8,128)(2,1)S(1)} %get-tuple-element.207.refs_2_), channel_id=1, source_target_pairs={{0,16},{16,0},{1,17},{17,1},{2,18},{18,2},{3,19},{19,3},{4,20},{20... | collective-permute-start | bytes 786440 | tf_op jit(solution)/shard_map/ppermute | solution.py:539
  7.0 1.5 collective-permute-start
  9.6 0.9 fusion.15
  11.1 2.4 %collective-permute-done.5.refs_5_ = bf16[512,256]{1,0:T(8,128)(2,1)S(1)} collective-permute-done((bf16[512,256]{1,0:T(8,128)(2,1)S(1)}, bf16[512,256]{1,0:T(8,128)(2,1)S(1)}, u32[]{:S(2)}, u32[]{:S(2)}) %collective-permute-start.5) | collective-permute-done | bytes 262176 | tf_op jit(solution)/shard_map/ppermute | solution.py:539
  14.4 3.1 %collective-permute-start.6 = (bf16[256,256]{1,0:T(8,128)(2,1)}, bf16[256,256]{1,0:T(8,128)(2,1)}, u32[]{:S(2)}, u32[]{:S(2)}) collective-permute-start(bf16[256,256]{1,0:T(8,128)(2,1)} %fusion.4.r_7_.r_8_.r_1_), channel_id=1, source_target_pairs={{0,8},{4,12},{8,0},{12,4},{1,9},{5,13},{9,1},{13,5},{2,10},{6,14},... | collective-permute-start | bytes 393224 | tf_op jit(solution)/shard_map/ppermute | solution.py:539
  17.5 1.6 collective-permute-done.1.refs_4_
  19.3 3.2 %collective-permute-start.2 = (bf16[256,256]{1,0:T(8,128)(2,1)S(1)}, bf16[256,256]{1,0:T(8,128)(2,1)}, u32[]{:S(2)}, u32[]{:S(2)}) collective-permute-start(bf16[256,256]{1,0:T(8,128)(2,1)S(1)} %fusion.3.r_3_.r_4_.r_0_), channel_id=1, source_target_pairs={{0,8},{4,12},{8,0},{12,4},{1,9},{5,13},{9,1},{13,5},{2,10},{6,14},... | collective-permute-start | bytes 393224 | tf_op jit(solution)/shard_map/ppermute | solution.py:539
  22.6 1.6 collective-permute-start.7
  24.2 1.5 collective-permute-start.3
  25.7 1.7 collective-permute-done.2.r_4_.r_5_
  27.4 1.3 collective-permute-start.8
  28.7 1.7 collective-permute-done.r_2_.r_4_.refs_3_
  30.4 2.1 %collective-permute-start.4 = (bf16[256,256]{1,0:T(8,128)(2,1)}, bf16[256,256]{1,0:T(8,128)(2,1)S(1)}, u32[]{:S(2)}, u32[]{:S(2)}) collective-permute-start(bf16[256,256]{1,0:T(8,128)(2,1)} %collective-permute-done.2.r_4_.r_5_), channel_id=1, source_target_pairs={{0,4},{4,0},{8,12},{12,8},{1,5},{5,1},{9,13},{13,9},{2,6},{6,2},{1... | collective-permute-start | bytes 393224 | tf_op jit(solution)/shard_map/ppermute | solution.py:539
  33.2 1.2 fusion.5.r_0_.r_2_
  34.4 1.6 collective-permute-start.13
  36.9 3.4 %attend.1 = (bf16[256,256]{1,0:T(8,128)(2,1)S(1)}, f32[4,256]{1,0:T(4,128)S(1)}, f32[128,1024]{1,0:T(8,128)S(1)}, bf16[128,1024]{1,0:T(8,128)(2,1)S(1)}) custom-call(bf16[256,256]{1,0:T(8,128)(2,1)S(1)} %fusion.5.r_0_.r_2_, bf16[512,512]{1,0:T(8,128)(2,1)S(1)} %pad_maximum_fusion.r_1_.r_3_.refs_0_, bf16[512,512]{1,0:T(8,128)(2,1)} %collective-permute-done.r_2_.r_4_.refs_3_, ...), custom_call_target="tpu_custom_call" | custom-call | flops 1073741824 | bytes 1310720 | tf_op jit(solution)/shard_map/attend/pallas_call | solution.py:106
  40.4 1.5 collective-permute-done.9
  41.9 1.9 collective-permute-start.10
  43.8 13.7 %collective-permute-done.13.refs_0_ = bf16[128,1024]{1,0:T(8,128)(2,1)S(1)} collective-permute-done((bf16[128,1024]{1,0:T(8,128)(2,1)S(1)}, bf16[128,1024]{1,0:T(8,128)(2,1)S(1)}, u32[]{:S(2)}, u32[]{:S(2)}) %collective-permute-start.13) | collective-permute-done | bytes 262176 | tf_op jit(solution)/shard_map/ppermute | solution.py:539
  57.5 2.8 %collective-permute-start.14 = (bf16[128,1024]{1,0:T(8,128)(2,1)S(1)}, bf16[128,1024]{1,0:T(8,128)(2,1)S(1)}, u32[]{:S(2)}, u32[]{:S(2)}) collective-permute-start(bf16[128,1024]{1,0:T(8,128)(2,1)S(1)} %collective-permute-done.13.refs_0_), channel_id=1, source_target_pairs={{0,8},{4,12},{8,0},{12,4},{1,9},{5,13},{9,1},{13,5},{2,10},{6,14},... | collective-permute-start | bytes 786440 | tf_op jit(solution)/shard_map/ppermute | solution.py:539
  60.8 1.6 collective-permute-start.15
  62.4 9.2 %collective-permute-done.14.refs_1_ = bf16[128,1024]{1,0:T(8,128)(2,1)S(1)} collective-permute-done((bf16[128,1024]{1,0:T(8,128)(2,1)S(1)}, bf16[128,1024]{1,0:T(8,128)(2,1)S(1)}, u32[]{:S(2)}, u32[]{:S(2)}) %collective-permute-start.14) | collective-permute-done | bytes 262176 | tf_op jit(solution)/shard_map/ppermute | solution.py:539
  72.2 2.1 shard_map.195
  74.6 5.1 %collective-permute-done.16.refs_3_ = bf16[128,1024]{1,0:T(8,128)(2,1)S(1)} collective-permute-done((bf16[128,1024]{1,0:T(8,128)(2,1)S(1)}, bf16[128,1024]{1,0:T(8,128)(2,1)S(1)}, u32[]{:S(2)}, u32[]{:S(2)}) %collective-permute-start.16) | collective-permute-done | bytes 262176 | tf_op jit(solution)/shard_map/ppermute | solution.py:539
  80.9 1.1 collective-permute-done.17
  82.1 1.6 collective-permute-start.18
  83.8 6.7 %collective-permute-done.18.got_ref = bf16[128,1024]{1,0:T(8,128)(2,1)S(1)} collective-permute-done((bf16[128,1024]{1,0:T(8,128)(2,1)S(1)}, bf16[128,1024]{1,0:T(8,128)(2,1)S(1)}, u32[]{:S(2)}, u32[]{:S(2)}) %collective-permute-start.18) | collective-permute-done | bytes 262176 | tf_op jit(solution)/shard_map/ppermute | solution.py:539
  91.1 1.9 collective-permute-done.19.r_2_.got_ref
  93.0 2.9 %shard_map.199 = (bf16[256,1024]{1,0:T(8,128)(2,1)S(1)}, f32[1,1024]{1,0:T(1,128)S(1)}, f32[128,1024]{1,0:T(8,128)S(1)}, bf16[128,1024]{1,0:T(8,128)(2,1)S(1)}) custom-call(bf16[256,1024]{1,0:T(8,128)(2,1)S(1)} %get-tuple-element.184.r_1_.own_ref, bf16[256,1024]{1,0:T(8,128)(2,1)S(1)} %collective-permute-done.19.r_2_.got_ref, bf16[512,1024]{1,0:T(8,128)(2,1)S(1)} %copy-done, ...), custom_call_target="tpu_custom_call" | custom-call | flops 1073741824 | bytes 7606272 | tf_op jit(solution)/shard_map/pallas_call | solution.py:314
  96.2 1.4 collective-permute-done.23
  97.6 1.6 collective-permute-start.24
  99.2 2.5 %collective-permute-start.27 = (bf16[256,256]{1,0:T(8,128)(2,1)S(1)}, bf16[256,256]{1,0:T(8,128)(2,1)S(1)}, u32[]{:S(2)}, u32[]{:S(2)}) collective-permute-start(bf16[256,256]{1,0:T(8,128)(2,1)S(1)} %fusion.5.r_0_.r_2_), channel_id=1, source_target_pairs={{0,8},{4,12},{8,0},{12,4},{1,9},{5,13},{9,1},{13,5},{2,10},{6,14},... | collective-permute-start | bytes 393224 | tf_op jit(solution)/shard_map/ppermute | solution.py:539
  101.6 4.4 %collective-permute-done.24.got_ref = bf16[128,1024]{1,0:T(8,128)(2,1)S(1)} collective-permute-done((bf16[128,1024]{1,0:T(8,128)(2,1)S(1)}, bf16[128,1024]{1,0:T(8,128)(2,1)S(1)}, u32[]{:S(2)}, u32[]{:S(2)}) %collective-permute-start.24) | collective-permute-done | bytes 262176 | tf_op jit(solution)/shard_map/ppermute | solution.py:539
  106.6 1.6 collective-permute-done.27.r_3_
  108.8 1.6 shard_map.201
  110.4 3.4 %collective-permute-start.29 = (bf16[288,256]{1,0:T(8,128)(2,1)S(1)}, bf16[288,256]{1,0:T(8,128)(2,1)S(1)}, u32[]{:S(2)}, u32[]{:S(2)}) collective-permute-start(bf16[288,256]{1,0:T(8,128)(2,1)S(1)} %get-tuple-element.146.r_1_.r_5_), channel_id=1, source_target_pairs={{0,8},{4,12},{8,0},{12,4},{1,9},{5,13},{9,1},{13,5},{2,10},{6,14},... | collective-permute-start | bytes 442376 | tf_op jit(solution)/shard_map/ppermute | solution.py:539
  113.8 1.5 collective-permute-start.21
  115.9 1.6 collective-permute-start.20
  117.5 1.1 collective-permute-done.28.r_4_
  118.6 3.2 %collective-permute-start.31 = (bf16[288,256]{1,0:T(8,128)(2,1)S(1)}, bf16[288,256]{1,0:T(8,128)(2,1)S(1)}, u32[]{:S(2)}, u32[]{:S(2)}) collective-permute-start(bf16[288,256]{1,0:T(8,128)(2,1)S(1)} %collective-permute-done.29.r_6_), channel_id=1, source_target_pairs={{0,4},{4,0},{8,12},{12,8},{1,5},{5,1},{9,13},{13,9},{2,6},{6,2},{1... | collective-permute-start | bytes 442376 | tf_op jit(solution)/shard_map/ppermute | solution.py:539
  121.8 3.8 %query_grads.1.dq_ref.r_7_.r_12_ = bf16[272,256]{1,0:T(8,128)(2,1)S(1)} custom-call(bf16[256,256]{1,0:T(8,128)(2,1)S(1)} %fusion.5.r_0_.r_2_, bf16[288,256]{1,0:T(8,128)(2,1)S(1)} %get-tuple-element.146.r_1_.r_5_, bf16[256,256]{1,0:T(8,128)(2,1)S(1)} %get-tuple-element.143.r_5_.r_2_.r_3_, f32[4,256]{1,0:T(4,128)S(1)} %get-tuple-element.144.r_6_.r_3_, ...), custom_call_target="tpu_custom_call" | custom-call | flops 1610612736 | bytes 1572864 | tf_op jit(solution)/shard_map/query_grads/pallas_call | solution.py:245
  125.6 1.6 collective-permute-start.32
  127.2 1.1 collective-permute-start.36
  128.3 4.0 %key_grads.1.dkv_ref.r_2_ = bf16[256,512]{1,0:T(8,128)(2,1)S(1)} custom-call(bf16[256,256]{1,0:T(8,128)(2,1)S(1)} %fusion.3.r_3_.r_4_.r_0_, bf16[256,256]{1,0:T(8,128)(2,1)} %fusion.4.r_7_.r_8_.r_1_, bf16[256,256]{1,0:T(8,128)(2,1)S(1)} %fusion.5.r_0_.r_2_, bf16[256,256]{1,0:T(8,128)(2,1)S(1)} %collective-permute-done.27.r_3_, ...), custom_call_target="tpu_custom_call" | custom-call | flops 2147483648 | bytes 1572864 | tf_op jit(solution)/shard_map/key_grads/pallas_call | solution.py:294
  132.4 1.6 shard_map.203
  134.1 11.3 %collective-permute-done.20.r_4_ = bf16[256,512]{1,0:T(8,128)(2,1)S(1)} collective-permute-done((bf16[256,512]{1,0:T(8,128)(2,1)S(1)}, bf16[256,512]{1,0:T(8,128)(2,1)S(1)}, u32[]{:S(2)}, u32[]{:S(2)}) %collective-permute-start.20) | collective-permute-done | bytes 262176 | tf_op jit(solution)/shard_map/ppermute | solution.py:539
  146.5 4.6 %collective-permute-done.32.r_4_ = bf16[256,512]{1,0:T(8,128)(2,1)S(1)} collective-permute-done((bf16[256,512]{1,0:T(8,128)(2,1)S(1)}, bf16[256,512]{1,0:T(8,128)(2,1)S(1)}, u32[]{:S(2)}, u32[]{:S(2)}) %collective-permute-start.32) | collective-permute-done | bytes 262176 | tf_op jit(solution)/shard_map/ppermute | solution.py:539
  152.1 1.5 collective-permute-start.40
  153.6 1.6 collective-permute-start.44
  155.2 5.8 %collective-permute-done.22.r_2_ = bf16[256,1024]{1,0:T(8,128)(2,1)S(1)} collective-permute-done((bf16[256,1024]{1,0:T(8,128)(2,1)S(1)}, bf16[256,1024]{1,0:T(8,128)(2,1)S(1)}, u32[]{:S(2)}, u32[]{:S(2)}) %collective-permute-start.22) | collective-permute-done | bytes 524320 | tf_op jit(solution)/shard_map/ppermute | solution.py:539
  161.1 1.5 collective-permute-start.37
  162.7 7.0 %collective-permute-done.34.r_2_ = bf16[256,1024]{1,0:T(8,128)(2,1)S(1)} collective-permute-done((bf16[256,1024]{1,0:T(8,128)(2,1)S(1)}, bf16[256,1024]{1,0:T(8,128)(2,1)S(1)}, u32[]{:S(2)}, u32[]{:S(2)}) %collective-permute-start.34) | collective-permute-done | bytes 524320 | tf_op jit(solution)/shard_map/ppermute | solution.py:539
  170.8 1.7 collective-permute-done.40.r_4_
  172.5 1.3 collective-permute-start.35
  175.5 1.4 collective-permute-start.38
  177.2 10.5 %collective-permute-done.26.refs_2_ = bf16[128,1024]{1,0:T(8,128)(2,1)S(1)} collective-permute-done((bf16[128,1024]{1,0:T(8,128)(2,1)S(1)}, bf16[128,1024]{1,0:T(8,128)(2,1)S(1)}, u32[]{:S(2)}, u32[]{:S(2)}) %collective-permute-start.26) | collective-permute-done | bytes 262176 | tf_op jit(solution)/shard_map/ppermute | solution.py:539
  187.7 1.0 maximum_select_fusion.4
  188.7 2.1 %collective-permute-done.35.refs_4_ = bf16[128,1024]{1,0:T(8,128)(2,1)S(1)} collective-permute-done((bf16[128,1024]{1,0:T(8,128)(2,1)S(1)}, bf16[128,1024]{1,0:T(8,128)(2,1)S(1)}, u32[]{:S(2)}, u32[]{:S(2)}) %collective-permute-start.35) | collective-permute-done | bytes 262176 | tf_op jit(solution)/shard_map/ppermute | solution.py:539
  192.0 5.2 %collective-permute-done.38.r_2_ = bf16[304,512]{1,0:T(8,128)(2,1)S(1)} collective-permute-done((bf16[304,512]{1,0:T(8,128)(2,1)S(1)}, bf16[304,512]{1,0:T(8,128)(2,1)S(1)}, u32[]{:S(2)}, u32[]{:S(2)}) %collective-permute-start.38) | collective-permute-done | bytes 311328 | tf_op jit(solution)/shard_map/ppermute | solution.py:539
  197.6 1.0 maximum_select_fusion.6
  198.6 4.5 %collective-permute-done.42.refs_8_ = bf16[128,512]{1,0:T(8,128)(2,1)S(1)} collective-permute-done((bf16[128,512]{1,0:T(8,128)(2,1)S(1)}, bf16[128,512]{1,0:T(8,128)(2,1)S(1)}, u32[]{:S(2)}, u32[]{:S(2)}) %collective-permute-start.42) | collective-permute-done | bytes 131104 | tf_op jit(solution)/shard_map/ppermute | solution.py:539
  203.1 1.9 collective-permute-done.39.refs_6_
  205.0 1.3 shard_map.210
  (131 shorter events, 18.8 us)
Async XLA Ops:
  0.7 1.2 copy-start.11
  2.1 1.1 copy-start.10
  3.2 3.7 %copy-start.14 = (bf16[512,256]{1,0:T(8,128)(2,1)S(1)}, bf16[512,256]{1,0:T(8,128)(2,1)}, u32[]{:S(2)}) copy-start(bf16[512,256]{1,0:T(8,128)(2,1)} %param.13) | copy-start | bytes 786436
  3.2 3.1 %copy-start.5 = (bf16[512,256]{1,0:T(8,128)(2,1)}, bf16[512,256]{1,0:T(8,128)(2,1)S(1)}, u32[]{:S(2)}) copy-start(bf16[512,256]{1,0:T(8,128)(2,1)S(1)} %get-tuple-element.207.refs_2_) | copy-start | bytes 786436
  3.3 5.3 %copy-start.1 = (bf16[512,1024]{1,0:T(8,128)(2,1)S(1)}, bf16[512,1024]{1,0:T(8,128)(2,1)}, u32[]{:S(2)}) copy-start(bf16[512,1024]{1,0:T(8,128)(2,1)} %un_ref) | copy-start | bytes 3145732
  3.3 10.2 %collective-permute-start.5 = (bf16[512,256]{1,0:T(8,128)(2,1)S(1)}, bf16[512,256]{1,0:T(8,128)(2,1)S(1)}, u32[]{:S(2)}, u32[]{:S(2)}) collective-permute-start(bf16[512,256]{1,0:T(8,128)(2,1)S(1)} %get-tuple-element.207.refs_2_), channel_id=1, source_target_pairs={{0,16},{16,0},{1,17},{17,1},{2,18},{18,2},{3,19},{19,3},{4,20},{20... | collective-permute-start | bytes 786440 | tf_op jit(solution)/shard_map/ppermute | solution.py:539
  6.3 12.7 %collective-permute-start.1 = (bf16[512,256]{1,0:T(8,128)(2,1)S(1)}, bf16[512,256]{1,0:T(8,128)(2,1)S(1)}, u32[]{:S(2)}, u32[]{:S(2)}) collective-permute-start(bf16[512,256]{1,0:T(8,128)(2,1)S(1)} %slice_bitcast_fusion.1.refs_1_), channel_id=1, source_target_pairs={{0,16},{16,0},{1,17},{17,1},{2,18},{18,2},{3,19},{19,3},{4,20},{20... | collective-permute-start | bytes 786440 | tf_op jit(solution)/shard_map/ppermute | solution.py:539
  7.0 23.4 %collective-permute-start = (bf16[512,512]{1,0:T(8,128)(2,1)S(1)}, bf16[512,512]{1,0:T(8,128)(2,1)}, u32[]{:S(2)}, u32[]{:S(2)}) collective-permute-start(bf16[512,512]{1,0:T(8,128)(2,1)S(1)} %pad_maximum_fusion.r_1_.r_3_.refs_0_), channel_id=1, source_target_pairs={{0,16},{16,0},{1,17},{17,1},{2,18},{18,2},{3,19},{19,3},{4,20},{20... | collective-permute-start | bytes 1572872 | tf_op jit(solution)/shard_map/ppermute | solution.py:539
  8.6 63.7 %collective-permute-start.12 = (bf16[512,1024]{1,0:T(8,128)(2,1)S(1)}, bf16[512,1024]{1,0:T(8,128)(2,1)}, u32[]{:S(2)}, u32[]{:S(2)}) collective-permute-start(bf16[512,1024]{1,0:T(8,128)(2,1)S(1)} %copy-done.1), channel_id=1, source_target_pairs={{0,16},{16,0},{1,17},{17,1},{2,18},{18,2},{3,19},{19,3},{4,20},{20... | collective-permute-start | bytes 3145736 | tf_op jit(solution)/shard_map/ppermute | solution.py:539
  9.5 0.9 copy-start.18
  10.5 12.0 %copy-start = (bf16[512,1024]{1,0:T(8,128)(2,1)S(1)}, bf16[512,1024]{1,0:T(8,128)(2,1)}, u32[]{:S(2)}) copy-start(bf16[512,1024]{1,0:T(8,128)(2,1)} %dn_ref) | copy-start | bytes 3145732
  14.3 8.1 %copy-start.16 = (f32[2,1024]{1,0:T(2,128)S(1)}, f32[2,1024]{1,0:T(2,128)}, u32[]{:S(2)}) copy-start(f32[2,1024]{1,0:T(2,128)} %param.19) | copy-start | bytes 24580
  14.4 9.9 %collective-permute-start.6 = (bf16[256,256]{1,0:T(8,128)(2,1)}, bf16[256,256]{1,0:T(8,128)(2,1)}, u32[]{:S(2)}, u32[]{:S(2)}) collective-permute-start(bf16[256,256]{1,0:T(8,128)(2,1)} %fusion.4.r_7_.r_8_.r_1_), channel_id=1, source_target_pairs={{0,8},{4,12},{8,0},{12,4},{1,9},{5,13},{9,1},{13,5},{2,10},{6,14},... | collective-permute-start | bytes 393224 | tf_op jit(solution)/shard_map/ppermute | solution.py:539
  19.3 8.1 %collective-permute-start.2 = (bf16[256,256]{1,0:T(8,128)(2,1)S(1)}, bf16[256,256]{1,0:T(8,128)(2,1)}, u32[]{:S(2)}, u32[]{:S(2)}) collective-permute-start(bf16[256,256]{1,0:T(8,128)(2,1)S(1)} %fusion.3.r_3_.r_4_.r_0_), channel_id=1, source_target_pairs={{0,8},{4,12},{8,0},{12,4},{1,9},{5,13},{9,1},{13,5},{2,10},{6,14},... | collective-permute-start | bytes 393224 | tf_op jit(solution)/shard_map/ppermute | solution.py:539
  22.5 10.0 %copy-start.13 = (f32[256,256]{1,0:T(8,128)S(1)}, f32[256,256]{1,0:T(8,128)}, u32[]{:S(2)}) copy-start(f32[256,256]{1,0:T(8,128)} %fusion.15) | copy-start | bytes 786436
  22.6 11.8 %collective-permute-start.7 = (bf16[256,256]{1,0:T(8,128)(2,1)}, bf16[256,256]{1,0:T(8,128)(2,1)S(1)}, u32[]{:S(2)}, u32[]{:S(2)}) collective-permute-start(bf16[256,256]{1,0:T(8,128)(2,1)} %fusion.4.r_7_.r_8_.r_1_), channel_id=1, source_target_pairs={{0,4},{4,0},{8,12},{12,8},{1,5},{5,1},{9,13},{13,9},{2,6},{6,2},{1... | collective-permute-start | bytes 393224 | tf_op jit(solution)/shard_map/ppermute | solution.py:539
  24.2 11.7 %collective-permute-start.3 = (bf16[256,256]{1,0:T(8,128)(2,1)S(1)}, bf16[256,256]{1,0:T(8,128)(2,1)S(1)}, u32[]{:S(2)}, u32[]{:S(2)}) collective-permute-start(bf16[256,256]{1,0:T(8,128)(2,1)S(1)} %fusion.3.r_3_.r_4_.r_0_), channel_id=1, source_target_pairs={{0,4},{4,0},{8,12},{12,8},{1,5},{5,1},{9,13},{13,9},{2,6},{6,2},{1... | collective-permute-start | bytes 393224 | tf_op jit(solution)/shard_map/ppermute | solution.py:539
  27.4 8.6 %collective-permute-start.8 = (bf16[256,256]{1,0:T(8,128)(2,1)}, bf16[256,256]{1,0:T(8,128)(2,1)S(1)}, u32[]{:S(2)}, u32[]{:S(2)}) collective-permute-start(bf16[256,256]{1,0:T(8,128)(2,1)} %collective-permute-done.6.r_8_.r_9_), channel_id=1, source_target_pairs={{0,4},{4,0},{8,12},{12,8},{1,5},{5,1},{9,13},{13,9},{2,6},{6,2},{1... | collective-permute-start | bytes 393224 | tf_op jit(solution)/shard_map/ppermute | solution.py:539
  30.4 6.5 %collective-permute-start.4 = (bf16[256,256]{1,0:T(8,128)(2,1)}, bf16[256,256]{1,0:T(8,128)(2,1)S(1)}, u32[]{:S(2)}, u32[]{:S(2)}) collective-permute-start(bf16[256,256]{1,0:T(8,128)(2,1)} %collective-permute-done.2.r_4_.r_5_), channel_id=1, source_target_pairs={{0,4},{4,0},{8,12},{12,8},{1,5},{5,1},{9,13},{13,9},{2,6},{6,2},{1... | collective-permute-start | bytes 393224 | tf_op jit(solution)/shard_map/ppermute | solution.py:539
  34.4 6.0 %copy-start.15 = (f32[2,1024]{1,0:T(2,128)S(1)}, f32[2,1024]{1,0:T(2,128)}, u32[]{:S(2)}) copy-start(f32[2,1024]{1,0:T(2,128)} %param.18) | copy-start | bytes 24580
  34.4 23.1 %collective-permute-start.13 = (bf16[128,1024]{1,0:T(8,128)(2,1)S(1)}, bf16[128,1024]{1,0:T(8,128)(2,1)S(1)}, u32[]{:S(2)}, u32[]{:S(2)}) collective-permute-start(bf16[128,1024]{1,0:T(8,128)(2,1)S(1)} %constant_dynamic-slice_fusion), channel_id=1, source_target_pairs={{0,16},{16,0},{1,17},{17,1},{2,18},{18,2},{3,19},{19,3},{4,20},{20... | collective-permute-start | bytes 786440 | tf_op jit(solution)/shard_map/ppermute | solution.py:539
  40.3 1.6 collective-permute-start.9
  41.9 1.9 copy-start.17
  41.9 18.5 %collective-permute-start.10 = (bf16[128,1024]{1,0:T(8,128)(2,1)S(1)}, bf16[128,1024]{1,0:T(8,128)(2,1)S(1)}, u32[]{:S(2)}, u32[]{:S(2)}) collective-permute-start(bf16[128,1024]{1,0:T(8,128)(2,1)S(1)} %add_convert_fusion.4.sent_ref), channel_id=1, source_target_pairs={{0,2},{1,3},{2,0},{3,1},{4,6},{5,7},{6,4},{7,5},{8,10},{9,11},{10,... | collective-permute-start | bytes 786440 | tf_op jit(solution)/shard_map/ppermute | solution.py:539
  57.5 14.1 %collective-permute-start.14 = (bf16[128,1024]{1,0:T(8,128)(2,1)S(1)}, bf16[128,1024]{1,0:T(8,128)(2,1)S(1)}, u32[]{:S(2)}, u32[]{:S(2)}) collective-permute-start(bf16[128,1024]{1,0:T(8,128)(2,1)S(1)} %collective-permute-done.13.refs_0_), channel_id=1, source_target_pairs={{0,8},{4,12},{8,0},{12,4},{1,9},{5,13},{9,1},{13,5},{2,10},{6,14},... | collective-permute-start | bytes 786440 | tf_op jit(solution)/shard_map/ppermute | solution.py:539
  60.4 11.8 %copy-start.9 = (f32[1024]{0:T(1024)S(1)}, f32[1024]{0:T(1024)}, u32[]{:S(2)}) copy-start(f32[1024]{0:T(1024)} %param.17) | copy-start | bytes 12292
  60.7 11.5 %collective-permute-start.11 = (bf16[128,1024]{1,0:T(8,128)(2,1)S(1)}, bf16[128,1024]{1,0:T(8,128)(2,1)S(1)}, u32[]{:S(2)}, u32[]{:S(2)}) collective-permute-start(bf16[128,1024]{1,0:T(8,128)(2,1)S(1)} %get-tuple-element.121.own_ref.r_1_), channel_id=1, source_target_pairs={{0,1},{1,0},{2,3},{3,2},{4,5},{5,4},{6,7},{7,6},{8,9},{9,8},{10,11... | collective-permute-start | bytes 786440 | tf_op jit(solution)/shard_map/ppermute | solution.py:539
  60.8 13.8 %collective-permute-start.15 = (bf16[128,1024]{1,0:T(8,128)(2,1)S(1)}, bf16[128,1024]{1,0:T(8,128)(2,1)S(1)}, u32[]{:S(2)}, u32[]{:S(2)}) collective-permute-start(bf16[128,1024]{1,0:T(8,128)(2,1)S(1)} %collective-permute-done.13.refs_0_), channel_id=1, source_target_pairs={{0,4},{4,0},{8,12},{12,8},{1,5},{5,1},{9,13},{13,9},{2,6},{6,2},{1... | collective-permute-start | bytes 786440 | tf_op jit(solution)/shard_map/ppermute | solution.py:539
  71.6 8.0 %collective-permute-start.16 = (bf16[128,1024]{1,0:T(8,128)(2,1)S(1)}, bf16[128,1024]{1,0:T(8,128)(2,1)S(1)}, u32[]{:S(2)}, u32[]{:S(2)}) collective-permute-start(bf16[128,1024]{1,0:T(8,128)(2,1)S(1)} %collective-permute-done.14.refs_1_), channel_id=1, source_target_pairs={{0,4},{4,0},{8,12},{12,8},{1,5},{5,1},{9,13},{13,9},{2,6},{6,2},{1... | collective-permute-start | bytes 786440 | tf_op jit(solution)/shard_map/ppermute | solution.py:539
  79.7 1.0 copy-start.12
  80.4 1.6 collective-permute-start.17
  82.1 8.4 %collective-permute-start.18 = (bf16[128,1024]{1,0:T(8,128)(2,1)S(1)}, bf16[128,1024]{1,0:T(8,128)(2,1)S(1)}, u32[]{:S(2)}, u32[]{:S(2)}) collective-permute-start(bf16[128,1024]{1,0:T(8,128)(2,1)S(1)} %add_convert_fusion.3.sent_ref), channel_id=1, source_target_pairs={{0,2},{1,3},{2,0},{3,1},{4,6},{5,7},{6,4},{7,5},{8,10},{9,11},{10,... | collective-permute-start | bytes 786440 | tf_op jit(solution)/shard_map/ppermute | solution.py:539
  91.1 2.0 collective-permute-start.19
  93.0 69.6 %copy-start.2 = (bf16[256,1024]{1,0:T(8,128)(2,1)}, bf16[256,1024]{1,0:T(8,128)(2,1)S(1)}, u32[]{:S(2)}) copy-start(bf16[256,1024]{1,0:T(8,128)(2,1)S(1)} %collective-permute-done.19.r_2_.got_ref) | copy-start | bytes 1572868
  96.0 1.6 collective-permute-start.23
  97.6 8.4 %collective-permute-start.24 = (bf16[128,1024]{1,0:T(8,128)(2,1)S(1)}, bf16[128,1024]{1,0:T(8,128)(2,1)S(1)}, u32[]{:S(2)}, u32[]{:S(2)}) collective-permute-start(bf16[128,1024]{1,0:T(8,128)(2,1)S(1)} %add_convert_fusion.2.sent_ref), channel_id=1, source_target_pairs={{0,2},{1,3},{2,0},{3,1},{4,6},{5,7},{6,4},{7,5},{8,10},{9,11},{10,... | collective-permute-start | bytes 786440 | tf_op jit(solution)/shard_map/ppermute | solution.py:539
  99.2 9.0 %collective-permute-start.27 = (bf16[256,256]{1,0:T(8,128)(2,1)S(1)}, bf16[256,256]{1,0:T(8,128)(2,1)S(1)}, u32[]{:S(2)}, u32[]{:S(2)}) collective-permute-start(bf16[256,256]{1,0:T(8,128)(2,1)S(1)} %fusion.5.r_0_.r_2_), channel_id=1, source_target_pairs={{0,8},{4,12},{8,0},{12,4},{1,9},{5,13},{9,1},{13,5},{2,10},{6,14},... | collective-permute-start | bytes 393224 | tf_op jit(solution)/shard_map/ppermute | solution.py:539
  106.5 2.3 %collective-permute-start.25 = (bf16[160,1024]{1,0:T(8,128)(2,1)S(1)}, bf16[160,1024]{1,0:T(8,128)(2,1)S(1)}, u32[]{:S(2)}, u32[]{:S(2)}) collective-permute-start(bf16[160,1024]{1,0:T(8,128)(2,1)S(1)} %get-tuple-element.142.r_1_), channel_id=1, source_target_pairs={{0,1},{1,0},{2,3},{3,2},{4,5},{5,4},{6,7},{7,6},{8,9},{9,8},{10,11... | collective-permute-start | bytes 983048 | tf_op jit(solution)/shard_map/ppermute | solution.py:539
  108.2 10.5 %collective-permute-start.28 = (bf16[512,256]{1,0:T(8,128)(2,1)S(1)}, bf16[512,256]{1,0:T(8,128)(2,1)S(1)}, u32[]{:S(2)}, u32[]{:S(2)}) collective-permute-start(bf16[512,256]{1,0:T(8,128)(2,1)S(1)} %pad_maximum_fusion.3), channel_id=1, source_target_pairs={{0,4},{4,0},{8,12},{12,8},{1,5},{5,1},{9,13},{13,9},{2,6},{6,2},{1... | collective-permute-start | bytes 786440 | tf_op jit(solution)/shard_map/ppermute | solution.py:539
  110.4 8.3 %collective-permute-start.29 = (bf16[288,256]{1,0:T(8,128)(2,1)S(1)}, bf16[288,256]{1,0:T(8,128)(2,1)S(1)}, u32[]{:S(2)}, u32[]{:S(2)}) collective-permute-start(bf16[288,256]{1,0:T(8,128)(2,1)S(1)} %get-tuple-element.146.r_1_.r_5_), channel_id=1, source_target_pairs={{0,8},{4,12},{8,0},{12,4},{1,9},{5,13},{9,1},{13,5},{2,10},{6,14},... | collective-permute-start | bytes 442376 | tf_op jit(solution)/shard_map/ppermute | solution.py:539
  113.8 20.2 %collective-permute-start.21 = (bf16[256,1024]{1,0:T(8,128)(2,1)S(1)}, bf16[256,1024]{1,0:T(8,128)(2,1)S(1)}, u32[]{:S(2)}, u32[]{:S(2)}) collective-permute-start(bf16[256,1024]{1,0:T(8,128)(2,1)S(1)} %get-tuple-element.123.act_ref.r_3_), channel_id=1, source_target_pairs={{0,16},{16,0},{1,17},{17,1},{2,18},{18,2},{3,19},{19,3},{4,20},{20... | collective-permute-start | bytes 1572872 | tf_op jit(solution)/shard_map/ppermute | solution.py:539
  115.3 35.8 %collective-permute-start.33 = (bf16[256,1024]{1,0:T(8,128)(2,1)S(1)}, bf16[256,1024]{1,0:T(8,128)(2,1)S(1)}, u32[]{:S(2)}, u32[]{:S(2)}) collective-permute-start(bf16[256,1024]{1,0:T(8,128)(2,1)S(1)} %get-tuple-element.154.r_3_), channel_id=1, source_target_pairs={{0,16},{16,0},{1,17},{17,1},{2,18},{18,2},{3,19},{19,3},{4,20},{20... | collective-permute-start | bytes 1572872 | tf_op jit(solution)/shard_map/ppermute | solution.py:539
  115.9 29.5 %collective-permute-start.20 = (bf16[256,512]{1,0:T(8,128)(2,1)S(1)}, bf16[256,512]{1,0:T(8,128)(2,1)S(1)}, u32[]{:S(2)}, u32[]{:S(2)}) collective-permute-start(bf16[256,512]{1,0:T(8,128)(2,1)S(1)} %pad_maximum_fusion.2), channel_id=1, source_target_pairs={{0,16},{16,0},{1,17},{17,1},{2,18},{18,2},{3,19},{19,3},{4,20},{20... | collective-permute-start | bytes 786440 | tf_op jit(solution)/shard_map/ppermute | solution.py:539
  118.6 7.0 %collective-permute-start.30 = (bf16[288,256]{1,0:T(8,128)(2,1)S(1)}, bf16[288,256]{1,0:T(8,128)(2,1)S(1)}, u32[]{:S(2)}, u32[]{:S(2)}) collective-permute-start(bf16[288,256]{1,0:T(8,128)(2,1)S(1)} %get-tuple-element.146.r_1_.r_5_), channel_id=1, source_target_pairs={{0,4},{4,0},{8,12},{12,8},{1,5},{5,1},{9,13},{13,9},{2,6},{6,2},{1... | collective-permute-start | bytes 442376 | tf_op jit(solution)/shard_map/ppermute | solution.py:539
  118.6 8.5 %collective-permute-start.31 = (bf16[288,256]{1,0:T(8,128)(2,1)S(1)}, bf16[288,256]{1,0:T(8,128)(2,1)S(1)}, u32[]{:S(2)}, u32[]{:S(2)}) collective-permute-start(bf16[288,256]{1,0:T(8,128)(2,1)S(1)} %collective-permute-done.29.r_6_), channel_id=1, source_target_pairs={{0,4},{4,0},{8,12},{12,8},{1,5},{5,1},{9,13},{13,9},{2,6},{6,2},{1... | collective-permute-start | bytes 442376 | tf_op jit(solution)/shard_map/ppermute | solution.py:539
  125.6 25.4 %collective-permute-start.32 = (bf16[256,512]{1,0:T(8,128)(2,1)S(1)}, bf16[256,512]{1,0:T(8,128)(2,1)S(1)}, u32[]{:S(2)}, u32[]{:S(2)}) collective-permute-start(bf16[256,512]{1,0:T(8,128)(2,1)S(1)} %get-tuple-element.155), channel_id=1, source_target_pairs={{0,16},{16,0},{1,17},{17,1},{2,18},{18,2},{3,19},{19,3},{4,20},{20... | collective-permute-start | bytes 786440 | tf_op jit(solution)/shard_map/ppermute | solution.py:539
  127.2 5.1 %copy-start.4 = (bf16[512,256]{1,0:T(8,128)(2,1)S(1)}, bf16[512,256]{1,0:T(8,128)(2,1)}, u32[]{:S(2)}) copy-start(bf16[512,256]{1,0:T(8,128)(2,1)} %copy-done.3) | copy-start | bytes 786436
  127.2 5.2 %copy-start.6 = (bf16[512,256]{1,0:T(8,128)(2,1)S(1)}, bf16[512,256]{1,0:T(8,128)(2,1)}, u32[]{:S(2)}) copy-start(bf16[512,256]{1,0:T(8,128)(2,1)} %copy-done.5) | copy-start | bytes 786436
  127.2 5.2 %copy-start.8 = (bf16[512,256]{1,0:T(8,128)(2,1)S(1)}, bf16[512,256]{1,0:T(8,128)(2,1)}, u32[]{:S(2)}) copy-start(bf16[512,256]{1,0:T(8,128)(2,1)} %copy-done.7) | copy-start | bytes 786436
  127.2 46.6 %collective-permute-start.36 = (bf16[288,1280]{1,0:T(8,128)(2,1)S(1)}, bf16[288,1280]{1,0:T(8,128)(2,1)S(1)}, u32[]{:S(2)}, u32[]{:S(2)}) collective-permute-start(bf16[288,1280]{1,0:T(8,128)(2,1)S(1)} %get-tuple-element.164), channel_id=1, source_target_pairs={{0,16},{16,0},{1,17},{17,1},{2,18},{18,2},{3,19},{19,3},{4,20},{20... | collective-permute-start | bytes 2211848 | tf_op jit(solution)/shard_map/ppermute | solution.py:539
  134.0 19.5 %collective-permute-start.43 = (bf16[128,1024]{1,0:T(8,128)(2,1)S(1)}, bf16[128,1024]{1,0:T(8,128)(2,1)S(1)}, u32[]{:S(2)}, u32[]{:S(2)}) collective-permute-start(bf16[128,1024]{1,0:T(8,128)(2,1)S(1)} %get-tuple-element.151), channel_id=1, source_target_pairs={{0,1},{1,0},{2,3},{3,2},{4,5},{5,4},{6,7},{7,6},{8,9},{9,8},{10,11... | collective-permute-start | bytes 786440 | tf_op jit(solution)/shard_map/ppermute | solution.py:539
  146.2 14.9 %collective-permute-start.22 = (bf16[256,1024]{1,0:T(8,128)(2,1)S(1)}, bf16[256,1024]{1,0:T(8,128)(2,1)S(1)}, u32[]{:S(2)}, u32[]{:S(2)}) collective-permute-start(bf16[256,1024]{1,0:T(8,128)(2,1)S(1)} %get-tuple-element.131), channel_id=1, source_target_pairs={{0,4},{4,0},{8,12},{12,8},{1,5},{5,1},{9,13},{13,9},{2,6},{6,2},{1... | collective-permute-start | bytes 1572872 | tf_op jit(solution)/shard_map/ppermute | solution.py:539
  151.8 17.9 %collective-permute-start.34 = (bf16[256,1024]{1,0:T(8,128)(2,1)S(1)}, bf16[256,1024]{1,0:T(8,128)(2,1)S(1)}, u32[]{:S(2)}, u32[]{:S(2)}) collective-permute-start(bf16[256,1024]{1,0:T(8,128)(2,1)S(1)} %get-tuple-element.156), channel_id=1, source_target_pairs={{0,4},{4,0},{8,12},{12,8},{1,5},{5,1},{9,13},{13,9},{2,6},{6,2},{1... | collective-permute-start | bytes 1572872 | tf_op jit(solution)/shard_map/ppermute | solution.py:539
  152.1 20.4 %collective-permute-start.40 = (bf16[256,512]{1,0:T(8,128)(2,1)S(1)}, bf16[256,512]{1,0:T(8,128)(2,1)S(1)}, u32[]{:S(2)}, u32[]{:S(2)}) collective-permute-start(bf16[256,512]{1,0:T(8,128)(2,1)S(1)} %key_grads.1.dkv_ref.r_2_), channel_id=1, source_target_pairs={{0,16},{16,0},{1,17},{17,1},{2,18},{18,2},{3,19},{19,3},{4,20},{20... | collective-permute-start | bytes 786440 | tf_op jit(solution)/shard_map/ppermute | solution.py:539
  153.6 23.3 %collective-permute-start.44 = (bf16[128,1024]{1,0:T(8,128)(2,1)S(1)}, bf16[128,1024]{1,0:T(8,128)(2,1)S(1)}, u32[]{:S(2)}, u32[]{:S(2)}) collective-permute-start(bf16[128,1024]{1,0:T(8,128)(2,1)S(1)} %add_convert_fusion.1), channel_id=1, source_target_pairs={{0,2},{1,3},{2,0},{3,1},{4,6},{5,7},{6,4},{7,5},{8,10},{9,11},{10,... | collective-permute-start | bytes 786440 | tf_op jit(solution)/shard_map/ppermute | solution.py:539
  161.1 13.9 %collective-permute-start.37 = (bf16[272,256]{1,0:T(8,128)(2,1)S(1)}, bf16[272,256]{1,0:T(8,128)(2,1)S(1)}, u32[]{:S(2)}, u32[]{:S(2)}) collective-permute-start(bf16[272,256]{1,0:T(8,128)(2,1)S(1)} %query_grads.1.dq_ref.r_7_.r_12_), channel_id=1, source_target_pairs={{0,16},{16,0},{1,17},{17,1},{2,18},{18,2},{3,19},{19,3},{4,20},{20... | collective-permute-start | bytes 417800 | tf_op jit(solution)/shard_map/ppermute | solution.py:539
  169.7 18.0 %collective-permute-start.26 = (bf16[128,1024]{1,0:T(8,128)(2,1)S(1)}, bf16[128,1024]{1,0:T(8,128)(2,1)S(1)}, u32[]{:S(2)}, u32[]{:S(2)}) collective-permute-start(bf16[128,1024]{1,0:T(8,128)(2,1)S(1)} %get-tuple-element.149), channel_id=1, source_target_pairs={{0,8},{4,12},{8,0},{12,4},{1,9},{5,13},{9,1},{13,5},{2,10},{6,14},... | collective-permute-start | bytes 786440 | tf_op jit(solution)/shard_map/ppermute | solution.py:539
  169.7 1.0 slice-start
  172.5 18.3 %collective-permute-start.35 = (bf16[128,1024]{1,0:T(8,128)(2,1)S(1)}, bf16[128,1024]{1,0:T(8,128)(2,1)S(1)}, u32[]{:S(2)}, u32[]{:S(2)}) collective-permute-start(bf16[128,1024]{1,0:T(8,128)(2,1)S(1)} %get-tuple-element.160), channel_id=1, source_target_pairs={{0,8},{4,12},{8,0},{12,4},{1,9},{5,13},{9,1},{13,5},{2,10},{6,14},... | collective-permute-start | bytes 786440 | tf_op jit(solution)/shard_map/ppermute | solution.py:539
  174.3 16.9 %collective-permute-start.41 = (bf16[256,512]{1,0:T(8,128)(2,1)S(1)}, bf16[256,512]{1,0:T(8,128)(2,1)S(1)}, u32[]{:S(2)}, u32[]{:S(2)}) collective-permute-start(bf16[256,512]{1,0:T(8,128)(2,1)S(1)} %get-tuple-element.175), channel_id=1, source_target_pairs={{0,4},{4,0},{8,12},{12,8},{1,5},{5,1},{9,13},{13,9},{2,6},{6,2},{1... | collective-permute-start | bytes 786440 | tf_op jit(solution)/shard_map/ppermute | solution.py:539
  175.5 21.6 %collective-permute-start.38 = (bf16[304,512]{1,0:T(8,128)(2,1)S(1)}, bf16[304,512]{1,0:T(8,128)(2,1)S(1)}, u32[]{:S(2)}, u32[]{:S(2)}) collective-permute-start(bf16[304,512]{1,0:T(8,128)(2,1)S(1)} %get-tuple-element.166), channel_id=1, source_target_pairs={{0,4},{4,0},{8,12},{12,8},{1,5},{5,1},{9,13},{13,9},{2,6},{6,2},{1... | collective-permute-start | bytes 933896 | tf_op jit(solution)/shard_map/ppermute | solution.py:539
  177.1 20.3 %collective-permute-start.45 = (bf16[128,1024]{1,0:T(8,128)(2,1)S(1)}, bf16[128,1024]{1,0:T(8,128)(2,1)S(1)}, u32[]{:S(2)}, u32[]{:S(2)}) collective-permute-start(bf16[128,1024]{1,0:T(8,128)(2,1)S(1)} %add_convert_fusion), channel_id=1, source_target_pairs={{0,1},{1,0},{2,3},{3,2},{4,5},{5,4},{6,7},{7,6},{8,9},{9,8},{10,11... | collective-permute-start | bytes 786440 | tf_op jit(solution)/shard_map/ppermute | solution.py:539
  191.3 11.8 %collective-permute-start.42 = (bf16[128,512]{1,0:T(8,128)(2,1)S(1)}, bf16[128,512]{1,0:T(8,128)(2,1)S(1)}, u32[]{:S(2)}, u32[]{:S(2)}) collective-permute-start(bf16[128,512]{1,0:T(8,128)(2,1)S(1)} %get-tuple-element.179), channel_id=1, source_target_pairs={{0,8},{4,12},{8,0},{12,4},{1,9},{5,13},{9,1},{13,5},{2,10},{6,14},... | collective-permute-start | bytes 393224 | tf_op jit(solution)/shard_map/ppermute | solution.py:539
  197.3 7.7 %collective-permute-start.39 = (bf16[176,512]{1,0:T(8,128)(2,1)S(1)}, bf16[176,512]{1,0:T(8,128)(2,1)S(1)}, u32[]{:S(2)}, u32[]{:S(2)}) collective-permute-start(bf16[176,512]{1,0:T(8,128)(2,1)S(1)} %get-tuple-element.171), channel_id=1, source_target_pairs={{0,8},{4,12},{8,0},{12,4},{1,9},{5,13},{9,1},{13,5},{2,10},{6,14},... | collective-permute-start | bytes 540680 | tf_op jit(solution)/shard_map/ppermute | solution.py:539
  (3 other events, 2.3 us)

commit v3 on v2

--- a/solution.py
+++ b/solution.py
@@ -169,9 +169,10 @@
     tokens, cols = at_ref.shape
     part = tokens // 2
     one = jnp.concatenate([own_ref[:part, :], got_ref[:part, :]], axis=0)
-    bundle_ref[:tokens, :half] = one[:, half:]
-    bundle_ref[:tokens, pl.ds(half, half)] = x_ref[:, pl.ds(half, half)]
-    bundle_ref[:tokens, pl.ds(2 * half, cols)] = at_ref[...]
+    bundle_ref[:part, :half] = own_ref[:part, half:]
+    bundle_ref[:part, pl.ds(half, half)] = x_ref[:part, pl.ds(half, half)]
+    bundle_ref[:part, pl.ds(2 * half, cols)] = at_ref[:part, :]
+    bundle_ref[:part, pl.ds(2 * half + cols, cols)] = at_ref[part:, :]
     out = pl.ds(near_ref.shape[1] - cols, cols)
     da = dot(one[:, :half], near_ref[:, out], NN) + dot(one[:, half:], far_ref[:, out], NN)
     da = da.astype(BF)
@@ -181,9 +182,9 @@
     vector_ref[6:7, :] = up_ref[...]
     vector_ref[7:8, :] = jnp.zeros((1, 2 * half), F32)
     vector_ref[7:8, pl.ds(cols, cols)] = jnp.sum(da.astype(F32), axis=0, keepdims=True)
-    extra = bundle_ref.shape[0] - tokens
-    bundle_ref[tokens:, : 2 * half] = stack_rows(split_rows(vector_ref[...]), extra)
-    bundle_ref[tokens:, pl.ds(2 * half, cols)] = jnp.zeros((extra, cols), BF)
+    extra = bundle_ref.shape[0] - part
+    bundle_ref[part:, : 2 * half] = stack_rows(split_rows(vector_ref[...]), extra)
+    bundle_ref[part:, pl.ds(2 * half, 2 * cols)] = jnp.zeros((extra, 2 * cols), BF)
     prod = da.astype(F32) * at_ref[...].astype(F32)
     deltas = []
     for h in range(heads):
@@ -203,7 +204,7 @@
         lambda *r: pack_kernel(heads, *r),
         (
             arr(message_rows(tokens, heads), cols, BF),
-            arr(tokens + 32, width + cols, BF),
+            arr(tokens // 2 + 32, width + 2 * cols, BF),
             arr(8, width, F32),
         ),
         flags, own, got, near, far, attended, lse, x, up_row,
@@ -458,17 +459,17 @@
                     block = pl.ds(pl.multiple_of(at + low, 128), rows)
                     a = [ins[k][pl.ds(0, tall), block] for k, tall in pieces]
                     a = a[0] if len(a) == 1 else jnp.concatenate(a, axis=0)
-                    where, first, cols = b
-                    b = ins[where][pl.ds(0, a.shape[0]), pl.ds(first, cols)]
+                    b = [ins[k][pl.ds(0, tall), pl.ds(first, cols)] for k, tall, first, cols in b]
+                    b = b[0] if len(b) == 1 else jnp.concatenate(b, axis=0)
                     term = dot(a, b, TN)
                     value = term if value is None else value + term
                 out[pl.ds(i * rows, rows), pl.ds(col, value.shape[1])] = value.astype(BF)
                 col += value.shape[1]
     if ride:
-        tokens, vector, bundle, dq, dq_mate = ride
+        part, tokens, vector, bundle, dq, dq_mate = ride
         width = ins[vector].shape[1]
         rows_x = settled_rows(ins[vector][...])
-        outs[2][...] = rows_x + join_rows(ins[bundle][tokens:, :width], 8)
+        outs[2][...] = rows_x + join_rows(ins[bundle][part:, :width], 8)
         sums = join_rows(ins[dq][tokens:, :], 1) + join_rows(ins[dq_mate][tokens:, :], 1)
         outs[2][7:8, pl.ds(0, sums.shape[1])] = sums
         put_vector(outs[2][...], away_ref, n // 2 * rows)
@@ -501,23 +502,26 @@
         put_vector(total_ref[...], away_ref, blocks // 2 * rows)
 
 
+def add_kernel(down_ref, down_got_ref, up_ref, up_got_ref, down_out_ref, up_out_ref):
+    down_out_ref[...] = down_ref[...].astype(F32) + down_got_ref[...].astype(F32)
+    up_out_ref[...] = up_ref[...].astype(F32) + up_got_ref[...].astype(F32)
+
+
 def finish_kernel(*refs):
     vector_ref, refs = refs[0], refs[1:]
-    down_ref, up_ref, out_ref, qkv_ref = refs[8:12]
-    head_ref, bias_up_ref, bias_ref, gain_ref, shift_ref = refs[12:]
+    out_ref, qkv_ref = refs[4:6]
+    head_ref, bias_up_ref, bias_ref, gain_ref, shift_ref = refs[6:]
     rows, cols = out_ref.shape
-    down, up, oq, kv = (
-        refs[2 * i][...].astype(F32) + refs[2 * i + 1][:rows, :].astype(F32) for i in range(4)
+    oq, kv = (
+        refs[2 * i][...].astype(F32) + refs[2 * i + 1][:rows, :].astype(F32) for i in range(2)
     )
-    down_ref[...] = down
-    up_ref[...] = up
     out_ref[...] = oq[:, :cols]
     qkv_ref[0] = oq[:, cols:]
     qkv_ref[1] = kv[:, :cols]
     qkv_ref[2] = kv[:, cols:]
     total = vector_ref[...]
-    if refs[5].shape[0] > rows:
-        total = settled_rows(total) + take_vector(refs[5], rows, total.shape[1])
+    if refs[1].shape[0] > rows:
+        total = settled_rows(total) + take_vector(refs[1], rows, total.shape[1])
     bias_ref[...] = total[0:2]
     gain_ref[...] = total[2:4]
     shift_ref[...] = total[4:6]
@@ -565,21 +569,23 @@
 
     def owned(products, after, mines, ride=None):
         rows = products[0][0][3] // nc
-        cols = sum(p[0][2][2] for p in products)
+        cols = sum(p[0][2][0][3] for p in products)
         blocks, extra, vector = nc // 2, 0, None
         if rows % 128 == 0:
             flat, terms, flops = [], [], 0
             for group in products:
                 terms.append([])
-                for stack, low, (b, first, wide), high in group:
+                for stack, low, b, high in group:
                     pieces = [(len(flat) + i, count) for i, (_, count) in enumerate(stack)]
-                    flat += [ref for ref, _ in stack] + [b]
-                    terms[-1].append((pieces, low, (len(flat) - 1, first, wide)))
-                    flops += 2 * b.shape[0] * high * wide
+                    flat += [ref for ref, _ in stack]
+                    others = [(len(flat) + i, *piece[1:]) for i, piece in enumerate(b)]
+                    flat += [piece[0] for piece in b]
+                    terms[-1].append((pieces, low, others))
+                    flops += sum(2 * tall * high * wide for _, tall, _, wide in b)
             spec, outs = None, ()
             if ride:
-                tokens, *carried = ride
-                spec = (tokens, *range(len(flat), len(flat) + 4))
+                part, tokens, *carried = ride
+                spec = (part, tokens, *range(len(flat), len(flat) + 4))
                 flat += carried
                 extra = 24 * carried[0].shape[1] // cols
                 outs = (arr(*carried[0].shape, F32),)
@@ -596,9 +602,10 @@
             grad = []
             for group in products:
                 value = 0.0
-                for stack, low, (b, first, wide), high in group:
+                for stack, low, b, high in group:
                     lhs = jnp.concatenate([r[:c, low : low + high] for r, c in stack], axis=0)
-                    value = value + dot(lhs, b[: lhs.shape[0], first : first + wide], TN)
+                    rhs = jnp.concatenate([r[:c, f : f + wide] for r, c, f, wide in b], axis=0)
+                    value = value + dot(lhs, rhs, TN)
                 grad.append(value.astype(BF))
             view = jnp.concatenate(grad, axis=1).reshape(blocks, 2, rows, cols)
             upper = mines[0][0] == 1
@@ -727,6 +734,7 @@
         )
         msgs = gather(msg)
         bundle = send(bundle_own, "weight")
+        bundle_got = send(bundle, "tensor")
         dq = query_grads(q, msg, attended, lse, ks, vs)
         dq_mate = send(dq, "weight")
         dkv = key_grads(k, v, qs, msgs)
@@ -738,9 +746,14 @@
         )
         late = [sent] * 8
 
-        def term(stack, b, low=0, first=0, wide=None):
-            return ([(r, r.shape[0] if c is None else c) for r, c in stack], low,
-                    (b, first, b.shape[1] if wide is None else wide), half_d)
+        def term(stack, b, low=0):
+            stack = [(r, r.shape[0] if c is None else c) for r, c in stack]
+            if not isinstance(b, list):
+                b = [(b, sum(c for _, c in stack), 0, b.shape[1])]
+            return stack, low, b, half_d
+
+        mate = [(bundle, half_t), (bundle_got, half_t)]
+        attended_mate = [(bundle, half_t, width, cols), (bundle, half_t, width + cols, cols)]
 
         grad_w_down = owned(
             [[term([(pair, half_t), (pair_got, half_t)], act), term([(two_mate, None)], act_mate)]],
@@ -759,26 +772,24 @@
             [
                 [
                     term([(one_own, half_t), (one_got, half_t)], attended),
-                    term([(bundle, tokens)], bundle, first=width, wide=cols),
+                    term(mate, attended_mate),
                 ],
-                [term([(x, None)], dq), term([(bundle, tokens)], dq_mate, low=half_d)],
+                [term([(x, None)], dq), term(mate, dq_mate, low=half_d)],
             ],
             late,
             mines,
-            (tokens, vector, bundle, dq, dq_mate),
+            (half_t, tokens, vector, bundle, dq, dq_mate),
         )
         sent, got = settle(keep, sent)
-        grad_wkv = owned(
-            [[term([(x, None)], dkv), term([(bundle, tokens)], dkv_mate, low=half_d)]], late, mines
-        )
+        grad_wkv = owned([[term([(x, None)], dkv), term(mate, dkv_mate, low=half_d)]], late, mines)
         grad_own = (grad_one + (sent.astype(F32) + got.astype(F32))).astype(BF)
         grad_got = send(grad_own, "tensor")
         grad_input = turn_d(turn_t(jnp.concatenate([grad_own, grad_got], axis=0)))
-        pair, pair_got, _ = lax.optimization_barrier((pair, pair_got, late[0]))
+        pair, pair_got, _ = lax.optimization_barrier((pair, pair_got, grad_w_up[1]))
         layer_out = turn_d(turn_t(jnp.concatenate([pair[half_t:], pair_got[half_t:]], axis=0)))
 
         if half_d // nc % 128:
-            rows = join_rows(bundle[tokens:, :width], 8) + vector
+            rows = join_rows(bundle[half_t:, :width], 8) + vector
             sums = join_rows(dq[tokens:], 1) + join_rows(dq_mate[tokens:], 1)
             vector = jnp.concatenate(
                 [rows[:7], jnp.concatenate([sums, rows[7:, cols:]], axis=1)], axis=0
@@ -789,13 +800,18 @@
                 bit *= 2
         else:
             vector = oq_grad[2]
-        terms = [a_ for triple in (grad_w_down, grad_w_up, oq_grad, grad_wkv) for a_ in triple[:2]]
-        terms, layer_out, grad_input = lax.optimization_barrier((terms, layer_out, grad_input))
         block = half_d // nc
-        down_grad, up_grad, out_grad, qkv_grad, head, up_row, bias, gain, shift = call(
+        down_grad, up_grad = call(
+            add_kernel, (arr(block, hidden, F32),) * 2,
+            *grad_w_down[:2], *grad_w_up[:2],
+        )
+        terms = [*oq_grad[:2], *grad_wkv[:2]]
+        terms, layer_out, grad_input, down_grad, up_grad = lax.optimization_barrier(
+            (terms, layer_out, grad_input, down_grad, up_grad)
+        )
+        out_grad, qkv_grad, head, up_row, bias, gain, shift = call(
             finish_kernel,
-            (arr(block, hidden, F32), arr(block, hidden, F32), arr(block, cols, F32),
-             jax.ShapeDtypeStruct((3, block, cols), F32), arr(2, cols, F32), arr(1, hidden, F32))
+            (arr(block, cols, F32), jax.ShapeDtypeStruct((3, block, cols), F32), arr(2, cols, F32), arr(1, hidden, F32))
             + (arr(2, width, F32),) * 3,
             vector, *terms,
         )

time: 207 us -> 237 us (1.14)
  waiting for transfers between devices: 112 us -> 134 us
  starting transfers between devices: 56.1 us -> 62.3 us
    ppermute x46 -> x47, waiting for transfers between devices: 112 us -> 134 us  [send(): return lax.ppermute(a, axis, [(i, i ^ bit) for i in range(sizes[axis])])]
    ppermute x46 -> x47, starting transfers between devices: 56.1 us -> 62.3 us  [send(): return lax.ppermute(a, axis, [(i, i ^ bit) for i in range(sizes[axis])])]
    pallas_call x17 -> x18, Pallas kernels: 14.4 us -> 15 us  [call(): pl.pallas_call(kernel, out_shape=outs, in_specs=[pl.BlockSpec(memory_spac...]
  transfers between devices with their start and end apart: 46 -> 47, of which waited for: 28 -> 26; matrix products, arithmetic and copies ran while one was open for 4% -> 3% of each run, Pallas kernels for 10% -> 9%
where the time goes in v3:
time: 237 us; the launch traced here: 236 us
  waiting for transfers between devices  134 us (57%)
  starting transfers between devices  62.3 us (26%)
  Pallas kernels  26 us (11%)
  local copies, waits for them, and re-layouts  5.36 us (2%)
  matrix products  3.69 us (2%)
  other arithmetic  3.19 us (1%)
    ppermute x47, waiting for transfers between devices, send(): return lax.ppermute(a, axis, [(i, i ^ bit) for i in range(sizes[axis])])  134 us
    ppermute x47, starting transfers between devices, send(): return lax.ppermute(a, axis, [(i, i ^ bit) for i in range(sizes[axis])])  62.3 us
    pallas_call x18, Pallas kernels, call(): pl.pallas_call(kernel, out_shape=outs, in_specs=[pl.BlockSpec(memory_spac...  15 us
  transfers between devices with their start and end apart: 47, of which 26 were waited for; matrix products, arithmetic and copies ran while one was open for 3% of the time, Pallas kernels for 9%

profile of v3, /device:TPU:0, one launch (start us, length us, event | category | flops | bytes accessed | tf_op | source)
XLA Modules:
  0.0 236.1 jit_solution(11513016536345168748)
XLA Ops:
  0.7 1.1 fusion.22
  2.3 0.9 copy-done.10
  3.3 0.9 copy-done.14
  4.2 3.0 %collective-permute-start = (bf16[512,512]{1,0:T(8,128)(2,1)S(1)}, bf16[512,512]{1,0:T(8,128)(2,1)}, u32[]{:S(2)}, u32[]{:S(2)}) collective-permute-start(bf16[512,512]{1,0:T(8,128)(2,1)S(1)} %pad_maximum_fusion.r_1_.r_3_.refs_0_), channel_id=1, source_target_pairs={{0,16},{16,0},{1,17},{17,1},{2,18},{18,2},{3,19},{19,3},{4,20},{20... | collective-permute-start | bytes 1572872 | tf_op jit(solution)/shard_map/ppermute | solution.py:543
  7.4 2.0 collective-permute-start.5
  9.5 0.9 fusion.15
  11.9 13.8 %collective-permute-done.1.refs_4_ = bf16[512,256]{1,0:T(8,128)(2,1)S(1)} collective-permute-done((bf16[512,256]{1,0:T(8,128)(2,1)S(1)}, bf16[512,256]{1,0:T(8,128)(2,1)S(1)}, u32[]{:S(2)}, u32[]{:S(2)}) %collective-permute-start.1) | collective-permute-done | bytes 262176 | tf_op jit(solution)/shard_map/ppermute | solution.py:543
  25.9 3.2 %collective-permute-start.2 = (bf16[256,256]{1,0:T(8,128)(2,1)S(1)}, bf16[256,256]{1,0:T(8,128)(2,1)}, u32[]{:S(2)}, u32[]{:S(2)}) collective-permute-start(bf16[256,256]{1,0:T(8,128)(2,1)S(1)} %fusion.3.r_3_.r_4_.r_0_), channel_id=1, source_target_pairs={{0,8},{4,12},{8,0},{12,4},{1,9},{5,13},{9,1},{13,5},{2,10},{6,14},... | collective-permute-start | bytes 393224 | tf_op jit(solution)/shard_map/ppermute | solution.py:543
  29.1 2.2 collective-permute-done.5.refs_5_
  32.2 3.1 %collective-permute-start.6 = (bf16[256,256]{1,0:T(8,128)(2,1)}, bf16[256,256]{1,0:T(8,128)(2,1)}, u32[]{:S(2)}, u32[]{:S(2)}) collective-permute-start(bf16[256,256]{1,0:T(8,128)(2,1)} %fusion.4.r_7_.r_8_.r_1_), channel_id=1, source_target_pairs={{0,8},{4,12},{8,0},{12,4},{1,9},{5,13},{9,1},{13,5},{2,10},{6,14},... | collective-permute-start | bytes 393224 | tf_op jit(solution)/shard_map/ppermute | solution.py:543
  35.4 1.6 collective-permute-start.3
  37.5 2.0 collective-permute-done.6.r_8_.r_9_
  39.5 2.1 collective-permute-start.4
  42.3 1.2 fusion.5.r_0_.r_2_
  43.5 1.6 collective-permute-start.13
  45.1 2.1 collective-permute-done.4.r_6_.r_7_
  47.2 1.4 collective-permute-done.8.r_10_.r_11_
  48.6 3.3 %attend.1 = (bf16[256,256]{1,0:T(8,128)(2,1)S(1)}, f32[4,256]{1,0:T(4,128)S(1)}, f32[128,1024]{1,0:T(8,128)S(1)}, bf16[128,1024]{1,0:T(8,128)(2,1)S(1)}) custom-call(bf16[256,256]{1,0:T(8,128)(2,1)S(1)} %fusion.5.r_0_.r_2_, bf16[512,512]{1,0:T(8,128)(2,1)S(1)} %pad_maximum_fusion.r_1_.r_3_.refs_0_, bf16[512,512]{1,0:T(8,128)(2,1)} %collective-permute-done.r_2_.r_4_.refs_3_, ...), custom_call_target="tpu_custom_call" | custom-call | flops 1073741824 | bytes 1310720 | tf_op jit(solution)/shard_map/attend/pallas_call | solution.py:106
  52.0 1.5 collective-permute-done.9
  53.6 1.6 collective-permute-start.10
  55.2 3.3 %collective-permute-done.13.refs_0_ = bf16[128,1024]{1,0:T(8,128)(2,1)S(1)} collective-permute-done((bf16[128,1024]{1,0:T(8,128)(2,1)S(1)}, bf16[128,1024]{1,0:T(8,128)(2,1)S(1)}, u32[]{:S(2)}, u32[]{:S(2)}) %collective-permute-start.13) | collective-permute-done | bytes 262176 | tf_op jit(solution)/shard_map/ppermute | solution.py:543
  58.5 2.8 %collective-permute-start.14 = (bf16[128,1024]{1,0:T(8,128)(2,1)S(1)}, bf16[128,1024]{1,0:T(8,128)(2,1)S(1)}, u32[]{:S(2)}, u32[]{:S(2)}) collective-permute-start(bf16[128,1024]{1,0:T(8,128)(2,1)S(1)} %collective-permute-done.13.refs_0_), channel_id=1, source_target_pairs={{0,8},{4,12},{8,0},{12,4},{1,9},{5,13},{9,1},{13,5},{2,10},{6,14},... | collective-permute-start | bytes 786440 | tf_op jit(solution)/shard_map/ppermute | solution.py:543
  62.4 1.5 collective-permute-start.15
  63.9 8.7 %collective-permute-done.14.refs_1_ = bf16[128,1024]{1,0:T(8,128)(2,1)S(1)} collective-permute-done((bf16[128,1024]{1,0:T(8,128)(2,1)S(1)}, bf16[128,1024]{1,0:T(8,128)(2,1)S(1)}, u32[]{:S(2)}, u32[]{:S(2)}) %collective-permute-start.14) | collective-permute-done | bytes 262176 | tf_op jit(solution)/shard_map/ppermute | solution.py:543
  73.2 2.0 shard_map.195
  75.3 0.9 collective-permute-done.15.refs_2_
  76.2 5.1 %collective-permute-done.16.refs_3_ = bf16[128,1024]{1,0:T(8,128)(2,1)S(1)} collective-permute-done((bf16[128,1024]{1,0:T(8,128)(2,1)S(1)}, bf16[128,1024]{1,0:T(8,128)(2,1)S(1)}, u32[]{:S(2)}, u32[]{:S(2)}) %collective-permute-start.16) | collective-permute-done | bytes 262176 | tf_op jit(solution)/shard_map/ppermute | solution.py:543
  82.5 1.1 collective-permute-done.17
  83.7 1.5 collective-permute-start.18
  85.4 6.8 %collective-permute-done.18.got_ref = bf16[128,1024]{1,0:T(8,128)(2,1)S(1)} collective-permute-done((bf16[128,1024]{1,0:T(8,128)(2,1)S(1)}, bf16[128,1024]{1,0:T(8,128)(2,1)S(1)}, u32[]{:S(2)}, u32[]{:S(2)}) %collective-permute-start.18) | collective-permute-done | bytes 262176 | tf_op jit(solution)/shard_map/ppermute | solution.py:543
  92.7 1.9 collective-permute-done.19.got_ref.r_2_
  94.6 2.9 %shard_map.198 = (bf16[256,1024]{1,0:T(8,128)(2,1)S(1)}, f32[1,1024]{1,0:T(1,128)S(1)}, f32[128,1024]{1,0:T(8,128)S(1)}, bf16[128,1024]{1,0:T(8,128)(2,1)S(1)}) custom-call(bf16[256,1024]{1,0:T(8,128)(2,1)S(1)} %get-tuple-element.173.own_ref.r_1_, bf16[256,1024]{1,0:T(8,128)(2,1)S(1)} %collective-permute-done.19.got_ref.r_2_, bf16[512,1024]{1,0:T(8,128)(2,1)S(1)} %copy-done, ...), custom_call_target="tpu_custom_call" | custom-call | flops 1073741824 | bytes 7606272 | tf_op jit(solution)/shard_map/pallas_call | solution.py:315
  97.8 1.4 collective-permute-start.44
  99.3 1.6 collective-permute-start.21
  100.8 1.4 collective-permute-start.37
  103.0 4.6 %collective-permute-done.21.got_ref = bf16[128,1024]{1,0:T(8,128)(2,1)S(1)} collective-permute-done((bf16[128,1024]{1,0:T(8,128)(2,1)S(1)}, bf16[128,1024]{1,0:T(8,128)(2,1)S(1)}, u32[]{:S(2)}, u32[]{:S(2)}) %collective-permute-start.21) | collective-permute-done | bytes 262176 | tf_op jit(solution)/shard_map/ppermute | solution.py:543
  108.2 1.5 collective-permute-start.36
  109.6 2.9 %collective-permute-done.44.r_5_ = bf16[256,1024]{1,0:T(8,128)(2,1)S(1)} collective-permute-done((bf16[256,1024]{1,0:T(8,128)(2,1)S(1)}, bf16[256,1024]{1,0:T(8,128)(2,1)S(1)}, u32[]{:S(2)}, u32[]{:S(2)}) %collective-permute-start.44) | collective-permute-done | bytes 524320 | tf_op jit(solution)/shard_map/ppermute | solution.py:543
  112.6 16.9 %collective-permute-done.43.r_4_ = bf16[256,512]{1,0:T(8,128)(2,1)S(1)} collective-permute-done((bf16[256,512]{1,0:T(8,128)(2,1)S(1)}, bf16[256,512]{1,0:T(8,128)(2,1)S(1)}, u32[]{:S(2)}, u32[]{:S(2)}) %collective-permute-start.43) | collective-permute-done | bytes 262176 | tf_op jit(solution)/shard_map/ppermute | solution.py:543
  130.4 4.1 %collective-permute-start.27 = (bf16[256,256]{1,0:T(8,128)(2,1)S(1)}, bf16[256,256]{1,0:T(8,128)(2,1)S(1)}, u32[]{:S(2)}, u32[]{:S(2)}) collective-permute-start(bf16[256,256]{1,0:T(8,128)(2,1)S(1)} %fusion.5.r_0_.r_2_), channel_id=1, source_target_pairs={{0,8},{4,12},{8,0},{12,4},{1,9},{5,13},{9,1},{13,5},{2,10},{6,14},... | collective-permute-start | bytes 393224 | tf_op jit(solution)/shard_map/ppermute | solution.py:543
  135.5 1.6 shard_map.200
  137.0 4.3 %collective-permute-start.29 = (bf16[288,256]{1,0:T(8,128)(2,1)S(1)}, bf16[288,256]{1,0:T(8,128)(2,1)S(1)}, u32[]{:S(2)}, u32[]{:S(2)}) collective-permute-start(bf16[288,256]{1,0:T(8,128)(2,1)S(1)} %get-tuple-element.143.r_1_.r_5_), channel_id=1, source_target_pairs={{0,8},{4,12},{8,0},{12,4},{1,9},{5,13},{9,1},{13,5},{2,10},{6,14},... | collective-permute-start | bytes 442376 | tf_op jit(solution)/shard_map/ppermute | solution.py:543
  141.3 4.2 %collective-permute-done.27.r_3_ = bf16[256,256]{1,0:T(8,128)(2,1)S(1)} collective-permute-done((bf16[256,256]{1,0:T(8,128)(2,1)S(1)}, bf16[256,256]{1,0:T(8,128)(2,1)S(1)}, u32[]{:S(2)}, u32[]{:S(2)}) %collective-permute-start.27) | collective-permute-done | bytes 131104 | tf_op jit(solution)/shard_map/ppermute | solution.py:543
  145.6 4.6 %collective-permute-start.28 = (bf16[512,256]{1,0:T(8,128)(2,1)S(1)}, bf16[512,256]{1,0:T(8,128)(2,1)S(1)}, u32[]{:S(2)}, u32[]{:S(2)}) collective-permute-start(bf16[512,256]{1,0:T(8,128)(2,1)S(1)} %pad_maximum_fusion.2), channel_id=1, source_target_pairs={{0,4},{4,0},{8,12},{12,8},{1,5},{5,1},{9,13},{13,9},{2,6},{6,2},{1... | collective-permute-start | bytes 786440 | tf_op jit(solution)/shard_map/ppermute | solution.py:543
  150.3 9.7 %collective-permute-done.29.r_6_ = bf16[288,256]{1,0:T(8,128)(2,1)S(1)} collective-permute-done((bf16[288,256]{1,0:T(8,128)(2,1)S(1)}, bf16[288,256]{1,0:T(8,128)(2,1)S(1)}, u32[]{:S(2)}, u32[]{:S(2)}) %collective-permute-start.29) | collective-permute-done | bytes 147488 | tf_op jit(solution)/shard_map/ppermute | solution.py:543
  159.9 4.5 %collective-permute-start.31 = (bf16[288,256]{1,0:T(8,128)(2,1)S(1)}, bf16[288,256]{1,0:T(8,128)(2,1)S(1)}, u32[]{:S(2)}, u32[]{:S(2)}) collective-permute-start(bf16[288,256]{1,0:T(8,128)(2,1)S(1)} %collective-permute-done.29.r_6_), channel_id=1, source_target_pairs={{0,4},{4,0},{8,12},{12,8},{1,5},{5,1},{9,13},{13,9},{2,6},{6,2},{1... | collective-permute-start | bytes 442376 | tf_op jit(solution)/shard_map/ppermute | solution.py:543
  164.5 3.6 %query_grads.1.r_9_.r_15_.dq_ref = bf16[272,256]{1,0:T(8,128)(2,1)S(1)} custom-call(bf16[256,256]{1,0:T(8,128)(2,1)S(1)} %fusion.5.r_0_.r_2_, bf16[288,256]{1,0:T(8,128)(2,1)S(1)} %get-tuple-element.143.r_1_.r_5_, bf16[256,256]{1,0:T(8,128)(2,1)S(1)} %get-tuple-element.138.r_5_.r_2_.r_3_, f32[4,256]{1,0:T(4,128)S(1)} %get-tuple-element.140.r_6_.r_3_, ...), custom_call_target="tpu_custom_call" | custom-call | flops 1610612736 | bytes 1572864 | tf_op jit(solution)/shard_map/query_grads/pallas_call | solution.py:246
  168.1 1.6 collective-permute-start.23
  170.1 3.3 %collective-permute-done.30.r_7_ = bf16[288,256]{1,0:T(8,128)(2,1)S(1)} collective-permute-done((bf16[288,256]{1,0:T(8,128)(2,1)S(1)}, bf16[288,256]{1,0:T(8,128)(2,1)S(1)}, u32[]{:S(2)}, u32[]{:S(2)}) %collective-permute-start.30) | collective-permute-done | bytes 147488 | tf_op jit(solution)/shard_map/ppermute | solution.py:543
  173.4 2.2 collective-permute-done.31.r_8_
  175.6 4.0 %key_grads.1.dkv_ref.r_2_ = bf16[256,512]{1,0:T(8,128)(2,1)S(1)} custom-call(bf16[256,256]{1,0:T(8,128)(2,1)S(1)} %fusion.3.r_3_.r_4_.r_0_, bf16[256,256]{1,0:T(8,128)(2,1)} %fusion.4.r_7_.r_8_.r_1_, bf16[256,256]{1,0:T(8,128)(2,1)S(1)} %fusion.5.r_0_.r_2_, bf16[256,256]{1,0:T(8,128)(2,1)S(1)} %collective-permute-done.27.r_3_, ...), custom_call_target="tpu_custom_call" | custom-call | flops 2147483648 | bytes 1572864 | tf_op jit(solution)/shard_map/key_grads/pallas_call | solution.py:295
  179.7 1.6 shard_map.202
  182.3 1.5 collective-permute-start.25
  184.4 9.3 %collective-permute-done.39.up_got_ref = bf16[128,1024]{1,0:T(8,128)(2,1)S(1)} collective-permute-done((bf16[128,1024]{1,0:T(8,128)(2,1)S(1)}, bf16[128,1024]{1,0:T(8,128)(2,1)S(1)}, u32[]{:S(2)}, u32[]{:S(2)}) %collective-permute-start.39) | collective-permute-done | bytes 262176 | tf_op jit(solution)/shard_map/ppermute | solution.py:543
  193.8 1.4 collective-permute-start.41
  195.4 1.1 shard_map.210
  196.5 4.1 %collective-permute-done.41 = bf16[128,1024]{1,0:T(8,128)(2,1)S(1)} collective-permute-done((bf16[128,1024]{1,0:T(8,128)(2,1)S(1)}, bf16[128,1024]{1,0:T(8,128)(2,1)S(1)}, u32[]{:S(2)}, u32[]{:S(2)}) %collective-permute-start.41) | collective-permute-done | bytes 262176 | tf_op jit(solution)/shard_map/ppermute | solution.py:543
  200.8 1.0 maximum_select_fusion.4
  202.3 1.7 collective-permute-start.26
  205.2 12.6 %collective-permute-done.34.r_2_ = bf16[256,512]{1,0:T(8,128)(2,1)S(1)} collective-permute-done((bf16[256,512]{1,0:T(8,128)(2,1)S(1)}, bf16[256,512]{1,0:T(8,128)(2,1)S(1)}, u32[]{:S(2)}, u32[]{:S(2)}) %collective-permute-start.34) | collective-permute-done | bytes 262176 | tf_op jit(solution)/shard_map/ppermute | solution.py:543
  217.8 3.3 %collective-permute-start.35 = (bf16[128,512]{1,0:T(8,128)(2,1)S(1)}, bf16[128,512]{1,0:T(8,128)(2,1)S(1)}, u32[]{:S(2)}, u32[]{:S(2)}) collective-permute-start(bf16[128,512]{1,0:T(8,128)(2,1)S(1)} %get-tuple-element.159), channel_id=1, source_target_pairs={{0,8},{4,12},{8,0},{12,4},{1,9},{5,13},{9,1},{13,5},{2,10},{6,14},... | collective-permute-start | bytes 393224 | tf_op jit(solution)/shard_map/ppermute | solution.py:543
  221.4 1.0 maximum_select_fusion.6
  222.3 9.8 %collective-permute-done.35.refs_4_ = bf16[128,512]{1,0:T(8,128)(2,1)S(1)} collective-permute-done((bf16[128,512]{1,0:T(8,128)(2,1)S(1)}, bf16[128,512]{1,0:T(8,128)(2,1)S(1)}, u32[]{:S(2)}, u32[]{:S(2)}) %collective-permute-start.35) | collective-permute-done | bytes 131104 | tf_op jit(solution)/shard_map/ppermute | solution.py:543
  232.2 3.1 %collective-permute-done.32.refs_2_ = bf16[176,512]{1,0:T(8,128)(2,1)S(1)} collective-permute-done((bf16[176,512]{1,0:T(8,128)(2,1)S(1)}, bf16[176,512]{1,0:T(8,128)(2,1)S(1)}, u32[]{:S(2)}, u32[]{:S(2)}) %collective-permute-start.32) | collective-permute-done | bytes 180256 | tf_op jit(solution)/shard_map/ppermute | solution.py:543
  (134 shorter events, 17.1 us)
Async XLA Ops:
  0.7 1.2 copy-start.11
  2.1 1.1 copy-start.10
  3.2 4.2 %copy-start.5 = (bf16[512,256]{1,0:T(8,128)(2,1)}, bf16[512,256]{1,0:T(8,128)(2,1)S(1)}, u32[]{:S(2)}) copy-start(bf16[512,256]{1,0:T(8,128)(2,1)S(1)} %get-tuple-element.203.refs_2_) | copy-start | bytes 786436
  3.3 6.1 %copy-start.1 = (bf16[512,1024]{1,0:T(8,128)(2,1)S(1)}, bf16[512,1024]{1,0:T(8,128)(2,1)}, u32[]{:S(2)}) copy-start(bf16[512,1024]{1,0:T(8,128)(2,1)} %un_ref) | copy-start | bytes 3145732
  4.2 37.4 %collective-permute-start = (bf16[512,512]{1,0:T(8,128)(2,1)S(1)}, bf16[512,512]{1,0:T(8,128)(2,1)}, u32[]{:S(2)}, u32[]{:S(2)}) collective-permute-start(bf16[512,512]{1,0:T(8,128)(2,1)S(1)} %pad_maximum_fusion.r_1_.r_3_.refs_0_), channel_id=1, source_target_pairs={{0,16},{16,0},{1,17},{17,1},{2,18},{18,2},{3,19},{19,3},{4,20},{20... | collective-permute-start | bytes 1572872 | tf_op jit(solution)/shard_map/ppermute | solution.py:543
  7.3 3.1 %copy-start.3 = (bf16[512,256]{1,0:T(8,128)(2,1)}, bf16[512,256]{1,0:T(8,128)(2,1)S(1)}, u32[]{:S(2)}) copy-start(bf16[512,256]{1,0:T(8,128)(2,1)S(1)} %slice_bitcast_fusion.1.refs_1_) | copy-start | bytes 786436
  7.3 18.4 %collective-permute-start.1 = (bf16[512,256]{1,0:T(8,128)(2,1)S(1)}, bf16[512,256]{1,0:T(8,128)(2,1)S(1)}, u32[]{:S(2)}, u32[]{:S(2)}) collective-permute-start(bf16[512,256]{1,0:T(8,128)(2,1)S(1)} %slice_bitcast_fusion.1.refs_1_), channel_id=1, source_target_pairs={{0,16},{16,0},{1,17},{17,1},{2,18},{18,2},{3,19},{19,3},{4,20},{20... | collective-permute-start | bytes 786440 | tf_op jit(solution)/shard_map/ppermute | solution.py:543
  7.4 23.9 %collective-permute-start.5 = (bf16[512,256]{1,0:T(8,128)(2,1)S(1)}, bf16[512,256]{1,0:T(8,128)(2,1)S(1)}, u32[]{:S(2)}, u32[]{:S(2)}) collective-permute-start(bf16[512,256]{1,0:T(8,128)(2,1)S(1)} %get-tuple-element.203.refs_2_), channel_id=1, source_target_pairs={{0,16},{16,0},{1,17},{17,1},{2,18},{18,2},{3,19},{19,3},{4,20},{20... | collective-permute-start | bytes 786440 | tf_op jit(solution)/shard_map/ppermute | solution.py:543
  9.4 63.8 %collective-permute-start.12 = (bf16[512,1024]{1,0:T(8,128)(2,1)S(1)}, bf16[512,1024]{1,0:T(8,128)(2,1)}, u32[]{:S(2)}, u32[]{:S(2)}) collective-permute-start(bf16[512,1024]{1,0:T(8,128)(2,1)S(1)} %copy-done.1), channel_id=1, source_target_pairs={{0,16},{16,0},{1,17},{17,1},{2,18},{18,2},{3,19},{19,3},{4,20},{20... | collective-permute-start | bytes 3145736 | tf_op jit(solution)/shard_map/ppermute | solution.py:543
  11.3 24.0 %copy-start = (bf16[512,1024]{1,0:T(8,128)(2,1)S(1)}, bf16[512,1024]{1,0:T(8,128)(2,1)}, u32[]{:S(2)}) copy-start(bf16[512,1024]{1,0:T(8,128)(2,1)} %dn_ref) | copy-start | bytes 3145732
  25.9 11.1 %collective-permute-start.2 = (bf16[256,256]{1,0:T(8,128)(2,1)S(1)}, bf16[256,256]{1,0:T(8,128)(2,1)}, u32[]{:S(2)}, u32[]{:S(2)}) collective-permute-start(bf16[256,256]{1,0:T(8,128)(2,1)S(1)} %fusion.3.r_3_.r_4_.r_0_), channel_id=1, source_target_pairs={{0,8},{4,12},{8,0},{12,4},{1,9},{5,13},{9,1},{13,5},{2,10},{6,14},... | collective-permute-start | bytes 393224 | tf_op jit(solution)/shard_map/ppermute | solution.py:543
  31.3 4.0 %copy-start.15 = (f32[2,1024]{1,0:T(2,128)S(1)}, f32[2,1024]{1,0:T(2,128)}, u32[]{:S(2)}) copy-start(f32[2,1024]{1,0:T(2,128)} %param.18) | copy-start | bytes 24580
  32.2 7.3 %collective-permute-start.6 = (bf16[256,256]{1,0:T(8,128)(2,1)}, bf16[256,256]{1,0:T(8,128)(2,1)}, u32[]{:S(2)}, u32[]{:S(2)}) collective-permute-start(bf16[256,256]{1,0:T(8,128)(2,1)} %fusion.4.r_7_.r_8_.r_1_), channel_id=1, source_target_pairs={{0,8},{4,12},{8,0},{12,4},{1,9},{5,13},{9,1},{13,5},{2,10},{6,14},... | collective-permute-start | bytes 393224 | tf_op jit(solution)/shard_map/ppermute | solution.py:543
  35.3 6.3 %copy-start.13 = (f32[256,256]{1,0:T(8,128)S(1)}, f32[256,256]{1,0:T(8,128)}, u32[]{:S(2)}) copy-start(f32[256,256]{1,0:T(8,128)} %fusion.15) | copy-start | bytes 786436
  35.4 8.1 %collective-permute-start.3 = (bf16[256,256]{1,0:T(8,128)(2,1)S(1)}, bf16[256,256]{1,0:T(8,128)(2,1)S(1)}, u32[]{:S(2)}, u32[]{:S(2)}) collective-permute-start(bf16[256,256]{1,0:T(8,128)(2,1)S(1)} %fusion.3.r_3_.r_4_.r_0_), channel_id=1, source_target_pairs={{0,4},{4,0},{8,12},{12,8},{1,5},{5,1},{9,13},{13,9},{2,6},{6,2},{1... | collective-permute-start | bytes 393224 | tf_op jit(solution)/shard_map/ppermute | solution.py:543
  37.0 8.0 %collective-permute-start.7 = (bf16[256,256]{1,0:T(8,128)(2,1)}, bf16[256,256]{1,0:T(8,128)(2,1)S(1)}, u32[]{:S(2)}, u32[]{:S(2)}) collective-permute-start(bf16[256,256]{1,0:T(8,128)(2,1)} %fusion.4.r_7_.r_8_.r_1_), channel_id=1, source_target_pairs={{0,4},{4,0},{8,12},{12,8},{1,5},{5,1},{9,13},{13,9},{2,6},{6,2},{1... | collective-permute-start | bytes 393224 | tf_op jit(solution)/shard_map/ppermute | solution.py:543
  39.5 7.7 %collective-permute-start.4 = (bf16[256,256]{1,0:T(8,128)(2,1)}, bf16[256,256]{1,0:T(8,128)(2,1)S(1)}, u32[]{:S(2)}, u32[]{:S(2)}) collective-permute-start(bf16[256,256]{1,0:T(8,128)(2,1)} %collective-permute-done.2.r_4_.r_5_), channel_id=1, source_target_pairs={{0,4},{4,0},{8,12},{12,8},{1,5},{5,1},{9,13},{13,9},{2,6},{6,2},{1... | collective-permute-start | bytes 393224 | tf_op jit(solution)/shard_map/ppermute | solution.py:543
  41.6 7.0 %collective-permute-start.8 = (bf16[256,256]{1,0:T(8,128)(2,1)}, bf16[256,256]{1,0:T(8,128)(2,1)S(1)}, u32[]{:S(2)}, u32[]{:S(2)}) collective-permute-start(bf16[256,256]{1,0:T(8,128)(2,1)} %collective-permute-done.6.r_8_.r_9_), channel_id=1, source_target_pairs={{0,4},{4,0},{8,12},{12,8},{1,5},{5,1},{9,13},{13,9},{2,6},{6,2},{1... | collective-permute-start | bytes 393224 | tf_op jit(solution)/shard_map/ppermute | solution.py:543
  43.5 8.5 %copy-start.16 = (f32[2,1024]{1,0:T(2,128)S(1)}, f32[2,1024]{1,0:T(2,128)}, u32[]{:S(2)}) copy-start(f32[2,1024]{1,0:T(2,128)} %param.19) | copy-start | bytes 24580
  43.5 15.0 %collective-permute-start.13 = (bf16[128,1024]{1,0:T(8,128)(2,1)S(1)}, bf16[128,1024]{1,0:T(8,128)(2,1)S(1)}, u32[]{:S(2)}, u32[]{:S(2)}) collective-permute-start(bf16[128,1024]{1,0:T(8,128)(2,1)S(1)} %constant_dynamic-slice_fusion), channel_id=1, source_target_pairs={{0,16},{16,0},{1,17},{17,1},{2,18},{18,2},{3,19},{19,3},{4,20},{20... | collective-permute-start | bytes 786440 | tf_op jit(solution)/shard_map/ppermute | solution.py:543
  51.9 1.6 collective-permute-start.9
  53.5 1.6 copy-start.17
  53.6 8.4 %collective-permute-start.10 = (bf16[128,1024]{1,0:T(8,128)(2,1)S(1)}, bf16[128,1024]{1,0:T(8,128)(2,1)S(1)}, u32[]{:S(2)}, u32[]{:S(2)}) collective-permute-start(bf16[128,1024]{1,0:T(8,128)(2,1)S(1)} %add_convert_fusion.4.sent_ref), channel_id=1, source_target_pairs={{0,2},{1,3},{2,0},{3,1},{4,6},{5,7},{6,4},{7,5},{8,10},{9,11},{10,... | collective-permute-start | bytes 786440 | tf_op jit(solution)/shard_map/ppermute | solution.py:543
  58.5 14.1 %collective-permute-start.14 = (bf16[128,1024]{1,0:T(8,128)(2,1)S(1)}, bf16[128,1024]{1,0:T(8,128)(2,1)S(1)}, u32[]{:S(2)}, u32[]{:S(2)}) collective-permute-start(bf16[128,1024]{1,0:T(8,128)(2,1)S(1)} %collective-permute-done.13.refs_0_), channel_id=1, source_target_pairs={{0,8},{4,12},{8,0},{12,4},{1,9},{5,13},{9,1},{13,5},{2,10},{6,14},... | collective-permute-start | bytes 786440 | tf_op jit(solution)/shard_map/ppermute | solution.py:543
  62.0 11.2 %copy-start.9 = (f32[1024]{0:T(1024)S(1)}, f32[1024]{0:T(1024)}, u32[]{:S(2)}) copy-start(f32[1024]{0:T(1024)} %param.17) | copy-start | bytes 12292
  62.3 10.9 %collective-permute-start.11 = (bf16[128,1024]{1,0:T(8,128)(2,1)S(1)}, bf16[128,1024]{1,0:T(8,128)(2,1)S(1)}, u32[]{:S(2)}, u32[]{:S(2)}) collective-permute-start(bf16[128,1024]{1,0:T(8,128)(2,1)S(1)} %get-tuple-element.119.own_ref.r_1_), channel_id=1, source_target_pairs={{0,1},{1,0},{2,3},{3,2},{4,5},{5,4},{6,7},{7,6},{8,9},{9,8},{10,11... | collective-permute-start | bytes 786440 | tf_op jit(solution)/shard_map/ppermute | solution.py:543
  62.4 13.8 %collective-permute-start.15 = (bf16[128,1024]{1,0:T(8,128)(2,1)S(1)}, bf16[128,1024]{1,0:T(8,128)(2,1)S(1)}, u32[]{:S(2)}, u32[]{:S(2)}) collective-permute-start(bf16[128,1024]{1,0:T(8,128)(2,1)S(1)} %collective-permute-done.13.refs_0_), channel_id=1, source_target_pairs={{0,4},{4,0},{8,12},{12,8},{1,5},{5,1},{9,13},{13,9},{2,6},{6,2},{1... | collective-permute-start | bytes 786440 | tf_op jit(solution)/shard_map/ppermute | solution.py:543
  72.6 8.7 %collective-permute-start.16 = (bf16[128,1024]{1,0:T(8,128)(2,1)S(1)}, bf16[128,1024]{1,0:T(8,128)(2,1)S(1)}, u32[]{:S(2)}, u32[]{:S(2)}) collective-permute-start(bf16[128,1024]{1,0:T(8,128)(2,1)S(1)} %collective-permute-done.14.refs_1_), channel_id=1, source_target_pairs={{0,4},{4,0},{8,12},{12,8},{1,5},{5,1},{9,13},{13,9},{2,6},{6,2},{1... | collective-permute-start | bytes 786440 | tf_op jit(solution)/shard_map/ppermute | solution.py:543
  81.3 1.0 copy-start.12
  82.0 1.6 collective-permute-start.17
  83.7 8.4 %collective-permute-start.18 = (bf16[128,1024]{1,0:T(8,128)(2,1)S(1)}, bf16[128,1024]{1,0:T(8,128)(2,1)S(1)}, u32[]{:S(2)}, u32[]{:S(2)}) collective-permute-start(bf16[128,1024]{1,0:T(8,128)(2,1)S(1)} %add_convert_fusion.3.sent_ref), channel_id=1, source_target_pairs={{0,2},{1,3},{2,0},{3,1},{4,6},{5,7},{6,4},{7,5},{8,10},{9,11},{10,... | collective-permute-start | bytes 786440 | tf_op jit(solution)/shard_map/ppermute | solution.py:543
  92.7 2.0 collective-permute-start.19
  94.6 99.1 %copy-start.2 = (bf16[256,1024]{1,0:T(8,128)(2,1)}, bf16[256,1024]{1,0:T(8,128)(2,1)S(1)}, u32[]{:S(2)}) copy-start(bf16[256,1024]{1,0:T(8,128)(2,1)S(1)} %collective-permute-done.19.got_ref.r_2_) | copy-start | bytes 1572868
  97.6 1.6 collective-permute-start.20
  97.8 14.8 %collective-permute-start.44 = (bf16[256,1024]{1,0:T(8,128)(2,1)S(1)}, bf16[256,1024]{1,0:T(8,128)(2,1)S(1)}, u32[]{:S(2)}, u32[]{:S(2)}) collective-permute-start(bf16[256,1024]{1,0:T(8,128)(2,1)S(1)} %get-tuple-element.121.act_ref.r_3_), channel_id=1, source_target_pairs={{0,16},{16,0},{1,17},{17,1},{2,18},{18,2},{3,19},{19,3},{4,20},{20... | collective-permute-start | bytes 1572872 | tf_op jit(solution)/shard_map/ppermute | solution.py:543
  99.3 8.4 %collective-permute-start.21 = (bf16[128,1024]{1,0:T(8,128)(2,1)S(1)}, bf16[128,1024]{1,0:T(8,128)(2,1)S(1)}, u32[]{:S(2)}, u32[]{:S(2)}) collective-permute-start(bf16[128,1024]{1,0:T(8,128)(2,1)S(1)} %add_convert_fusion.2.sent_ref), channel_id=1, source_target_pairs={{0,2},{1,3},{2,0},{3,1},{4,6},{5,7},{6,4},{7,5},{8,10},{9,11},{10,... | collective-permute-start | bytes 786440 | tf_op jit(solution)/shard_map/ppermute | solution.py:543
  100.8 33.7 %collective-permute-start.37 = (bf16[256,1024]{1,0:T(8,128)(2,1)S(1)}, bf16[256,1024]{1,0:T(8,128)(2,1)S(1)}, u32[]{:S(2)}, u32[]{:S(2)}) collective-permute-start(bf16[256,1024]{1,0:T(8,128)(2,1)S(1)} %get-tuple-element.163.r_3_), channel_id=1, source_target_pairs={{0,16},{16,0},{1,17},{17,1},{2,18},{18,2},{3,19},{19,3},{4,20},{20... | collective-permute-start | bytes 1572872 | tf_op jit(solution)/shard_map/ppermute | solution.py:543
  102.3 27.1 %collective-permute-start.43 = (bf16[256,512]{1,0:T(8,128)(2,1)S(1)}, bf16[256,512]{1,0:T(8,128)(2,1)S(1)}, u32[]{:S(2)}, u32[]{:S(2)}) collective-permute-start(bf16[256,512]{1,0:T(8,128)(2,1)S(1)} %pad_maximum_fusion.3), channel_id=1, source_target_pairs={{0,16},{16,0},{1,17},{17,1},{2,18},{18,2},{3,19},{19,3},{4,20},{20... | collective-permute-start | bytes 786440 | tf_op jit(solution)/shard_map/ppermute | solution.py:543
  108.1 27.4 %collective-permute-start.22 = (bf16[160,1024]{1,0:T(8,128)(2,1)S(1)}, bf16[160,1024]{1,0:T(8,128)(2,1)S(1)}, u32[]{:S(2)}, u32[]{:S(2)}) collective-permute-start(bf16[160,1024]{1,0:T(8,128)(2,1)S(1)} %get-tuple-element.137.r_1_), channel_id=1, source_target_pairs={{0,1},{1,0},{2,3},{3,2},{4,5},{5,4},{6,7},{7,6},{8,9},{9,8},{10,11... | collective-permute-start | bytes 983048 | tf_op jit(solution)/shard_map/ppermute | solution.py:543
  108.2 26.4 %collective-permute-start.36 = (bf16[256,512]{1,0:T(8,128)(2,1)S(1)}, bf16[256,512]{1,0:T(8,128)(2,1)S(1)}, u32[]{:S(2)}, u32[]{:S(2)}) collective-permute-start(bf16[256,512]{1,0:T(8,128)(2,1)S(1)} %get-tuple-element.164), channel_id=1, source_target_pairs={{0,16},{16,0},{1,17},{17,1},{2,18},{18,2},{3,19},{19,3},{4,20},{20... | collective-permute-start | bytes 786440 | tf_op jit(solution)/shard_map/ppermute | solution.py:543
  130.2 37.9 %collective-permute-start.45 = (bf16[256,1024]{1,0:T(8,128)(2,1)S(1)}, bf16[256,1024]{1,0:T(8,128)(2,1)S(1)}, u32[]{:S(2)}, u32[]{:S(2)}) collective-permute-start(bf16[256,1024]{1,0:T(8,128)(2,1)S(1)} %get-tuple-element.176), channel_id=1, source_target_pairs={{0,4},{4,0},{8,12},{12,8},{1,5},{5,1},{9,13},{13,9},{2,6},{6,2},{1... | collective-permute-start | bytes 1572872 | tf_op jit(solution)/shard_map/ppermute | solution.py:543
  130.4 15.1 %collective-permute-start.27 = (bf16[256,256]{1,0:T(8,128)(2,1)S(1)}, bf16[256,256]{1,0:T(8,128)(2,1)S(1)}, u32[]{:S(2)}, u32[]{:S(2)}) collective-permute-start(bf16[256,256]{1,0:T(8,128)(2,1)S(1)} %fusion.5.r_0_.r_2_), channel_id=1, source_target_pairs={{0,8},{4,12},{8,0},{12,4},{1,9},{5,13},{9,1},{13,5},{2,10},{6,14},... | collective-permute-start | bytes 393224 | tf_op jit(solution)/shard_map/ppermute | solution.py:543
  135.3 46.0 %collective-permute-start.38 = (bf16[256,1024]{1,0:T(8,128)(2,1)S(1)}, bf16[256,1024]{1,0:T(8,128)(2,1)S(1)}, u32[]{:S(2)}, u32[]{:S(2)}) collective-permute-start(bf16[256,1024]{1,0:T(8,128)(2,1)S(1)} %get-tuple-element.165), channel_id=1, source_target_pairs={{0,4},{4,0},{8,12},{12,8},{1,5},{5,1},{9,13},{13,9},{2,6},{6,2},{1... | collective-permute-start | bytes 1572872 | tf_op jit(solution)/shard_map/ppermute | solution.py:543
  137.0 22.9 %collective-permute-start.29 = (bf16[288,256]{1,0:T(8,128)(2,1)S(1)}, bf16[288,256]{1,0:T(8,128)(2,1)S(1)}, u32[]{:S(2)}, u32[]{:S(2)}) collective-permute-start(bf16[288,256]{1,0:T(8,128)(2,1)S(1)} %get-tuple-element.143.r_1_.r_5_), channel_id=1, source_target_pairs={{0,8},{4,12},{8,0},{12,4},{1,9},{5,13},{9,1},{13,5},{2,10},{6,14},... | collective-permute-start | bytes 442376 | tf_op jit(solution)/shard_map/ppermute | solution.py:543
  145.6 24.2 %collective-permute-start.28 = (bf16[512,256]{1,0:T(8,128)(2,1)S(1)}, bf16[512,256]{1,0:T(8,128)(2,1)S(1)}, u32[]{:S(2)}, u32[]{:S(2)}) collective-permute-start(bf16[512,256]{1,0:T(8,128)(2,1)S(1)} %pad_maximum_fusion.2), channel_id=1, source_target_pairs={{0,4},{4,0},{8,12},{12,8},{1,5},{5,1},{9,13},{13,9},{2,6},{6,2},{1... | collective-permute-start | bytes 786440 | tf_op jit(solution)/shard_map/ppermute | solution.py:543
  150.2 23.2 %collective-permute-start.30 = (bf16[288,256]{1,0:T(8,128)(2,1)S(1)}, bf16[288,256]{1,0:T(8,128)(2,1)S(1)}, u32[]{:S(2)}, u32[]{:S(2)}) collective-permute-start(bf16[288,256]{1,0:T(8,128)(2,1)S(1)} %get-tuple-element.143.r_1_.r_5_), channel_id=1, source_target_pairs={{0,4},{4,0},{8,12},{12,8},{1,5},{5,1},{9,13},{13,9},{2,6},{6,2},{1... | collective-permute-start | bytes 442376 | tf_op jit(solution)/shard_map/ppermute | solution.py:543
  159.9 15.7 %collective-permute-start.31 = (bf16[288,256]{1,0:T(8,128)(2,1)S(1)}, bf16[288,256]{1,0:T(8,128)(2,1)S(1)}, u32[]{:S(2)}, u32[]{:S(2)}) collective-permute-start(bf16[288,256]{1,0:T(8,128)(2,1)S(1)} %collective-permute-done.29.r_6_), channel_id=1, source_target_pairs={{0,4},{4,0},{8,12},{12,8},{1,5},{5,1},{9,13},{13,9},{2,6},{6,2},{1... | collective-permute-start | bytes 442376 | tf_op jit(solution)/shard_map/ppermute | solution.py:543
  168.1 16.3 %collective-permute-start.23 = (bf16[160,1536]{1,0:T(8,128)(2,1)S(1)}, bf16[160,1536]{1,0:T(8,128)(2,1)S(1)}, u32[]{:S(2)}, u32[]{:S(2)}) collective-permute-start(bf16[160,1536]{1,0:T(8,128)(2,1)S(1)} %get-tuple-element.142), channel_id=1, source_target_pairs={{0,16},{16,0},{1,17},{17,1},{2,18},{18,2},{3,19},{19,3},{4,20},{20... | collective-permute-start | bytes 1474568 | tf_op jit(solution)/shard_map/ppermute | solution.py:543
  169.7 9.9 %copy-start.4 = (bf16[512,256]{1,0:T(8,128)(2,1)S(1)}, bf16[512,256]{1,0:T(8,128)(2,1)}, u32[]{:S(2)}) copy-start(bf16[512,256]{1,0:T(8,128)(2,1)} %copy-done.3) | copy-start | bytes 786436
  169.8 9.9 %copy-start.6 = (bf16[512,256]{1,0:T(8,128)(2,1)S(1)}, bf16[512,256]{1,0:T(8,128)(2,1)}, u32[]{:S(2)}) copy-start(bf16[512,256]{1,0:T(8,128)(2,1)} %copy-done.5) | copy-start | bytes 786436
  169.8 9.9 %copy-start.8 = (bf16[512,256]{1,0:T(8,128)(2,1)S(1)}, bf16[512,256]{1,0:T(8,128)(2,1)}, u32[]{:S(2)}) copy-start(bf16[512,256]{1,0:T(8,128)(2,1)} %copy-done.7) | copy-start | bytes 786436
  169.8 14.0 %collective-permute-start.46 = (bf16[128,1024]{1,0:T(8,128)(2,1)S(1)}, bf16[128,1024]{1,0:T(8,128)(2,1)S(1)}, u32[]{:S(2)}, u32[]{:S(2)}) collective-permute-start(bf16[128,1024]{1,0:T(8,128)(2,1)S(1)} %get-tuple-element.180), channel_id=1, source_target_pairs={{0,8},{4,12},{8,0},{12,4},{1,9},{5,13},{9,1},{13,5},{2,10},{6,14},... | collective-permute-start | bytes 786440 | tf_op jit(solution)/shard_map/ppermute | solution.py:543
  181.5 12.2 %collective-permute-start.39 = (bf16[128,1024]{1,0:T(8,128)(2,1)S(1)}, bf16[128,1024]{1,0:T(8,128)(2,1)S(1)}, u32[]{:S(2)}, u32[]{:S(2)}) collective-permute-start(bf16[128,1024]{1,0:T(8,128)(2,1)S(1)} %get-tuple-element.169), channel_id=1, source_target_pairs={{0,8},{4,12},{8,0},{12,4},{1,9},{5,13},{9,1},{13,5},{2,10},{6,14},... | collective-permute-start | bytes 786440 | tf_op jit(solution)/shard_map/ppermute | solution.py:543
  182.3 11.4 %collective-permute-start.40 = (bf16[128,1024]{1,0:T(8,128)(2,1)S(1)}, bf16[128,1024]{1,0:T(8,128)(2,1)S(1)}, u32[]{:S(2)}, u32[]{:S(2)}) collective-permute-start(bf16[128,1024]{1,0:T(8,128)(2,1)S(1)} %get-tuple-element.147), channel_id=1, source_target_pairs={{0,1},{1,0},{2,3},{3,2},{4,5},{5,4},{6,7},{7,6},{8,9},{9,8},{10,11... | collective-permute-start | bytes 786440 | tf_op jit(solution)/shard_map/ppermute | solution.py:543
  182.3 19.5 %collective-permute-start.25 = (bf16[272,256]{1,0:T(8,128)(2,1)S(1)}, bf16[272,256]{1,0:T(8,128)(2,1)S(1)}, u32[]{:S(2)}, u32[]{:S(2)}) collective-permute-start(bf16[272,256]{1,0:T(8,128)(2,1)S(1)} %query_grads.1.r_9_.r_15_.dq_ref), channel_id=1, source_target_pairs={{0,16},{16,0},{1,17},{17,1},{2,18},{18,2},{3,19},{19,3},{4,20},{20... | collective-permute-start | bytes 417800 | tf_op jit(solution)/shard_map/ppermute | solution.py:543
  183.8 20.2 %collective-permute-start.33 = (bf16[256,512]{1,0:T(8,128)(2,1)S(1)}, bf16[256,512]{1,0:T(8,128)(2,1)S(1)}, u32[]{:S(2)}, u32[]{:S(2)}) collective-permute-start(bf16[256,512]{1,0:T(8,128)(2,1)S(1)} %key_grads.1.dkv_ref.r_2_), channel_id=1, source_target_pairs={{0,16},{16,0},{1,17},{17,1},{2,18},{18,2},{3,19},{19,3},{4,20},{20... | collective-permute-start | bytes 786440 | tf_op jit(solution)/shard_map/ppermute | solution.py:543
  184.4 17.4 %collective-permute-start.24 = (bf16[160,1536]{1,0:T(8,128)(2,1)S(1)}, bf16[160,1536]{1,0:T(8,128)(2,1)S(1)}, u32[]{:S(2)}, u32[]{:S(2)}) collective-permute-start(bf16[160,1536]{1,0:T(8,128)(2,1)S(1)} %collective-permute-done.23.r_4_.r_6_.r_7_.r_10_.r_14_.r_3_), channel_id=1, source_target_pairs={{0,1},{1,0},{2,3},{3,2},{4,5},{5,4},{6,7},{7,6},{8,9},{9,8},{10,11... | collective-permute-start | bytes 1474568 | tf_op jit(solution)/shard_map/ppermute | solution.py:543
  193.7 1.5 slice-start
  193.8 6.8 %collective-permute-start.41 = (bf16[128,1024]{1,0:T(8,128)(2,1)S(1)}, bf16[128,1024]{1,0:T(8,128)(2,1)S(1)}, u32[]{:S(2)}, u32[]{:S(2)}) collective-permute-start(bf16[128,1024]{1,0:T(8,128)(2,1)S(1)} %add_convert_fusion.1), channel_id=1, source_target_pairs={{0,2},{1,3},{2,0},{3,1},{4,6},{5,7},{6,4},{7,5},{8,10},{9,11},{10,... | collective-permute-start | bytes 786440 | tf_op jit(solution)/shard_map/ppermute | solution.py:543
  200.8 4.2 %collective-permute-start.42 = (bf16[128,1024]{1,0:T(8,128)(2,1)S(1)}, bf16[128,1024]{1,0:T(8,128)(2,1)S(1)}, u32[]{:S(2)}, u32[]{:S(2)}) collective-permute-start(bf16[128,1024]{1,0:T(8,128)(2,1)S(1)} %add_convert_fusion), channel_id=1, source_target_pairs={{0,1},{1,0},{2,3},{3,2},{4,5},{5,4},{6,7},{7,6},{8,9},{9,8},{10,11... | collective-permute-start | bytes 786440 | tf_op jit(solution)/shard_map/ppermute | solution.py:543
  202.3 18.8 %collective-permute-start.26 = (bf16[304,512]{1,0:T(8,128)(2,1)S(1)}, bf16[304,512]{1,0:T(8,128)(2,1)S(1)}, u32[]{:S(2)}, u32[]{:S(2)}) collective-permute-start(bf16[304,512]{1,0:T(8,128)(2,1)S(1)} %get-tuple-element.145), channel_id=1, source_target_pairs={{0,4},{4,0},{8,12},{12,8},{1,5},{5,1},{9,13},{13,9},{2,6},{6,2},{1... | collective-permute-start | bytes 933896 | tf_op jit(solution)/shard_map/ppermute | solution.py:543
  204.5 13.3 %collective-permute-start.34 = (bf16[256,512]{1,0:T(8,128)(2,1)S(1)}, bf16[256,512]{1,0:T(8,128)(2,1)S(1)}, u32[]{:S(2)}, u32[]{:S(2)}) collective-permute-start(bf16[256,512]{1,0:T(8,128)(2,1)S(1)} %get-tuple-element.155), channel_id=1, source_target_pairs={{0,4},{4,0},{8,12},{12,8},{1,5},{5,1},{9,13},{13,9},{2,6},{6,2},{1... | collective-permute-start | bytes 786440 | tf_op jit(solution)/shard_map/ppermute | solution.py:543
  217.8 14.3 %collective-permute-start.35 = (bf16[128,512]{1,0:T(8,128)(2,1)S(1)}, bf16[128,512]{1,0:T(8,128)(2,1)S(1)}, u32[]{:S(2)}, u32[]{:S(2)}) collective-permute-start(bf16[128,512]{1,0:T(8,128)(2,1)S(1)} %get-tuple-element.159), channel_id=1, source_target_pairs={{0,8},{4,12},{8,0},{12,4},{1,9},{5,13},{9,1},{13,5},{2,10},{6,14},... | collective-permute-start | bytes 393224 | tf_op jit(solution)/shard_map/ppermute | solution.py:543
  221.3 14.0 %collective-permute-start.32 = (bf16[176,512]{1,0:T(8,128)(2,1)S(1)}, bf16[176,512]{1,0:T(8,128)(2,1)S(1)}, u32[]{:S(2)}, u32[]{:S(2)}) collective-permute-start(bf16[176,512]{1,0:T(8,128)(2,1)S(1)} %get-tuple-element.151), channel_id=1, source_target_pairs={{0,8},{4,12},{8,0},{12,4},{1,9},{5,13},{9,1},{13,5},{2,10},{6,14},... | collective-permute-start | bytes 540680 | tf_op jit(solution)/shard_map/ppermute | solution.py:543
  (4 other events, 3.3 us)
